TPU v7x, 32 devices: a whole 2x2x4 slice. The times are simulated.
32 devices in a mesh: rep: 8 (over z, y), col: 4 (over x, core).
Axes of the slice: x: 2, y: 2, z: 4, core: 2. Of those that a mesh axis runs over, the one named last changes fastest.
Arguments:
- momentum: float32 [8, 288, 8192], P('rep', None, 'col'), may hold values from -6 to 6
- grads: bfloat16 [2, 8, 288, 8192], P(None, 'rep', None, 'col'), may hold values from -3 to 3
- weights: float32 [288, 8192], P(None, 'col'), may hold values from -6 to 6
- right_factor: float32 [8192, 256], P('col'), may hold values from -0.0625 to 0.0625
Outputs:
- new_weights: float32 [288, 8192], P(None, 'col')
- new_momentum: float32 [8, 288, 8192], P('rep', None, 'col')
- new_right: float32 [8192, 256], P('col')
All inputs are finite; a program needn't handle non-finite values.
Results may differ from a plain program's by a relative error of at most 0.0003.
Values sent between devices are 32-bit elements; how exact they have to be, the bound alone decides.
No kernel may reach another device: no remote copies, remote signals or barrier semaphores. Data moves between devices by JAX's collectives and lax.ppermute only.
A program may use at most 64 MiB of HBM per device.

v0:
```python
import functools
import math

import jax
import jax.numpy as jnp
from jax import lax
from jax.experimental import pallas as pl
from jax.experimental.pallas import tpu as pltpu
from jax.sharding import PartitionSpec as P


STEPS = 2
DAMPING = 0.1
RATE = 0.2
EPS = 1e-06
LANES = 128
GROUP = 8

precise = lax.Precision.HIGHEST
VMEM = pl.BlockSpec(memory_space=pltpu.VMEM)
SMEM = pl.BlockSpec(memory_space=pltpu.SMEM)
F32 = jnp.float32
BF16 = jnp.bfloat16


def dot(a, b, ca=1, cb=0):
    return lax.dot_general(
        a, b, (((ca,), (cb,)), ((), ())), precision=precise, preferred_element_type=F32
    )


def halves(x):
    high = x.astype(BF16)
    return high, (x - high.astype(F32)).astype(BF16)


def dot3(a, b, ca=1, cb=0):
    def one(x, y):
        return lax.dot_general(x, y, (((ca,), (cb,)), ((), ())), preferred_element_type=F32)

    return one(a[0], b[0]) + (one(a[0], b[1]) + one(a[1], b[0]))


def cost(flops, moved):
    return pl.CostEstimate(flops=int(flops), bytes_accessed=int(moved), transcendentals=0)


def eliminate(rows, group):
    count, n = len(rows), len(rows) * 8
    lane = lax.broadcasted_iota(jnp.int32, (8, n), 1)
    sub = lax.broadcasted_iota(jnp.int32, (8, n), 0)
    rows = list(rows)
    for j in range(0, n, group):
        rb, s = j // 8, j % 8

        def across(x, k):
            return jnp.broadcast_to(x[:, k : k + 1], (8, n))

        def down(x, k):
            return jnp.broadcast_to(x[k : k + 1, :], (8, n))

        column = [{i: across(rows[i], j + k) for i in range(rb, count)} for k in range(group)]
        unit = [[None] * group for _ in range(group)]
        scaled = [[None] * group for _ in range(group)]
        inverse = [None] * group
        for a in range(group):
            for b in range(a + 1):
                v = down(column[b][rb], s + a)
                for e in range(b):
                    v = v - unit[a][e] * scaled[b][e]
                scaled[a][b] = v
                if b < a:
                    unit[a][b] = v * inverse[b]
            inverse[a] = 1.0 / scaled[a][a]
        inside = (lane >= j) & (lane < j + group)
        pivot_rows = []
        for k in range(group):
            r = jnp.where(lane == j + k, 1.0, jnp.where(inside, 0.0, down(rows[rb], s + k)))
            for e in range(k):
                r = r - unit[k][e] * pivot_rows[e]
            pivot_rows.append(r)
        for i in range(rb, count):
            if i == rb and s + group == 8 and s == 0:
                out = rows[i]
                for k in range(group):
                    r = jnp.where(lane == j + k, scaled[k][k], pivot_rows[k])
                    out = jnp.where(sub == k, r, out)
                rows[i] = out
                continue
            left = []
            for k in range(group):
                v = column[k][i]
                for e in range(k):
                    v = v - unit[k][e] * left[e]
                left.append(v)
            y = jnp.where(inside, 0.0, rows[i])
            for k in range(group):
                m = left[k] * inverse[k]
                if i == rb:
                    m = jnp.where(sub > s + k, m, 0.0)
                y = y - m * pivot_rows[k]
            if i == rb:
                out = jnp.where(sub < s, rows[i], y)
                for k in range(group):
                    r = jnp.where(lane == j + k, scaled[k][k], pivot_rows[k])
                    out = jnp.where(sub == s + k, r, out)
                y = out
            rows[i] = y
    return rows


def inverse_factor(matrix):
    n = matrix.shape[0]
    rows = eliminate([matrix[8 * i : 8 * i + 8, :] for i in range(n // 8)], GROUP)
    rows = jnp.concatenate(rows, axis=0)
    lane = lax.broadcasted_iota(jnp.int32, (n, n), 1)
    sub = lax.broadcasted_iota(jnp.int32, (n, n), 0)
    pivots = jnp.sum(jnp.where(lane == sub, rows, 0.0), axis=1, keepdims=True)
    unit = jnp.where(lane < sub, rows, jnp.where(lane == sub, 1.0, 0.0))
    return unit / jnp.sqrt(pivots)


def orthonormal_blocks(blocks):
    out = []
    for block in blocks:
        for q in out:
            block = block - dot(q, dot(q, block, 0, 0))
        out.append(dot(block, inverse_factor(dot(block, block, 0, 0)), 1, 1))
    return out


def column_blocks(x):
    return [x[:, i : i + LANES] for i in range(0, x.shape[1], LANES)]


def first_kernel(scaled, me_ref, *refs):
    count = len(refs) - 3 - scaled
    parts, (left_ref, rest_ref), raw = refs[:count], refs[count : count + 2], refs[-1]
    rows = raw.shape[0] // count
    for d in range(count):
        at = pl.multiple_of((me_ref[0] ^ d) * rows, 8)
        raw[pl.ds(at, rows), :] = parts[d][:rows]
    left_raw = raw[...]
    if scaled:
        norm = jnp.sqrt(parts[0][rows : rows + 1] + EPS)
        refs[count + 2][...] = norm
        left_raw = left_raw / norm
    blocks = column_blocks(left_raw)
    middle = len(blocks) // 2
    done = orthonormal_blocks(blocks[:middle])
    left_ref[...] = jnp.concatenate(done, axis=1)
    rest = blocks[middle:]
    for q in done:
        rest = [block - dot(q, dot(q, block, 0, 0)) for block in rest]
    rest_ref[...] = jnp.concatenate(rest, axis=1)


def second_kernel(left_ref, rest_ref, out_ref, outt_ref):
    done = orthonormal_blocks(column_blocks(rest_ref[...]))
    left = jnp.concatenate([left_ref[...]] + done, axis=1)
    out_ref[...] = left
    outt_ref[...] = left.T


def orth_first(me, parts, rows, scaled):
    rank = parts[0].shape[1]
    part = jax.ShapeDtypeStruct((rows, rank // 2), F32)
    shapes = [part, part] + [jax.ShapeDtypeStruct((1, rank), F32)] * scaled
    return pl.pallas_call(
        functools.partial(first_kernel, scaled),
        out_shape=shapes,
        in_specs=[SMEM] + [VMEM] * len(parts),
        out_specs=[VMEM] * len(shapes),
        scratch_shapes=[pltpu.VMEM((rows, rank), F32)],
        cost_estimate=cost(6e9, 1e6),
        name="orth_first",
    )(me, *parts)


def orth_second(left, rest):
    rows, rank = left.shape[0], left.shape[1] + rest.shape[1]
    return pl.pallas_call(
        second_kernel,
        out_shape=[
            jax.ShapeDtypeStruct((rows, rank), F32),
            jax.ShapeDtypeStruct((rank, rows), F32),
        ],
        in_specs=[VMEM] * 2,
        out_specs=[VMEM] * 2,
        cost_estimate=cost(6e9, 1e6),
        name="orth_second",
    )(left, rest)


def chunk_rows(mom, grads):
    return jnp.concatenate([mom[0] + grads[0, 0].astype(F32), grads[1, 0].astype(F32)], axis=0)


def lead_kernel(at_ref, mom_up, grads_up, mom_dn, grads_dn, up_ref, dn_ref):
    up_ref[...] = chunk_rows(mom_up[...], grads_up[...])
    dn_ref[...] = chunk_rows(mom_dn[...], grads_dn[...])


def lead(at, momentum, grads, n):
    _, rows, cols = momentum.shape
    w = cols // n // 2
    part = jax.ShapeDtypeStruct((2 * rows, w), F32)
    specs = []
    for side in range(2):
        specs.append(pl.BlockSpec((1, rows, w), lambda i, at, side=side: (0, 0, 2 * at[side] + side)))
        specs.append(pl.BlockSpec((2, 1, rows, w), lambda i, at, side=side: (0, 0, 0, 2 * at[side] + side)))
    return pl.pallas_call(
        lead_kernel,
        out_shape=[part, part],
        grid_spec=pltpu.PrefetchScalarGridSpec(
            num_scalar_prefetch=1,
            grid=(1,),
            in_specs=specs,
            out_specs=[whole((2 * rows, w))] * 2,
        ),
        cost_estimate=cost(4 * rows * w, 32 * rows * w),
        name="lead",
    )(at, momentum, grads, momentum, grads)


def combine_kernel(count, inv, me_ref, mom_ref, grads_ref, right_ref, up_ref, dn_ref, both_ref, *refs):
    parts, acc_ref = refs[:count], refs[count]
    k = pl.program_id(0)
    rows = mom_ref.shape[1]
    total = mom_ref[0] + grads_ref[0, 0].astype(F32)
    later = grads_ref[1, 0].astype(F32)
    both_ref[...] = total + later
    w = total.shape[1] // 2
    up_ref[0, :rows] = total[:, :w]
    dn_ref[0, :rows] = total[:, w:]
    up_ref[0, rows:] = later[:, :w]
    dn_ref[0, rows:] = later[:, w:]
    part = dot(total, right_ref[...])

    @pl.when(k == 0)
    def _():
        acc_ref[...] = part

    @pl.when(k > 0)
    def _():
        acc_ref[...] += part

    @pl.when(k == pl.num_programs(0) - 1)
    def _():
        acc_ref[...] *= inv
        block = rows // count
        for d in range(count):
            at = pl.multiple_of((me_ref[0] ^ d) * block, 8)
            parts[d][...] = acc_ref[pl.ds(at, block), :]


def combine(me, momentum, grads, right_factor, n, count):
    _, rows, cols = momentum.shape
    rank = right_factor.shape[1]
    w = cols // n
    chunks = jax.ShapeDtypeStruct((n, 2 * rows, w // 2), F32)
    part = jax.ShapeDtypeStruct((rows // count, rank), F32)
    out = pl.pallas_call(
        functools.partial(combine_kernel, count, 1.0 / n),
        out_shape=[chunks, chunks, jax.ShapeDtypeStruct((rows, cols), F32)] + [part] * count,
        grid=(n,),
        in_specs=[
            SMEM,
            pl.BlockSpec((1, rows, w), lambda k: (0, 0, k)),
            pl.BlockSpec((2, 1, rows, w), lambda k: (0, 0, 0, k)),
            pl.BlockSpec((w, rank), lambda k: (k, 0)),
        ],
        out_specs=[
            pl.BlockSpec((1, 2 * rows, w // 2), lambda k: (k, 0, 0)),
            pl.BlockSpec((1, 2 * rows, w // 2), lambda k: (k, 0, 0)),
            pl.BlockSpec((rows, w), lambda k: (0, k)),
        ]
        + [pl.BlockSpec((rows // count, rank), lambda k: (0, 0))] * count,
        scratch_shapes=[pltpu.VMEM((rows, rank), F32)],
        cost_estimate=cost(12 * rows * cols * rank, 16 * rows * cols),
        name="combine",
    )(me, momentum, grads, right_factor)
    return out[0], out[1], out[2], out[3:]


def reduced_kernel(inv, at_ref, up_ref, dn_ref, up_all, dn_all, left_ref, leftt_ref, up_out, dn_out):
    rows, rank = left_ref.shape
    w = up_ref.shape[1]
    up, dn = up_ref[...] + up_all[0], dn_ref[...] + dn_all[0]
    mean = jnp.concatenate([up, dn], axis=1) * inv
    averaged, later = mean[:rows], mean[rows:]
    right = dot(leftt_ref[...], averaged)
    averaged = averaged - DAMPING * dot(left_ref[...], right) + later
    up_out[:rank] = right[:, :w]
    dn_out[:rank] = right[:, w:]
    up_out[rank:] = averaged[:, :w]
    dn_out[rank:] = averaged[:, w:]


def reduced(place, up, dn, up_all, dn_all, left, leftt, n):
    rows, rank = left.shape
    w = up.shape[1]
    ring = jax.ShapeDtypeStruct((rank + rows, w), F32)
    mine = pl.BlockSpec((1, 2 * rows, w), lambda i, at: (at[0], 0, 0))
    return pl.pallas_call(
        functools.partial(reduced_kernel, 1.0 / n),
        out_shape=[ring, ring],
        grid_spec=pltpu.PrefetchScalarGridSpec(
            num_scalar_prefetch=1,
            grid=(1,),
            in_specs=[whole(up.shape), whole(dn.shape), mine, mine, whole((rows, rank)), whole((rank, rows))],
            out_specs=[whole(ring.shape)] * 2,
        ),
        cost_estimate=cost(24 * rows * rank * rank, 4e6),
        name="reduced",
    )(place, up, dn, up_all, dn_all, left, leftt)


def partial_kernel(rank, me_ref, up_ref, dn_ref, *refs):
    parts, scratch = refs[:-1], refs[-1]
    rows = up_ref.shape[0] - rank
    both = jnp.concatenate([up_ref[...], dn_ref[...]], axis=1)
    right, averaged = both[:rank], both[rank:]
    scratch[...] = dot(averaged, right, 1, 1)
    squares = dot(jnp.ones((8, both.shape[1]), F32), right * right, 1, 1)
    block = rows // len(parts)
    for d, ref in enumerate(parts):
        at = pl.multiple_of((me_ref[0] ^ d) * block, 8)
        ref[:block] = scratch[pl.ds(at, block), :]
        ref[block:] = squares


def partial_raw(me, up, dn, rank, count):
    rows = up.shape[0] - rank
    part = jax.ShapeDtypeStruct((rows // count + 8, rank), F32)
    return pl.pallas_call(
        functools.partial(partial_kernel, rank),
        out_shape=[part] * count,
        in_specs=[SMEM] + [VMEM] * 2,
        out_specs=[VMEM] * count,
        scratch_shapes=[pltpu.VMEM((rows, rank), F32)],
        cost_estimate=cost(12 * rows * rank * rank, 2e6),
        name="partial",
    )(me, up, dn)


def squares_kernel(rank, up_ref, dn_ref, leftt_ref, out_ref):
    averaged = jnp.concatenate([up_ref[rank:], dn_ref[rank:]], axis=1)
    right = dot(leftt_ref[...], averaged)
    out_ref[...] = dot(jnp.ones((8, right.shape[1]), F32), right * right, 1, 1)


def squares_of(up, dn, leftt):
    rank = leftt.shape[0]
    return pl.pallas_call(
        functools.partial(squares_kernel, rank),
        out_shape=jax.ShapeDtypeStruct((8, rank), F32),
        in_specs=[VMEM] * 3,
        out_specs=VMEM,
        cost_estimate=cost(12 * rank * rank * rank, 2e6),
        name="squares",
    )(up, dn, leftt)


def fetcher(n, ups, dns, buf, sem):
    k = pl.program_id(0)
    w = buf.shape[2] // 2

    def copies(i, slot):
        return (
            pltpu.make_async_copy(ups[i], buf.at[slot, :, pl.ds(0, w)], sem.at[slot, 0]),
            pltpu.make_async_copy(dns[(n - i) % n], buf.at[slot, :, pl.ds(w, w)], sem.at[slot, 1]),
        )

    @pl.when(k == 0)
    def _():
        for c in copies(0, 0):
            c.start()

    for i in range(1, n):

        @pl.when(k == i - 1)
        def _():
            for c in copies(i, i % 2):
                c.start()

    slot = lax.rem(k, 2)
    for c in copies(0, slot):
        c.wait()
    return buf[slot]


def finish_kernel(n, rate, order_ref, *refs):
    ups, dns = refs[:n], refs[n : 2 * n]
    both_ref, w_ref, l1_ref, l2_ref, l2t_ref, norm_ref, total_ref = refs[2 * n : 2 * n + 7]
    mom_out, w_out, right_out, buf, sem, project, update = refs[2 * n + 7 :]
    rows, rank = l1_ref.shape
    norm = jnp.sqrt(total_ref[0:1] + EPS)

    @pl.when(pl.program_id(0) == 0)
    def _():
        project[0], project[1] = halves(l2t_ref[...])
        l1, l2 = l1_ref[...], l2_ref[...]
        moment = DAMPING * jnp.concatenate([l1, l2], axis=1)
        weight = rate * jnp.concatenate([l1 / norm_ref[...], l2 / norm], axis=1)
        update[0], update[1] = halves(jnp.concatenate([moment, weight], axis=0))

    chunk = fetcher(n, ups, dns, buf, sem)
    y1, averaged = chunk[:rank], chunk[rank:]
    y2 = dot3((project[0], project[1]), halves(averaged))
    change = dot3((update[0], update[1]), halves(jnp.concatenate([y1, y2], axis=0)))
    mom_out[0] = both_ref[...] - change[:rows]
    w_out[...] = w_ref[...] - change[rows:]
    right_out[...] = y2.T / norm


def finish(order, rings, both, weights, l1, l2, l2t, norm, totals, rate):
    n = len(rings) // 2
    rows, cols = both.shape
    rank = l1.shape[1]
    w = cols // n
    block = pl.BlockSpec((rows, w), lambda k, order: (0, order[k]))
    return pl.pallas_call(
        functools.partial(finish_kernel, n, rate),
        out_shape=[
            jax.ShapeDtypeStruct((1, rows, cols), F32),
            jax.ShapeDtypeStruct((rows, cols), F32),
            jax.ShapeDtypeStruct((cols, rank), F32),
        ],
        grid_spec=pltpu.PrefetchScalarGridSpec(
            num_scalar_prefetch=1,
            grid=(n,),
            in_specs=[pl.BlockSpec(memory_space=pl.ANY)] * len(rings)
            + [block, block, whole((rows, rank)), whole((rows, rank)), whole((rank, rows))]
            + [whole((1, rank)), whole((8, rank))],
            out_specs=[
                pl.BlockSpec((1, rows, w), lambda k, order: (0, 0, order[k])),
                block,
                pl.BlockSpec((w, rank), lambda k, order: (order[k], 0)),
            ],
            scratch_shapes=[
                pltpu.VMEM((2, rank + rows, w), F32),
                pltpu.SemaphoreType.DMA((2, 2)),
                pltpu.VMEM((2, rank, rows), BF16),
                pltpu.VMEM((2, 2 * rows, 2 * rank), BF16),
            ],
        ),
        cost_estimate=cost(30 * rows * cols * rank, 32 * rows * cols),
        name="finish",
    )(order, *rings, both, weights, l1, l2, l2t, norm, totals)


def whole(shape):
    return pl.BlockSpec(shape, lambda k, order: (0,) * len(shape))


def flip(x, axis, bits):
    size = lax.axis_size(axis)
    return lax.ppermute(x, axis, [(i, i ^ bits) for i in range(size)])


def all_sum_stages(box):
    cols, reps = lax.axis_size("col"), lax.axis_size("rep")

    def scatter():
        got = [flip(box["parts"][d], "col", d) for d in range(1, cols)]
        x = box["parts"][0]
        for other in got:
            x = x + other
        box["x"] = x

    def exchange(bit):
        def stage():
            got = flip(box["x"], "rep", 1 << bit)
            box["x"] = box["x"] + got

        return stage

    def gather():
        box["parts"] = [box["x"]] + [flip(box["x"], "col", d) for d in range(1, cols)]

    return [scatter] + [exchange(b) for b in range(reps.bit_length() - 1)] + [gather]


def ring_shards(rate, momentum, grads, weights, right_factor):
    n, count = lax.axis_size("rep"), lax.axis_size("col")
    _, rows, _ = momentum.shape
    rank = right_factor.shape[1]
    ring = list(range(0, n, 2)) + list(range(n - 1, 0, -2))
    rep = lax.axis_index("rep")
    place = jnp.where(rep % 2 == 0, rep // 2, n - 1 - rep // 2).astype(jnp.int32)
    ahead = [(ring[i], ring[(i + 1) % n]) for i in range(n)]
    back = [(b, a) for a, b in ahead]
    me = lax.axis_index("col").astype(jnp.int32)[None]
    order = lax.rem(place - jnp.arange(n, dtype=jnp.int32) + n, n)

    def chunk(x, k):
        return lax.dynamic_index_in_dim(x, lax.rem(place + k + 2 * n, n), 0, keepdims=False)

    def tie(box, *arrays):
        keys = list(box)
        tied = lax.optimization_barrier(([box[k] for k in keys], list(arrays)))
        box.update(zip(keys, tied[0]))
        return tied[1]

    def step(up, dn):
        return lax.ppermute(up, "rep", ahead), lax.ppermute(dn, "rep", back)

    def windows(box, scaled):
        stages = all_sum_stages(box)

        def first():
            out = orth_first(me, box.pop("parts"), rows, scaled)
            box.pop("x")
            box["left"], box["rest"] = out[:2]
            if scaled:
                box["norm"] = out[2]

        def second():
            box["left"], box["leftt"] = orth_second(box.pop("left"), box.pop("rest"))

        return [stages[:2]] + [[s] for s in stages[2:-2]] + [stages[-2:], [first], [second]]

    box = {}

    def prepare():
        up_all, dn_all, both, parts = combine(me, momentum, grads, right_factor, n, count)
        box.update(up_all=up_all, dn_all=dn_all, both=both, parts=list(parts))

    work = [[prepare]] + windows(box, False)
    up, dn = lead(lax.rem(jnp.stack([place + n - 1, place + 1]), n), momentum, grads, n)
    for k in range(1, n):
        up, dn = step(up, dn)
        if work:
            for stage in work.pop(0):
                stage()
            up, dn = tie(box, up, dn)
        if k < n - 1:
            up, dn = up + chunk(box["up_all"], -1 - k), dn + chunk(box["dn_all"], 1 + k)
    for stage in sum(work, []):
        stage()
    l1 = box["left"]
    both = box["both"]
    up, dn = reduced(place[None], up, dn, box["up_all"], box["dn_all"], l1, box["leftt"], n)

    box = {}
    mine = (up, dn)

    def begin():
        box["parts"] = list(partial_raw(me, *mine, rank, count))

    def total_columns():
        x = squares_of(*mine, box["leftt"])
        got = [flip(x, "col", d) for d in range(1, count)]
        terms = [x] + got
        while len(terms) > 1:
            terms = [a + b for a, b in zip(terms[::2], terms[1::2])]
        box["total"] = terms[0]

    def total_bit(bit):
        def stage():
            got = flip(box["total"], "rep", 1 << bit)
            box["total"] = box["total"] + got

        return stage

    work = windows(box, True)
    work[0].insert(0, begin)
    bits = [total_bit(b) for b in range(n.bit_length() - 1)]
    work += [[total_columns, bits[0]], bits[1:]]
    ups, dns = [up], [dn]
    for _ in range(1, n):
        up, dn = step(up, dn)
        if work:
            for stage in work.pop(0):
                stage()
            up, dn = tie(box, up, dn)
        ups.append(up)
        dns.append(dn)
    for stage in sum(work, []):
        stage()
    new_momentum, new_weights, new_right = finish(
        order, ups + dns, both, weights, l1, box["left"], box["leftt"], box["norm"], box["total"], rate
    )
    return new_weights, new_momentum, new_right


def plain_orthonormal(left_raw):
    zero = jnp.zeros((1,), jnp.int32)
    left, rest = orth_first(zero, [left_raw], left_raw.shape[0], False)
    return orth_second(left, rest)[0]


def plain_shards(rate, momentum, grads, weights, right_factor):
    n = lax.axis_size("rep")
    moment = momentum[0]
    combined = moment + grads[0, 0].astype(F32)
    averaged, later = lax.psum((combined / n, grads[1, 0].astype(F32) / n), "rep")
    for step in range(STEPS):
        if step > 0:
            combined = moment + grads[step, 0].astype(F32)
            averaged = averaged + later
        left = plain_orthonormal(lax.psum(dot(averaged, right_factor), "col"))
        right_raw = dot(averaged, left, 0, 0)
        correction = DAMPING * dot(left, right_raw, 1, 1)
        moment = combined - correction
        averaged = averaged - correction
        totals = lax.psum(jnp.sum(right_raw * right_raw, axis=0), "col")
        right_factor = right_raw / jnp.sqrt(totals + EPS)
        weights = weights - rate * dot(left, right_factor, 1, 1)
    return weights, moment[None], right_factor


def solution(mesh):
    def body(momentum, grads, weights, right_factor):
        rep, col = mesh.shape["rep"], mesh.shape["col"]
        _, rows, cols = momentum.shape
        rank = right_factor.shape[1]
        rate = RATE * math.sqrt(rows * cols / rank)
        powers = rep & (rep - 1) == 0 and col & (col - 1) == 0 and col > 1
        fits = cols % (2 * LANES * rep * col) == 0 and rows % (8 * col) == 0
        ring = powers and 4 < rep <= 16 and col <= 8 and fits

        def shards(*args):
            return (ring_shards if ring else plain_shards)(rate, *args)

        step = jax.shard_map(
            shards,
            mesh=mesh,
            in_specs=(
                P("rep", None, "col"),
                P(None, "rep", None, "col"),
                P(None, "col"),
                P("col", None),
            ),
            out_specs=(P(None, "col"), P("rep", None, "col"), P("col", None)),
            check_vma=False,
        )
        return step(momentum, grads, weights, right_factor)

    return body
```

profile of v0, /device:TPU:0, one launch (start us, length us, event | category | flops | bytes accessed | tf_op | source)
XLA Modules:
  0.0 210.4 jit_solution(3607462523505416599)
XLA Ops:
  1.2 2.6 %lead.1 = (f32[576,128]{1,0:T(8,128)}, f32[576,128]{1,0:T(8,128)}) custom-call(s32[2]{0:T(128)} %compare_select_fusion.at_ref, f32[1,288,2048]{2,1,0:T(8,128)} %mom_dn.1, bf16[2,1,288,2048]{3,2,1,0:T(8,128)(2,1)} %grads_dn.1, f32[1,288,2048]{2,1,0:T(8,128)} %mom_dn.1, bf16[2,1,288,2048]{3,2,1,0:T(8,128)(2,1)} %grads_dn.1), custom_call_target="tpu_custom_call" | custom-call | flops 147456 | bytes 1179648 | tf_op jit(solution)/shard_map/lead/pallas_call | solution.py:212
  3.9 3.1 %collective-permute-start = (f32[576,128]{1,0:T(8,128)}, f32[576,128]{1,0:T(8,128)S(1)}, u32[]{:S(2)}, u32[]{:S(2)}) collective-permute-start(f32[576,128]{1,0:T(8,128)} %get-tuple-element.115), channel_id=1, source_target_pairs={{0,8},{8,16},{16,24},{24,28},{28,20},{20,12},{12,4},{4,0},{1,9},{9... | collective-permute-start | bytes 884744 | tf_op jit(solution)/shard_map/ppermute | solution.py:507
  6.9 9.5 %combine.1 = (f32[8,576,128]{2,1,0:T(8,128)}, f32[8,576,128]{2,1,0:T(8,128)}, f32[288,2048]{1,0:T(8,128)}, f32[72,256]{1,0:T(8,128)}, f32[72,256]{1,0:T(8,128)}, /*index=5*/f32[72,256]{1,0:T(8,128)}, f32[72,256]{1,0:T(8,128)}) custom-call(s32[1]{0:T(128)} %bitcast.1.me_ref, f32[1,288,2048]{2,1,0:T(8,128)} %mom_dn.1, bf16[2,1,288,2048]{3,2,1,0:T(8,128)(2,1)} %grads_dn.1, ...), custom_call_target="tpu_custom_call" | custom-call | flops 1811939328 | bytes 9437184 | tf_op jit(solution)/shard_map/combine/pallas_call | solution.py:263
  26.3 6.8 %collective-permute-done.5 = f32[72,256]{1,0:T(8,128)} collective-permute-done((f32[72,256]{1,0:T(8,128)}, f32[72,256]{1,0:T(8,128)}, u32[]{:S(2)}, u32[]{:S(2)}) %collective-permute-start.5) | collective-permute-done | bytes 73760 | tf_op jit(solution)/shard_map/ppermute | solution.py:459
  37.9 7.5 %collective-permute-done.8 = f32[72,256]{1,0:T(8,128)} collective-permute-done((f32[72,256]{1,0:T(8,128)}, f32[72,256]{1,0:T(8,128)}, u32[]{:S(2)}, u32[]{:S(2)}) %collective-permute-start.8) | collective-permute-done | bytes 73760 | tf_op jit(solution)/shard_map/ppermute | solution.py:459
  52.6 6.8 %collective-permute-done.11 = f32[72,256]{1,0:T(8,128)S(1)} collective-permute-done((f32[72,256]{1,0:T(8,128)S(1)}, f32[72,256]{1,0:T(8,128)S(1)}, u32[]{:S(2)}, u32[]{:S(2)}) %collective-permute-start.11) | collective-permute-done | bytes 73760 | tf_op jit(solution)/shard_map/ppermute | solution.py:459
  61.9 3.0 %collective-permute-done.14.refs_3_ = f32[72,256]{1,0:T(8,128)} collective-permute-done((f32[72,256]{1,0:T(8,128)}, f32[72,256]{1,0:T(8,128)}, u32[]{:S(2)}, u32[]{:S(2)}) %collective-permute-start.14) | collective-permute-done | bytes 73760 | tf_op jit(solution)/shard_map/ppermute | solution.py:459
  67.5 4.0 %collective-permute-start.18 = (f32[576,128]{1,0:T(8,128)S(1)}, f32[576,128]{1,0:T(8,128)S(1)}, u32[]{:S(2)}, u32[]{:S(2)}) collective-permute-start(f32[576,128]{1,0:T(8,128)S(1)} %bitcast_add_fusion.4), channel_id=1, source_target_pairs={{8,0},{16,8},{24,16},{28,24},{20,28},{12,20},{4,12},{0,4},{9,1},{1... | collective-permute-start | bytes 884744 | tf_op jit(solution)/shard_map/ppermute | solution.py:507
  71.6 7.9 %orth_first.2 = (f32[288,128]{1,0:T(8,128)}, f32[288,128]{1,0:T(8,128)}) custom-call(s32[1]{0:T(128)} %bitcast.1.me_ref, f32[72,256]{1,0:T(8,128)} %add.234.refs_0_, f32[72,256]{1,0:T(8,128)} %collective-permute-done.12.refs_1_, f32[72,256]{1,0:T(8,128)} %collective-permute-done.13.refs_2_, f32[72,256]{1,0:T(8,128)} %collective-permute-done.14.refs_3_), custom_call_target="tpu_custom_call" | custom-call | flops 6000000000 | bytes 1000000 | tf_op jit(solution)/shard_map/orth_first/pallas_call | solution.py:169
  83.7 7.2 %orth_second.2 = (f32[288,256]{1,0:T(8,128)}, f32[256,288]{1,0:T(8,128)}) custom-call(f32[288,128]{1,0:T(8,128)} %get-tuple-element.152.left_ref, f32[288,128]{1,0:T(8,128)} %get-tuple-element.153.rest_ref), custom_call_target="tpu_custom_call" | custom-call | flops 6000000000 | bytes 1000000 | tf_op jit(solution)/shard_map/orth_second/pallas_call | solution.py:182
  94.2 5.2 %collective-permute-done.22.dn_ref = f32[576,128]{1,0:T(8,128)S(1)} collective-permute-done((f32[576,128]{1,0:T(8,128)S(1)}, f32[576,128]{1,0:T(8,128)S(1)}, u32[]{:S(2)}, u32[]{:S(2)}) %collective-permute-start.22) | collective-permute-done | bytes 294944 | tf_op jit(solution)/shard_map/ppermute | solution.py:507
  101.6 3.6 %reduced.1 = (f32[544,128]{1,0:T(8,128)}, f32[544,128]{1,0:T(8,128)}) custom-call(s32[1]{0:T(128)} %bitcast.at_ref, f32[576,128]{1,0:T(8,128)} %copy-done.2, f32[576,128]{1,0:T(8,128)} %copy-done.1, f32[8,576,128]{2,1,0:T(8,128)} %get-tuple-element.159.up_all, f32[8,576,128]{2,1,0:T(8,128)} %get-tuple-element.161.dn_all, ...), custom_call_target="tpu_custom_call" | custom-call | flops 452984832 | bytes 4000000 | tf_op jit(solution)/shard_map/reduced/pallas_call | solution.py:305
  105.2 2.4 %partial.1 = (f32[80,256]{1,0:T(8,128)}, f32[80,256]{1,0:T(8,128)}, f32[80,256]{1,0:T(8,128)}, f32[80,256]{1,0:T(8,128)}) custom-call(s32[1]{0:T(128)} %bitcast.1.me_ref, f32[544,128]{1,0:T(8,128)} %get-tuple-element.164.up_ref.refs_0_, f32[544,128]{1,0:T(8,128)} %get-tuple-element.165.dn_ref.refs_8_), custom_call_target="tpu_custom_call" | custom-call | flops 226492416 | bytes 2000000 | tf_op jit(solution)/shard_map/partial/pallas_call | solution.py:336
  115.2 5.0 %collective-permute-done.26 = f32[80,256]{1,0:T(8,128)S(1)} collective-permute-done((f32[80,256]{1,0:T(8,128)S(1)}, f32[80,256]{1,0:T(8,128)S(1)}, u32[]{:S(2)}, u32[]{:S(2)}) %collective-permute-start.26) | collective-permute-done | bytes 81952 | tf_op jit(solution)/shard_map/ppermute | solution.py:459
  122.5 8.0 %collective-permute-done.29 = f32[80,256]{1,0:T(8,128)S(1)} collective-permute-done((f32[80,256]{1,0:T(8,128)S(1)}, f32[80,256]{1,0:T(8,128)S(1)}, u32[]{:S(2)}, u32[]{:S(2)}) %collective-permute-start.29) | collective-permute-done | bytes 81952 | tf_op jit(solution)/shard_map/ppermute | solution.py:459
  133.7 7.8 %collective-permute-done.32 = f32[80,256]{1,0:T(8,128)S(1)} collective-permute-done((f32[80,256]{1,0:T(8,128)S(1)}, f32[80,256]{1,0:T(8,128)S(1)}, u32[]{:S(2)}, u32[]{:S(2)}) %collective-permute-start.32) | collective-permute-done | bytes 81952 | tf_op jit(solution)/shard_map/ppermute | solution.py:459
  143.5 2.2 %collective-permute-done.35.refs_3_ = f32[80,256]{1,0:T(8,128)S(1)} collective-permute-done((f32[80,256]{1,0:T(8,128)S(1)}, f32[80,256]{1,0:T(8,128)S(1)}, u32[]{:S(2)}, u32[]{:S(2)}) %collective-permute-start.35) | collective-permute-done | bytes 81952 | tf_op jit(solution)/shard_map/ppermute | solution.py:459
  149.1 7.9 %orth_first.3 = (f32[288,128]{1,0:T(8,128)}, f32[288,128]{1,0:T(8,128)}, f32[1,256]{1,0:T(1,128)}) custom-call(s32[1]{0:T(128)} %bitcast.1.me_ref, f32[80,256]{1,0:T(8,128)} %copy-done.4, f32[80,256]{1,0:T(8,128)} %copy-done.21, f32[80,256]{1,0:T(8,128)} %copy-done.20, f32[80,256]{1,0:T(8,128)} %copy-done.19), custom_call_target="tpu_custom_call" | custom-call | flops 6000000000 | bytes 1000000 | tf_op jit(solution)/shard_map/orth_first/pallas_call | solution.py:169
  159.2 7.3 %orth_second.3 = (f32[288,256]{1,0:T(8,128)}, f32[256,288]{1,0:T(8,128)}) custom-call(f32[288,128]{1,0:T(8,128)} %get-tuple-element.187.left_ref, f32[288,128]{1,0:T(8,128)} %get-tuple-element.188.rest_ref), custom_call_target="tpu_custom_call" | custom-call | flops 6000000000 | bytes 1000000 | tf_op jit(solution)/shard_map/orth_second/pallas_call | solution.py:182
  168.6 3.0 %squares.1 = f32[8,256]{1,0:T(8,128)} custom-call(f32[544,128]{1,0:T(8,128)} %get-tuple-element.164.up_ref.refs_0_, f32[544,128]{1,0:T(8,128)} %get-tuple-element.165.dn_ref.refs_8_, f32[256,288]{1,0:T(8,128)} %get-tuple-element.207.leftt_ref.refs_20_), custom_call_target="tpu_custom_call" | custom-call | flops 201326592 | bytes 2000000 | tf_op jit(solution)/shard_map/squares/pallas_call | solution.py:355
  177.6 2.2 %collective-permute-done.45 = f32[8,256]{1,0:T(8,128)S(1)} collective-permute-done((f32[8,256]{1,0:T(8,128)S(1)}, f32[8,256]{1,0:T(8,128)S(1)}, u32[]{:S(2)}, u32[]{:S(2)}) %collective-permute-start.45) | collective-permute-done | bytes 8224 | tf_op jit(solution)/shard_map/ppermute | solution.py:459
  182.2 5.9 %collective-permute-done.48 = f32[8,256]{1,0:T(8,128)S(1)} collective-permute-done((f32[8,256]{1,0:T(8,128)S(1)}, f32[8,256]{1,0:T(8,128)S(1)}, u32[]{:S(2)}, u32[]{:S(2)}) %collective-permute-start.48) | collective-permute-done | bytes 8224 | tf_op jit(solution)/shard_map/ppermute | solution.py:459
  188.2 2.8 %collective-permute-start.49 = (f32[8,256]{1,0:T(8,128)S(1)}, f32[8,256]{1,0:T(8,128)S(1)}, u32[]{:S(2)}, u32[]{:S(2)}) collective-permute-start(f32[8,256]{1,0:T(8,128)S(1)} %add.269), channel_id=1, source_target_pairs={{0,16},{4,20},{8,24},{12,28},{16,0},{20,4},{24,8},{28,12},{1,17},{... | collective-permute-start | bytes 24584 | tf_op jit(solution)/shard_map/ppermute | solution.py:459
  194.8 15.5 %finish.1 = (f32[1,288,2048]{2,1,0:T(8,128)}, f32[288,2048]{1,0:T(8,128)}, f32[2048,256]{1,0:T(8,128)}) custom-call(s32[8]{0:T(128)} %compare_select_fusion.2.order_ref, f32[544,128]{1,0:T(8,128)} %get-tuple-element.164.up_ref.refs_0_, f32[544,128]{1,0:T(8,128)} %copy-done.5, f32[544,128]{1,0:T(8,128)} %copy-done.7, f32[544,128]{1,0:T(8,128)} %copy-done.9, ...), custom_call_target="tpu_custom_call" | custom-call | flops 4529848320 | bytes 18874368 | tf_op jit(solution)/shard_map/finish/pallas_call | solution.py:423
  (160 shorter events, 71.8 us)
Async XLA Ops:
  3.9 12.6 %collective-permute-start = (f32[576,128]{1,0:T(8,128)}, f32[576,128]{1,0:T(8,128)S(1)}, u32[]{:S(2)}, u32[]{:S(2)}) collective-permute-start(f32[576,128]{1,0:T(8,128)} %get-tuple-element.115), channel_id=1, source_target_pairs={{0,8},{8,16},{16,24},{24,28},{28,20},{20,12},{12,4},{4,0},{1,9},{9... | collective-permute-start | bytes 884744 | tf_op jit(solution)/shard_map/ppermute | solution.py:507
  6.9 9.5 %collective-permute-start.1 = (f32[576,128]{1,0:T(8,128)}, f32[576,128]{1,0:T(8,128)S(1)}, u32[]{:S(2)}, u32[]{:S(2)}) collective-permute-start(f32[576,128]{1,0:T(8,128)} %get-tuple-element.116), channel_id=1, source_target_pairs={{8,0},{16,8},{24,16},{28,24},{20,28},{12,20},{4,12},{0,4},{9,1},{1... | collective-permute-start | bytes 884744 | tf_op jit(solution)/shard_map/ppermute | solution.py:507
  19.6 15.1 %collective-permute-start.7 = (f32[576,128]{1,0:T(8,128)S(1)}, f32[576,128]{1,0:T(8,128)S(1)}, u32[]{:S(2)}, u32[]{:S(2)}) collective-permute-start(f32[576,128]{1,0:T(8,128)S(1)} %bitcast_add_fusion.10), channel_id=1, source_target_pairs={{8,0},{16,8},{24,16},{28,24},{20,28},{12,20},{4,12},{0,4},{9,1},{1... | collective-permute-start | bytes 884744 | tf_op jit(solution)/shard_map/ppermute | solution.py:507
  22.4 12.3 %collective-permute-start.6 = (f32[576,128]{1,0:T(8,128)S(1)}, f32[576,128]{1,0:T(8,128)S(1)}, u32[]{:S(2)}, u32[]{:S(2)}) collective-permute-start(f32[576,128]{1,0:T(8,128)S(1)} %bitcast_add_fusion.11), channel_id=1, source_target_pairs={{0,8},{8,16},{16,24},{24,28},{28,20},{20,12},{12,4},{4,0},{1,9},{9... | collective-permute-start | bytes 884744 | tf_op jit(solution)/shard_map/ppermute | solution.py:507
  35.7 10.7 %collective-permute-start.10 = (f32[576,128]{1,0:T(8,128)S(1)}, f32[576,128]{1,0:T(8,128)S(1)}, u32[]{:S(2)}, u32[]{:S(2)}) collective-permute-start(f32[576,128]{1,0:T(8,128)S(1)} %bitcast_add_fusion.8), channel_id=1, source_target_pairs={{8,0},{16,8},{24,16},{28,24},{20,28},{12,20},{4,12},{0,4},{9,1},{1... | collective-permute-start | bytes 884744 | tf_op jit(solution)/shard_map/ppermute | solution.py:507
  35.8 10.6 %collective-permute-start.9 = (f32[576,128]{1,0:T(8,128)S(1)}, f32[576,128]{1,0:T(8,128)S(1)}, u32[]{:S(2)}, u32[]{:S(2)}) collective-permute-start(f32[576,128]{1,0:T(8,128)S(1)} %bitcast_add_fusion.9), channel_id=1, source_target_pairs={{0,8},{8,16},{16,24},{24,28},{28,20},{20,12},{12,4},{4,0},{1,9},{9... | collective-permute-start | bytes 884744 | tf_op jit(solution)/shard_map/ppermute | solution.py:507
  48.1 18.4 %collective-permute-start.16 = (f32[576,128]{1,0:T(8,128)S(1)}, f32[576,128]{1,0:T(8,128)S(1)}, u32[]{:S(2)}, u32[]{:S(2)}) collective-permute-start(f32[576,128]{1,0:T(8,128)S(1)} %bitcast_add_fusion.6), channel_id=1, source_target_pairs={{8,0},{16,8},{24,16},{28,24},{20,28},{12,20},{4,12},{0,4},{9,1},{1... | collective-permute-start | bytes 884744 | tf_op jit(solution)/shard_map/ppermute | solution.py:507
  49.2 17.3 %collective-permute-start.15 = (f32[576,128]{1,0:T(8,128)S(1)}, f32[576,128]{1,0:T(8,128)S(1)}, u32[]{:S(2)}, u32[]{:S(2)}) collective-permute-start(f32[576,128]{1,0:T(8,128)S(1)} %bitcast_add_fusion.7), channel_id=1, source_target_pairs={{0,8},{8,16},{16,24},{24,28},{28,20},{20,12},{12,4},{4,0},{1,9},{9... | collective-permute-start | bytes 884744 | tf_op jit(solution)/shard_map/ppermute | solution.py:507
  67.5 12.0 %collective-permute-start.18 = (f32[576,128]{1,0:T(8,128)S(1)}, f32[576,128]{1,0:T(8,128)S(1)}, u32[]{:S(2)}, u32[]{:S(2)}) collective-permute-start(f32[576,128]{1,0:T(8,128)S(1)} %bitcast_add_fusion.4), channel_id=1, source_target_pairs={{8,0},{16,8},{24,16},{28,24},{20,28},{12,20},{4,12},{0,4},{9,1},{1... | collective-permute-start | bytes 884744 | tf_op jit(solution)/shard_map/ppermute | solution.py:507
  81.3 9.6 %collective-permute-start.20 = (f32[576,128]{1,0:T(8,128)S(1)}, f32[576,128]{1,0:T(8,128)S(1)}, u32[]{:S(2)}, u32[]{:S(2)}) collective-permute-start(f32[576,128]{1,0:T(8,128)S(1)} %bitcast_add_fusion.2), channel_id=1, source_target_pairs={{8,0},{16,8},{24,16},{28,24},{20,28},{12,20},{4,12},{0,4},{9,1},{1... | collective-permute-start | bytes 884744 | tf_op jit(solution)/shard_map/ppermute | solution.py:507
  109.5 10.8 %collective-permute-start.27 = (f32[544,128]{1,0:T(8,128)}, f32[544,128]{1,0:T(8,128)S(1)}, u32[]{:S(2)}, u32[]{:S(2)}) collective-permute-start(f32[544,128]{1,0:T(8,128)} %get-tuple-element.164.up_ref.refs_0_), channel_id=1, source_target_pairs={{0,8},{8,16},{16,24},{24,28},{28,20},{20,12},{12,4},{4,0},{1,9},{9... | collective-permute-start | bytes 835592 | tf_op jit(solution)/shard_map/ppermute | solution.py:507
  109.8 10.5 %collective-permute-start.28 = (f32[544,128]{1,0:T(8,128)}, f32[544,128]{1,0:T(8,128)S(1)}, u32[]{:S(2)}, u32[]{:S(2)}) collective-permute-start(f32[544,128]{1,0:T(8,128)} %get-tuple-element.165.dn_ref.refs_8_), channel_id=1, source_target_pairs={{8,0},{16,8},{24,16},{28,24},{20,28},{12,20},{4,12},{0,4},{9,1},{1... | collective-permute-start | bytes 835592 | tf_op jit(solution)/shard_map/ppermute | solution.py:507
  120.3 10.2 %collective-permute-start.30 = (f32[544,128]{1,0:T(8,128)S(1)}, f32[544,128]{1,0:T(8,128)S(1)}, u32[]{:S(2)}, u32[]{:S(2)}) collective-permute-start(f32[544,128]{1,0:T(8,128)S(1)} %collective-permute-done.27.refs_1_), channel_id=1, source_target_pairs={{0,8},{8,16},{16,24},{24,28},{28,20},{20,12},{12,4},{4,0},{1,9},{9... | collective-permute-start | bytes 835592 | tf_op jit(solution)/shard_map/ppermute | solution.py:507
  120.4 10.1 %collective-permute-start.31 = (f32[544,128]{1,0:T(8,128)S(1)}, f32[544,128]{1,0:T(8,128)S(1)}, u32[]{:S(2)}, u32[]{:S(2)}) collective-permute-start(f32[544,128]{1,0:T(8,128)S(1)} %collective-permute-done.28.refs_9_), channel_id=1, source_target_pairs={{8,0},{16,8},{24,16},{28,24},{20,28},{12,20},{4,12},{0,4},{9,1},{1... | collective-permute-start | bytes 835592 | tf_op jit(solution)/shard_map/ppermute | solution.py:507
  130.5 16.5 %collective-permute-start.36 = (f32[544,128]{1,0:T(8,128)S(1)}, f32[544,128]{1,0:T(8,128)S(1)}, u32[]{:S(2)}, u32[]{:S(2)}) collective-permute-start(f32[544,128]{1,0:T(8,128)S(1)} %collective-permute-done.30.refs_2_), channel_id=1, source_target_pairs={{0,8},{8,16},{16,24},{24,28},{28,20},{20,12},{12,4},{4,0},{1,9},{9... | collective-permute-start | bytes 835592 | tf_op jit(solution)/shard_map/ppermute | solution.py:507
  130.8 16.2 %collective-permute-start.37 = (f32[544,128]{1,0:T(8,128)S(1)}, f32[544,128]{1,0:T(8,128)S(1)}, u32[]{:S(2)}, u32[]{:S(2)}) collective-permute-start(f32[544,128]{1,0:T(8,128)S(1)} %collective-permute-done.31.refs_10_), channel_id=1, source_target_pairs={{8,0},{16,8},{24,16},{28,24},{20,28},{12,20},{4,12},{0,4},{9,1},{1... | collective-permute-start | bytes 835592 | tf_op jit(solution)/shard_map/ppermute | solution.py:507
  147.0 10.1 %collective-permute-start.38 = (f32[544,128]{1,0:T(8,128)S(1)}, f32[544,128]{1,0:T(8,128)S(1)}, u32[]{:S(2)}, u32[]{:S(2)}) collective-permute-start(f32[544,128]{1,0:T(8,128)S(1)} %collective-permute-done.36.refs_3_), channel_id=1, source_target_pairs={{0,8},{8,16},{16,24},{24,28},{28,20},{20,12},{12,4},{4,0},{1,9},{9... | collective-permute-start | bytes 835592 | tf_op jit(solution)/shard_map/ppermute | solution.py:507
  147.1 10.0 %collective-permute-start.39 = (f32[544,128]{1,0:T(8,128)S(1)}, f32[544,128]{1,0:T(8,128)S(1)}, u32[]{:S(2)}, u32[]{:S(2)}) collective-permute-start(f32[544,128]{1,0:T(8,128)S(1)} %collective-permute-done.37.refs_11_), channel_id=1, source_target_pairs={{8,0},{16,8},{24,16},{28,24},{20,28},{12,20},{4,12},{0,4},{9,1},{1... | collective-permute-start | bytes 835592 | tf_op jit(solution)/shard_map/ppermute | solution.py:507
  157.2 9.4 %collective-permute-start.40 = (f32[544,128]{1,0:T(8,128)S(1)}, f32[544,128]{1,0:T(8,128)S(1)}, u32[]{:S(2)}, u32[]{:S(2)}) collective-permute-start(f32[544,128]{1,0:T(8,128)S(1)} %collective-permute-done.38.refs_4_), channel_id=1, source_target_pairs={{0,8},{8,16},{16,24},{24,28},{28,20},{20,12},{12,4},{4,0},{1,9},{9... | collective-permute-start | bytes 835592 | tf_op jit(solution)/shard_map/ppermute | solution.py:507
  157.5 9.0 %collective-permute-start.41 = (f32[544,128]{1,0:T(8,128)S(1)}, f32[544,128]{1,0:T(8,128)S(1)}, u32[]{:S(2)}, u32[]{:S(2)}) collective-permute-start(f32[544,128]{1,0:T(8,128)S(1)} %collective-permute-done.39.refs_12_), channel_id=1, source_target_pairs={{8,0},{16,8},{24,16},{28,24},{20,28},{12,20},{4,12},{0,4},{9,1},{1... | collective-permute-start | bytes 835592 | tf_op jit(solution)/shard_map/ppermute | solution.py:507
  166.5 13.3 %collective-permute-start.46 = (f32[544,128]{1,0:T(8,128)S(1)}, f32[544,128]{1,0:T(8,128)S(1)}, u32[]{:S(2)}, u32[]{:S(2)}) collective-permute-start(f32[544,128]{1,0:T(8,128)S(1)} %collective-permute-done.40.refs_5_), channel_id=1, source_target_pairs={{0,8},{8,16},{16,24},{24,28},{28,20},{20,12},{12,4},{4,0},{1,9},{9... | collective-permute-start | bytes 835592 | tf_op jit(solution)/shard_map/ppermute | solution.py:507
  166.9 13.0 %collective-permute-start.47 = (f32[544,128]{1,0:T(8,128)S(1)}, f32[544,128]{1,0:T(8,128)S(1)}, u32[]{:S(2)}, u32[]{:S(2)}) collective-permute-start(f32[544,128]{1,0:T(8,128)S(1)} %collective-permute-done.41.refs_13_), channel_id=1, source_target_pairs={{8,0},{16,8},{24,16},{28,24},{20,28},{12,20},{4,12},{0,4},{9,1},{1... | collective-permute-start | bytes 835592 | tf_op jit(solution)/shard_map/ppermute | solution.py:507
  179.9 13.5 %collective-permute-start.50 = (f32[544,128]{1,0:T(8,128)S(1)}, f32[544,128]{1,0:T(8,128)S(1)}, u32[]{:S(2)}, u32[]{:S(2)}) collective-permute-start(f32[544,128]{1,0:T(8,128)S(1)} %collective-permute-done.46.refs_6_), channel_id=1, source_target_pairs={{0,8},{8,16},{16,24},{24,28},{28,20},{20,12},{12,4},{4,0},{1,9},{9... | collective-permute-start | bytes 835592 | tf_op jit(solution)/shard_map/ppermute | solution.py:507
  180.2 13.1 %collective-permute-start.51 = (f32[544,128]{1,0:T(8,128)S(1)}, f32[544,128]{1,0:T(8,128)S(1)}, u32[]{:S(2)}, u32[]{:S(2)}) collective-permute-start(f32[544,128]{1,0:T(8,128)S(1)} %collective-permute-done.47.refs_14_), channel_id=1, source_target_pairs={{8,0},{16,8},{24,16},{28,24},{20,28},{12,20},{4,12},{0,4},{9,1},{1... | collective-permute-start | bytes 835592 | tf_op jit(solution)/shard_map/ppermute | solution.py:507
  (50 other events, 450.6 us)
where the time goes:
time: 212 us; the launch traced here: 210 us
  waiting for transfers between devices  71.8 us (34%)
  Pallas kernels  66.9 us (32%)
  starting transfers between devices  51.3 us (24%)
  other arithmetic  16.1 us (8%)
  local copies, waits for them, and re-layouts  2.9 us (1%)
    ppermute x24, waiting for transfers between devices, flip(): return lax.ppermute(x, axis, [(i, i ^ bits) for i in range(size)])  64.2 us
    ppermute x28, starting transfers between devices, step(): return (lax.ppermute(up, 'rep', ahead), lax.ppermute(dn, 'rep', back))  32.4 us
    ppermute x24, starting transfers between devices, flip(): return lax.ppermute(x, axis, [(i, i ^ bits) for i in range(size)])  18.9 us
    pallas_call x2, Pallas kernels, orth_first(): pl.pallas_call(functools.partial(first_kernel, scaled), out_shape=shapes,...  15.8 us
    pallas_call x1, Pallas kernels, finish(): pl.pallas_call(functools.partial(finish_kernel, n, rate), out_shape=[jax....  15.5 us
    pallas_call x2, Pallas kernels, orth_second(): pl.pallas_call(second_kernel, out_shape=[jax.ShapeDtypeStruct((rows, rank...  14.5 us
    pallas_call x1, Pallas kernels, combine(): pl.pallas_call(functools.partial(combine_kernel, count, 1.0 / n), out_sha...  9.48 us
    ppermute x28, waiting for transfers between devices, step(): return (lax.ppermute(up, 'rep', ahead), lax.ppermute(dn, 'rep', back))  7.65 us
  transfers between devices with their start and end apart: 52, of which 22 were waited for; matrix products, arithmetic and copies ran while one was open for 5% of the time, Pallas kernels for 20%

commit v1 on v0

--- a/solution.py
+++ b/solution.py
@@ -39,6 +39,10 @@
         return lax.dot_general(x, y, (((ca,), (cb,)), ((), ())), preferred_element_type=F32)
 
     return one(a[0], b[0]) + (one(a[0], b[1]) + one(a[1], b[0]))
+
+
+def grant(mib):
+    return pltpu.CompilerParams(vmem_limit_bytes=mib << 20)
 
 
 def cost(flops, moved):
@@ -155,11 +159,18 @@
     rest_ref[...] = jnp.concatenate(rest, axis=1)
 
 
-def second_kernel(left_ref, rest_ref, out_ref, outt_ref):
+def second_kernel(left_ref, rest_ref, *refs):
+    out_ref, outt_ref = refs[-2:] if len(refs) == 2 else refs[2:4]
     done = orthonormal_blocks(column_blocks(rest_ref[...]))
     left = jnp.concatenate([left_ref[...]] + done, axis=1)
+    leftt = left.T
     out_ref[...] = left
-    outt_ref[...] = left.T
+    outt_ref[...] = leftt
+    if len(refs) > 2:
+        rank = leftt.shape[0]
+        averaged = jnp.concatenate([refs[0][rank:], refs[1][rank:]], axis=1)
+        right = dot(leftt, averaged)
+        refs[4][...] = dot(jnp.ones((8, right.shape[1]), F32), right * right, 1, 1)
 
 
 def orth_first(me, parts, rows, scaled):
@@ -173,23 +184,28 @@
         out_specs=[VMEM] * len(shapes),
         scratch_shapes=[pltpu.VMEM((rows, rank), F32)],
         cost_estimate=cost(6e9, 1e6),
+        compiler_params=grant(12),
         name="orth_first",
     )(me, *parts)
 
 
-def orth_second(left, rest):
+def orth_second(left, rest, *mine):
     rows, rank = left.shape[0], left.shape[1] + rest.shape[1]
+    shapes = [
+        jax.ShapeDtypeStruct((rows, rank), F32),
+        jax.ShapeDtypeStruct((rank, rows), F32),
+    ]
+    if mine:
+        shapes.append(jax.ShapeDtypeStruct((8, rank), F32))
     return pl.pallas_call(
         second_kernel,
-        out_shape=[
-            jax.ShapeDtypeStruct((rows, rank), F32),
-            jax.ShapeDtypeStruct((rank, rows), F32),
-        ],
-        in_specs=[VMEM] * 2,
-        out_specs=[VMEM] * 2,
+        out_shape=shapes,
+        in_specs=[VMEM] * (2 + len(mine)),
+        out_specs=[VMEM] * len(shapes),
         cost_estimate=cost(6e9, 1e6),
+        compiler_params=grant(12),
         name="orth_second",
-    )(left, rest)
+    )(left, rest, *mine)
 
 
 def chunk_rows(mom, grads):
@@ -219,13 +235,58 @@
             out_specs=[whole((2 * rows, w))] * 2,
         ),
         cost_estimate=cost(4 * rows * w, 32 * rows * w),
+        compiler_params=grant(58),
         name="lead",
     )(at, momentum, grads, momentum, grads)
 
 
-def combine_kernel(count, inv, me_ref, mom_ref, grads_ref, right_ref, up_ref, dn_ref, both_ref, *refs):
+def raw_kernel(count, inv, me_ref, mom_ref, grads_ref, right_ref, *refs):
     parts, acc_ref = refs[:count], refs[count]
     k = pl.program_id(0)
+    rows = mom_ref.shape[1]
+    part = dot(mom_ref[0] + grads_ref[0, 0].astype(F32), right_ref[...])
+
+    @pl.when(k == 0)
+    def _():
+        acc_ref[...] = part
+
+    @pl.when(k > 0)
+    def _():
+        acc_ref[...] += part
+
+    @pl.when(k == pl.num_programs(0) - 1)
+    def _():
+        acc_ref[...] *= inv
+        block = rows // count
+        for d in range(count):
+            at = pl.multiple_of((me_ref[0] ^ d) * block, 8)
+            parts[d][...] = acc_ref[pl.ds(at, block), :]
+
+
+def raw(me, momentum, grads, right_factor, n, count):
+    _, rows, cols = momentum.shape
+    rank = right_factor.shape[1]
+    w = 2 * cols // n
+    part = jax.ShapeDtypeStruct((rows // count, rank), F32)
+    return pl.pallas_call(
+        functools.partial(raw_kernel, count, 1.0 / n),
+        out_shape=[part] * count,
+        grid=(n // 2,),
+        in_specs=[
+            SMEM,
+            pl.BlockSpec((1, rows, w), lambda k: (0, 0, k)),
+            pl.BlockSpec((1, 1, rows, w), lambda k: (0, 0, 0, k)),
+            pl.BlockSpec((w, rank), lambda k: (k, 0)),
+        ],
+        out_specs=[pl.BlockSpec((rows // count, rank), lambda k: (0, 0))] * count,
+        scratch_shapes=[pltpu.VMEM((rows, rank), F32)],
+        cost_estimate=cost(12 * rows * cols * rank, 8 * rows * cols),
+        compiler_params=grant(16),
+        name="raw",
+    )(me, momentum, grads, right_factor)
+
+
+def combine_kernel(mom_ref, grads_ref, after_ref, up_ref, dn_ref, both_ref):
     rows = mom_ref.shape[1]
     total = mom_ref[0] + grads_ref[0, 0].astype(F32)
     later = grads_ref[1, 0].astype(F32)
@@ -235,52 +296,30 @@
     dn_ref[0, :rows] = total[:, w:]
     up_ref[0, rows:] = later[:, :w]
     dn_ref[0, rows:] = later[:, w:]
-    part = dot(total, right_ref[...])
-
-    @pl.when(k == 0)
-    def _():
-        acc_ref[...] = part
-
-    @pl.when(k > 0)
-    def _():
-        acc_ref[...] += part
-
-    @pl.when(k == pl.num_programs(0) - 1)
-    def _():
-        acc_ref[...] *= inv
-        block = rows // count
-        for d in range(count):
-            at = pl.multiple_of((me_ref[0] ^ d) * block, 8)
-            parts[d][...] = acc_ref[pl.ds(at, block), :]
-
-
-def combine(me, momentum, grads, right_factor, n, count):
+
+
+def combine(momentum, grads, after, n):
     _, rows, cols = momentum.shape
-    rank = right_factor.shape[1]
     w = cols // n
     chunks = jax.ShapeDtypeStruct((n, 2 * rows, w // 2), F32)
-    part = jax.ShapeDtypeStruct((rows // count, rank), F32)
-    out = pl.pallas_call(
-        functools.partial(combine_kernel, count, 1.0 / n),
-        out_shape=[chunks, chunks, jax.ShapeDtypeStruct((rows, cols), F32)] + [part] * count,
+    return pl.pallas_call(
+        combine_kernel,
+        out_shape=[chunks, chunks, jax.ShapeDtypeStruct((rows, cols), F32)],
         grid=(n,),
         in_specs=[
-            SMEM,
             pl.BlockSpec((1, rows, w), lambda k: (0, 0, k)),
             pl.BlockSpec((2, 1, rows, w), lambda k: (0, 0, 0, k)),
-            pl.BlockSpec((w, rank), lambda k: (k, 0)),
+            pl.BlockSpec(memory_space=pl.ANY),
         ],
         out_specs=[
             pl.BlockSpec((1, 2 * rows, w // 2), lambda k: (k, 0, 0)),
             pl.BlockSpec((1, 2 * rows, w // 2), lambda k: (k, 0, 0)),
             pl.BlockSpec((rows, w), lambda k: (0, k)),
-        ]
-        + [pl.BlockSpec((rows // count, rank), lambda k: (0, 0))] * count,
-        scratch_shapes=[pltpu.VMEM((rows, rank), F32)],
-        cost_estimate=cost(12 * rows * cols * rank, 16 * rows * cols),
+        ],
+        cost_estimate=cost(3 * rows * cols, 20 * rows * cols),
+        compiler_params=grant(16),
         name="combine",
-    )(me, momentum, grads, right_factor)
-    return out[0], out[1], out[2], out[3:]
+    )(momentum, grads, after)
 
 
 def reduced_kernel(inv, at_ref, up_ref, dn_ref, up_all, dn_all, left_ref, leftt_ref, up_out, dn_out):
@@ -312,6 +351,7 @@
             out_specs=[whole(ring.shape)] * 2,
         ),
         cost_estimate=cost(24 * rows * rank * rank, 4e6),
+        compiler_params=grant(12),
         name="reduced",
     )(place, up, dn, up_all, dn_all, left, leftt)
 
@@ -340,26 +380,9 @@
         out_specs=[VMEM] * count,
         scratch_shapes=[pltpu.VMEM((rows, rank), F32)],
         cost_estimate=cost(12 * rows * rank * rank, 2e6),
+        compiler_params=grant(8),
         name="partial",
     )(me, up, dn)
-
-
-def squares_kernel(rank, up_ref, dn_ref, leftt_ref, out_ref):
-    averaged = jnp.concatenate([up_ref[rank:], dn_ref[rank:]], axis=1)
-    right = dot(leftt_ref[...], averaged)
-    out_ref[...] = dot(jnp.ones((8, right.shape[1]), F32), right * right, 1, 1)
-
-
-def squares_of(up, dn, leftt):
-    rank = leftt.shape[0]
-    return pl.pallas_call(
-        functools.partial(squares_kernel, rank),
-        out_shape=jax.ShapeDtypeStruct((8, rank), F32),
-        in_specs=[VMEM] * 3,
-        out_specs=VMEM,
-        cost_estimate=cost(12 * rank * rank * rank, 2e6),
-        name="squares",
-    )(up, dn, leftt)
 
 
 def fetcher(n, ups, dns, buf, sem):
@@ -430,7 +453,7 @@
         grid_spec=pltpu.PrefetchScalarGridSpec(
             num_scalar_prefetch=1,
             grid=(n,),
-            in_specs=[pl.BlockSpec(memory_space=pl.ANY)] * len(rings)
+            in_specs=[VMEM] * len(rings)
             + [block, block, whole((rows, rank)), whole((rows, rank)), whole((rank, rows))]
             + [whole((1, rank)), whole((8, rank))],
             out_specs=[
@@ -446,6 +469,7 @@
             ],
         ),
         cost_estimate=cost(30 * rows * cols * rank, 32 * rows * cols),
+        compiler_params=grant(28),
         name="finish",
     )(order, *rings, both, weights, l1, l2, l2t, norm, totals)
 
@@ -506,28 +530,31 @@
     def step(up, dn):
         return lax.ppermute(up, "rep", ahead), lax.ppermute(dn, "rep", back)
 
-    def windows(box, scaled):
-        stages = all_sum_stages(box)
-
-        def first():
+    def first(scaled):
+        def stage():
             out = orth_first(me, box.pop("parts"), rows, scaled)
             box.pop("x")
             box["left"], box["rest"] = out[:2]
             if scaled:
                 box["norm"] = out[2]
 
-        def second():
-            box["left"], box["leftt"] = orth_second(box.pop("left"), box.pop("rest"))
-
-        return [stages[:2]] + [[s] for s in stages[2:-2]] + [stages[-2:], [first], [second]]
+        return stage
 
     box = {}
+    scatter, *bits, gather = all_sum_stages(box)
+
+    def begin():
+        box["parts"] = list(raw(me, momentum, grads, right_factor, n, count))
 
     def prepare():
-        up_all, dn_all, both, parts = combine(me, momentum, grads, right_factor, n, count)
-        box.update(up_all=up_all, dn_all=dn_all, both=both, parts=list(parts))
-
-    work = [[prepare]] + windows(box, False)
+        after = box["parts"][0]
+        box["up_all"], box["dn_all"], box["both"] = combine(momentum, grads, after, n)
+
+    def second():
+        box["left"], box["leftt"] = orth_second(box.pop("left"), box.pop("rest"))
+
+    work = [[begin, prepare, scatter]] + [[bit] for bit in bits] + [[first(False)], [second]]
+    work[len(bits)].append(gather)
     up, dn = lead(lax.rem(jnp.stack([place + n - 1, place + 1]), n), momentum, grads, n)
     for k in range(1, n):
         up, dn = step(up, dn)
@@ -537,37 +564,35 @@
             up, dn = tie(box, up, dn)
         if k < n - 1:
             up, dn = up + chunk(box["up_all"], -1 - k), dn + chunk(box["dn_all"], 1 + k)
-    for stage in sum(work, []):
-        stage()
     l1 = box["left"]
     both = box["both"]
     up, dn = reduced(place[None], up, dn, box["up_all"], box["dn_all"], l1, box["leftt"], n)
 
     box = {}
     mine = (up, dn)
-
-    def begin():
+    scatter, *bits, gather = all_sum_stages(box)
+
+    def begin_again():
         box["parts"] = list(partial_raw(me, *mine, rank, count))
 
+    def second_again():
+        box["left"], box["leftt"], box["total"] = orth_second(box.pop("left"), box.pop("rest"), *mine)
+
     def total_columns():
-        x = squares_of(*mine, box["leftt"])
-        got = [flip(x, "col", d) for d in range(1, count)]
-        terms = [x] + got
-        while len(terms) > 1:
-            terms = [a + b for a, b in zip(terms[::2], terms[1::2])]
-        box["total"] = terms[0]
-
-    def total_bit(bit):
+        got = [flip(box["total"], "col", d) for d in range(1, count)]
+        box["total"] = alike([box["total"]] + got)
+
+    def total_bits(masks):
         def stage():
-            got = flip(box["total"], "rep", 1 << bit)
-            box["total"] = box["total"] + got
+            got = [flip(box["total"], "rep", m) for m in masks]
+            box["total"] = alike([box["total"]] + got)
 
         return stage
 
-    work = windows(box, True)
-    work[0].insert(0, begin)
-    bits = [total_bit(b) for b in range(n.bit_length() - 1)]
-    work += [[total_columns, bits[0]], bits[1:]]
+    work = [[begin_again, scatter, bits[0]]] + [[bit] for bit in bits[1:]]
+    work[-1].append(gather)
+    work += [[first(True)], [second_again, total_columns], [total_bits([1, 2, 3])]]
+    work += [[total_bits([1 << b])] for b in range(2, n.bit_length() - 1)]
     ups, dns = [up], [dn]
     for _ in range(1, n):
         up, dn = step(up, dn)
@@ -577,12 +602,16 @@
             up, dn = tie(box, up, dn)
         ups.append(up)
         dns.append(dn)
-    for stage in sum(work, []):
-        stage()
     new_momentum, new_weights, new_right = finish(
         order, ups + dns, both, weights, l1, box["left"], box["leftt"], box["norm"], box["total"], rate
     )
     return new_weights, new_momentum, new_right
+
+
+def alike(terms):
+    while len(terms) > 1:
+        terms = [a + b for a, b in zip(terms[::2], terms[1::2])]
+    return terms[0]
 
 
 def plain_orthonormal(left_raw):

time: 212 us -> 198 us (0.934)
  Pallas kernels: 66.9 us -> 48 us
  other arithmetic: 16.1 us -> 9.54 us
  local copies, waits for them, and re-layouts: 2.9 us -> 8 us
  waiting for transfers between devices: 71.8 us -> 76 us
  starting transfers between devices: 51.3 us -> 54.5 us
    pallas_call x4, Pallas kernels: 27 us -> 16.9 us  [the longest x2 12.2 us: orth_second(): pl.pallas_call(second_kernel, out_shape=shapes, in_specs=[VMEM] * (2 + le...]
    ppermute x28, waiting for transfers between devices: 7.65 us -> 13.2 us  [step(): return (lax.ppermute(up, 'rep', ahead), lax.ppermute(dn, 'rep', back))]
    unnamed x44 -> x24, local copies, waits for them, and re-layouts: 2.9 us -> 8 us
    pallas_call x2, Pallas kernels: 15.8 us -> 12.5 us  [orth_first(): pl.pallas_call(functools.partial(first_kernel, scaled), out_shape=shapes,...]
    ppermute x24 -> x25, starting transfers between devices: 18.9 us -> 22.1 us  [flip(): return lax.ppermute(x, axis, [(i, i ^ bits) for i in range(size)])]
    add x6, other arithmetic: 5.96 us -> 3.09 us  [ring_shards(): dn + chunk(box['dn_all'], 1 + k)]
    pallas_call x1, Pallas kernels: 3.65 us -> 1.39 us  [reduced(): pl.pallas_call(functools.partial(reduced_kernel, 1.0 / n), out_shape=[rin...]
    ppermute x24 -> x25, waiting for transfers between devices: 64.2 us -> 62.8 us  [flip(): return lax.ppermute(x, axis, [(i, i ^ bits) for i in range(size)])]
  transfers between devices with their start and end apart: 52 -> 53, of which waited for: 22 -> 26; matrix products, arithmetic and copies ran while one was open for 5% -> 3% of each run, Pallas kernels for 20% -> 15%
where the time goes in v1:
time: 198 us; the launch traced here: 197 us
  waiting for transfers between devices  76 us (38%)
  starting transfers between devices  54.5 us (28%)
  Pallas kernels  48 us (24%)
  other arithmetic  9.54 us (5%)
  local copies, waits for them, and re-layouts  8 us (4%)
    ppermute x25, waiting for transfers between devices, flip(): return lax.ppermute(x, axis, [(i, i ^ bits) for i in range(size)])  62.8 us
    ppermute x28, starting transfers between devices, step(): return (lax.ppermute(up, 'rep', ahead), lax.ppermute(dn, 'rep', back))  32.4 us
    ppermute x25, starting transfers between devices, flip(): return lax.ppermute(x, axis, [(i, i ^ bits) for i in range(size)])  22.1 us
    pallas_call x1, Pallas kernels, finish(): pl.pallas_call(functools.partial(finish_kernel, n, rate), out_shape=[jax....  13.9 us
    ppermute x28, waiting for transfers between devices, step(): return (lax.ppermute(up, 'rep', ahead), lax.ppermute(dn, 'rep', back))  13.2 us
    pallas_call x2, Pallas kernels, orth_first(): pl.pallas_call(functools.partial(first_kernel, scaled), out_shape=shapes,...  12.5 us
    pallas_call x2, Pallas kernels, orth_second(): pl.pallas_call(second_kernel, out_shape=shapes, in_specs=[VMEM] * (2 + le...  12.2 us
    unnamed x24, local copies, waits for them, and re-layouts  8 us
  transfers between devices with their start and end apart: 53, of which 26 were waited for; matrix products, arithmetic and copies ran while one was open for 3% of the time, Pallas kernels for 15%

profile of v1, /device:TPU:0, one launch (start us, length us, event | category | flops | bytes accessed | tf_op | source)
XLA Modules:
  0.0 197.3 jit_solution(10939493426362491733)
XLA Ops:
  5.6 3.4 %raw.1 = (f32[72,256]{1,0:T(8,128)S(1)}, f32[72,256]{1,0:T(8,128)S(1)}, f32[72,256]{1,0:T(8,128)S(1)}, f32[72,256]{1,0:T(8,128)S(1)}) custom-call(s32[1]{0:T(128)} %bitcast.1.me_ref, f32[1,288,2048]{2,1,0:T(8,128)S(1)} %copy-done, bf16[2,1,288,2048]{3,2,1,0:T(8,128)(2,1)S(1)} %copy-done.2, f32[2048,256]{1,0:T(8,128)S(1)} %copy-done.8), custom_call_target="tpu_custom_call" | custom-call | flops 1811939328 | bytes 4718592 | tf_op jit(solution)/shard_map/raw/pallas_call | solution.py:271
  9.6 2.6 %collective-permute-start.1 = (f32[72,256]{1,0:T(8,128)S(1)}, f32[72,256]{1,0:T(8,128)S(1)}, u32[]{:S(2)}, u32[]{:S(2)}) collective-permute-start(f32[72,256]{1,0:T(8,128)S(1)} %get-tuple-element.109), channel_id=1, source_target_pairs={{0,2},{1,3},{2,0},{3,1},{4,6},{5,7},{6,4},{7,5},{8,10},{9,11},{10,... | collective-permute-start | bytes 221192 | tf_op jit(solution)/shard_map/ppermute | solution.py:483
  12.7 2.8 %lead.1 = (f32[576,128]{1,0:T(8,128)}, f32[576,128]{1,0:T(8,128)}) custom-call(s32[2]{0:T(128)} %compare_select_fusion.at_ref, f32[1,288,2048]{2,1,0:T(8,128)} %mom_dn.1, bf16[2,1,288,2048]{3,2,1,0:T(8,128)(2,1)} %grads_dn.1, f32[1,288,2048]{2,1,0:T(8,128)} %mom_dn.1, bf16[2,1,288,2048]{3,2,1,0:T(8,128)(2,1)} %grads_dn.1), custom_call_target="tpu_custom_call" | custom-call | flops 147456 | bytes 1179648 | tf_op jit(solution)/shard_map/lead/pallas_call | solution.py:228
  22.6 2.4 %collective-permute-done.3 = f32[576,128]{1,0:T(8,128)S(1)} collective-permute-done((f32[576,128]{1,0:T(8,128)}, f32[576,128]{1,0:T(8,128)S(1)}, u32[]{:S(2)}, u32[]{:S(2)}) %collective-permute-start.3) | collective-permute-done | bytes 294944 | tf_op jit(solution)/shard_map/ppermute | solution.py:531
  29.1 7.7 %collective-permute-done.5 = f32[72,256]{1,0:T(8,128)} collective-permute-done((f32[72,256]{1,0:T(8,128)}, f32[72,256]{1,0:T(8,128)}, u32[]{:S(2)}, u32[]{:S(2)}) %collective-permute-start.5) | collective-permute-done | bytes 73760 | tf_op jit(solution)/shard_map/ppermute | solution.py:483
  43.2 6.2 %collective-permute-done.8 = f32[72,256]{1,0:T(8,128)S(1)} collective-permute-done((f32[72,256]{1,0:T(8,128)}, f32[72,256]{1,0:T(8,128)S(1)}, u32[]{:S(2)}, u32[]{:S(2)}) %collective-permute-start.8) | collective-permute-done | bytes 73760 | tf_op jit(solution)/shard_map/ppermute | solution.py:483
  54.5 2.1 %collective-permute-start.11 = (f32[72,256]{1,0:T(8,128)S(1)}, f32[72,256]{1,0:T(8,128)S(1)}, u32[]{:S(2)}, u32[]{:S(2)}) collective-permute-start(f32[72,256]{1,0:T(8,128)S(1)} %add.230), channel_id=1, source_target_pairs={{0,16},{4,20},{8,24},{12,28},{16,0},{20,4},{24,8},{28,12},{1,17},{... | collective-permute-start | bytes 221192 | tf_op jit(solution)/shard_map/ppermute | solution.py:483
  56.6 5.7 %collective-permute-done.11 = f32[72,256]{1,0:T(8,128)S(1)} collective-permute-done((f32[72,256]{1,0:T(8,128)S(1)}, f32[72,256]{1,0:T(8,128)S(1)}, u32[]{:S(2)}, u32[]{:S(2)}) %collective-permute-start.11) | collective-permute-done | bytes 73760 | tf_op jit(solution)/shard_map/ppermute | solution.py:483
  64.3 2.7 %collective-permute-done.14.refs_3_ = f32[72,256]{1,0:T(8,128)S(1)} collective-permute-done((f32[72,256]{1,0:T(8,128)S(1)}, f32[72,256]{1,0:T(8,128)S(1)}, u32[]{:S(2)}, u32[]{:S(2)}) %collective-permute-start.14) | collective-permute-done | bytes 73760 | tf_op jit(solution)/shard_map/ppermute | solution.py:483
  69.2 4.8 %collective-permute-start.18 = (f32[576,128]{1,0:T(8,128)S(1)}, f32[576,128]{1,0:T(8,128)S(1)}, u32[]{:S(2)}, u32[]{:S(2)}) collective-permute-start(f32[576,128]{1,0:T(8,128)S(1)} %bitcast_add_fusion.4), channel_id=1, source_target_pairs={{8,0},{16,8},{24,16},{28,24},{20,28},{12,20},{4,12},{0,4},{9,1},{1... | collective-permute-start | bytes 884744 | tf_op jit(solution)/shard_map/ppermute | solution.py:531
  74.1 6.2 %orth_first.2 = (f32[288,128]{1,0:T(8,128)S(1)}, f32[288,128]{1,0:T(8,128)S(1)}) custom-call(s32[1]{0:T(128)} %bitcast.1.me_ref, f32[72,256]{1,0:T(8,128)S(1)} %add.237.refs_0_, f32[72,256]{1,0:T(8,128)S(1)} %collective-permute-done.12.refs_1_, f32[72,256]{1,0:T(8,128)S(1)} %collective-permute-done.13.refs_2_, f32[72,256]{1,0:T(8,128)S(1)} %collective-permute-done.14.refs_3_), custom_call_target="tpu_custom_call" | custom-call | flops 6000000000 | bytes 1000000 | tf_op jit(solution)/shard_map/orth_first/pallas_call | solution.py:180
  80.5 2.3 %collective-permute-done.17 = f32[576,128]{1,0:T(8,128)S(1)} collective-permute-done((f32[576,128]{1,0:T(8,128)S(1)}, f32[576,128]{1,0:T(8,128)S(1)}, u32[]{:S(2)}, u32[]{:S(2)}) %collective-permute-start.17) | collective-permute-done | bytes 294944 | tf_op jit(solution)/shard_map/ppermute | solution.py:531
  85.2 5.5 %orth_second.2 = (f32[288,256]{1,0:T(8,128)S(1)}, f32[256,288]{1,0:T(8,128)S(1)}) custom-call(f32[288,128]{1,0:T(8,128)S(1)} %get-tuple-element.148.left_ref, f32[288,128]{1,0:T(8,128)S(1)} %get-tuple-element.149.rest_ref), custom_call_target="tpu_custom_call" | custom-call | flops 6000000000 | bytes 1000000 | tf_op jit(solution)/shard_map/orth_second/pallas_call | solution.py:200
  93.5 4.9 %collective-permute-done.22.dn_ref = f32[576,128]{1,0:T(8,128)S(1)} collective-permute-done((f32[576,128]{1,0:T(8,128)S(1)}, f32[576,128]{1,0:T(8,128)S(1)}, u32[]{:S(2)}, u32[]{:S(2)}) %collective-permute-start.22) | collective-permute-done | bytes 294944 | tf_op jit(solution)/shard_map/ppermute | solution.py:531
  107.5 6.1 %collective-permute-done.26 = f32[80,256]{1,0:T(8,128)S(1)} collective-permute-done((f32[80,256]{1,0:T(8,128)S(1)}, f32[80,256]{1,0:T(8,128)S(1)}, u32[]{:S(2)}, u32[]{:S(2)}) %collective-permute-start.26) | collective-permute-done | bytes 81952 | tf_op jit(solution)/shard_map/ppermute | solution.py:483
  116.3 7.2 %collective-permute-done.29 = f32[80,256]{1,0:T(8,128)S(1)} collective-permute-done((f32[80,256]{1,0:T(8,128)S(1)}, f32[80,256]{1,0:T(8,128)S(1)}, u32[]{:S(2)}, u32[]{:S(2)}) %collective-permute-start.29) | collective-permute-done | bytes 81952 | tf_op jit(solution)/shard_map/ppermute | solution.py:483
  125.7 2.4 %collective-permute-start.32 = (f32[80,256]{1,0:T(8,128)S(1)}, f32[80,256]{1,0:T(8,128)S(1)}, u32[]{:S(2)}, u32[]{:S(2)}) collective-permute-start(f32[80,256]{1,0:T(8,128)S(1)} %add.266), channel_id=1, source_target_pairs={{0,16},{4,20},{8,24},{12,28},{16,0},{20,4},{24,8},{28,12},{1,17},{... | collective-permute-start | bytes 245768 | tf_op jit(solution)/shard_map/ppermute | solution.py:483
  128.1 7.9 %collective-permute-done.32 = f32[80,256]{1,0:T(8,128)S(1)} collective-permute-done((f32[80,256]{1,0:T(8,128)S(1)}, f32[80,256]{1,0:T(8,128)S(1)}, u32[]{:S(2)}, u32[]{:S(2)}) %collective-permute-start.32) | collective-permute-done | bytes 81952 | tf_op jit(solution)/shard_map/ppermute | solution.py:483
  137.9 2.5 %collective-permute-done.35.refs_3_ = f32[80,256]{1,0:T(8,128)S(1)} collective-permute-done((f32[80,256]{1,0:T(8,128)S(1)}, f32[80,256]{1,0:T(8,128)S(1)}, u32[]{:S(2)}, u32[]{:S(2)}) %collective-permute-start.35) | collective-permute-done | bytes 81952 | tf_op jit(solution)/shard_map/ppermute | solution.py:483
  143.5 6.3 %orth_first.3 = (f32[288,128]{1,0:T(8,128)S(1)}, f32[288,128]{1,0:T(8,128)S(1)}, f32[1,256]{1,0:T(1,128)S(1)}) custom-call(s32[1]{0:T(128)} %bitcast.1.me_ref, f32[80,256]{1,0:T(8,128)S(1)} %add.267.refs_0_, f32[80,256]{1,0:T(8,128)S(1)} %collective-permute-done.33.refs_1_, f32[80,256]{1,0:T(8,128)S(1)} %collective-permute-done.34.refs_2_, ...), custom_call_target="tpu_custom_call" | custom-call | flops 6000000000 | bytes 1000000 | tf_op jit(solution)/shard_map/orth_first/pallas_call | solution.py:180
  152.5 6.7 %orth_second.3 = (f32[288,256]{1,0:T(8,128)S(1)}, f32[256,288]{1,0:T(8,128)S(1)}, f32[8,256]{1,0:T(8,128)S(1)}) custom-call(f32[288,128]{1,0:T(8,128)S(1)} %get-tuple-element.183.left_ref, f32[288,128]{1,0:T(8,128)S(1)} %get-tuple-element.184.rest_ref, f32[544,128]{1,0:T(8,128)S(1)} %get-tuple-element.160.up_ref.refs_0_, ...), custom_call_target="tpu_custom_call" | custom-call | flops 6000000000 | bytes 1000000 | tf_op jit(solution)/shard_map/orth_second/pallas_call | solution.py:200
  168.5 4.6 %collective-permute-done.47 = f32[8,256]{1,0:T(8,128)S(1)} collective-permute-done((f32[8,256]{1,0:T(8,128)S(1)}, f32[8,256]{1,0:T(8,128)S(1)}, u32[]{:S(2)}, u32[]{:S(2)}) %collective-permute-start.47) | collective-permute-done | bytes 8224 | tf_op jit(solution)/shard_map/ppermute | solution.py:483
  177.3 5.9 %collective-permute-done.50 = f32[8,256]{1,0:T(8,128)S(1)} collective-permute-done((f32[8,256]{1,0:T(8,128)S(1)}, f32[8,256]{1,0:T(8,128)S(1)}, u32[]{:S(2)}, u32[]{:S(2)}) %collective-permute-start.50) | collective-permute-done | bytes 8224 | tf_op jit(solution)/shard_map/ppermute | solution.py:483
  183.2 13.9 %finish.1 = (f32[1,288,2048]{2,1,0:T(8,128)}, f32[288,2048]{1,0:T(8,128)}, f32[2048,256]{1,0:T(8,128)}) custom-call(s32[8]{0:T(128)S(1)} %compare_select_fusion.2.order_ref, f32[544,128]{1,0:T(8,128)S(1)} %get-tuple-element.160.up_ref.refs_0_, f32[544,128]{1,0:T(8,128)S(1)} %collective-permute-done.27.refs_1_, ...), custom_call_target="tpu_custom_call" | custom-call | flops 4529848320 | bytes 18874368 | tf_op jit(solution)/shard_map/finish/pallas_call | solution.py:446
  (141 shorter events, 73.4 us)
Async XLA Ops:
  9.0 12.9 %collective-permute-start = (f32[72,256]{1,0:T(8,128)S(1)}, f32[72,256]{1,0:T(8,128)S(1)}, u32[]{:S(2)}, u32[]{:S(2)}) collective-permute-start(f32[72,256]{1,0:T(8,128)S(1)} %get-tuple-element.108), channel_id=1, source_target_pairs={{0,1},{1,0},{2,3},{3,2},{4,5},{5,4},{6,7},{7,6},{8,9},{9,8},{10,11... | collective-permute-start | bytes 221192 | tf_op jit(solution)/shard_map/ppermute | solution.py:483
  9.6 12.3 %collective-permute-start.1 = (f32[72,256]{1,0:T(8,128)S(1)}, f32[72,256]{1,0:T(8,128)S(1)}, u32[]{:S(2)}, u32[]{:S(2)}) collective-permute-start(f32[72,256]{1,0:T(8,128)S(1)} %get-tuple-element.109), channel_id=1, source_target_pairs={{0,2},{1,3},{2,0},{3,1},{4,6},{5,7},{6,4},{7,5},{8,10},{9,11},{10,... | collective-permute-start | bytes 221192 | tf_op jit(solution)/shard_map/ppermute | solution.py:483
  12.1 9.8 %collective-permute-start.2 = (f32[72,256]{1,0:T(8,128)S(1)}, f32[72,256]{1,0:T(8,128)S(1)}, u32[]{:S(2)}, u32[]{:S(2)}) collective-permute-start(f32[72,256]{1,0:T(8,128)S(1)} %get-tuple-element.110), channel_id=1, source_target_pairs={{0,3},{1,2},{2,1},{3,0},{4,7},{5,6},{6,5},{7,4},{8,11},{9,10},{10,... | collective-permute-start | bytes 221192 | tf_op jit(solution)/shard_map/ppermute | solution.py:483
  15.5 9.5 %collective-permute-start.3 = (f32[576,128]{1,0:T(8,128)}, f32[576,128]{1,0:T(8,128)S(1)}, u32[]{:S(2)}, u32[]{:S(2)}) collective-permute-start(f32[576,128]{1,0:T(8,128)} %get-tuple-element.114), channel_id=1, source_target_pairs={{0,8},{8,16},{16,24},{24,28},{28,20},{20,12},{12,4},{4,0},{1,9},{9... | collective-permute-start | bytes 884744 | tf_op jit(solution)/shard_map/ppermute | solution.py:531
  17.3 9.2 %collective-permute-start.4 = (f32[576,128]{1,0:T(8,128)}, f32[576,128]{1,0:T(8,128)S(1)}, u32[]{:S(2)}, u32[]{:S(2)}) collective-permute-start(f32[576,128]{1,0:T(8,128)} %get-tuple-element.115), channel_id=1, source_target_pairs={{8,0},{16,8},{24,16},{28,24},{20,28},{12,20},{4,12},{0,4},{9,1},{1... | collective-permute-start | bytes 884744 | tf_op jit(solution)/shard_map/ppermute | solution.py:531
  26.6 11.8 %collective-permute-start.7 = (f32[576,128]{1,0:T(8,128)S(1)}, f32[576,128]{1,0:T(8,128)S(1)}, u32[]{:S(2)}, u32[]{:S(2)}) collective-permute-start(f32[576,128]{1,0:T(8,128)S(1)} %bitcast_add_fusion.10), channel_id=1, source_target_pairs={{8,0},{16,8},{24,16},{28,24},{20,28},{12,20},{4,12},{0,4},{9,1},{1... | collective-permute-start | bytes 884744 | tf_op jit(solution)/shard_map/ppermute | solution.py:531
  27.0 11.4 %collective-permute-start.6 = (f32[576,128]{1,0:T(8,128)S(1)}, f32[576,128]{1,0:T(8,128)S(1)}, u32[]{:S(2)}, u32[]{:S(2)}) collective-permute-start(f32[576,128]{1,0:T(8,128)S(1)} %bitcast_add_fusion.11), channel_id=1, source_target_pairs={{0,8},{8,16},{16,24},{24,28},{28,20},{20,12},{12,4},{4,0},{1,9},{9... | collective-permute-start | bytes 884744 | tf_op jit(solution)/shard_map/ppermute | solution.py:531
  39.4 10.9 %collective-permute-start.10 = (f32[576,128]{1,0:T(8,128)S(1)}, f32[576,128]{1,0:T(8,128)S(1)}, u32[]{:S(2)}, u32[]{:S(2)}) collective-permute-start(f32[576,128]{1,0:T(8,128)S(1)} %bitcast_add_fusion.8), channel_id=1, source_target_pairs={{8,0},{16,8},{24,16},{28,24},{20,28},{12,20},{4,12},{0,4},{9,1},{1... | collective-permute-start | bytes 884744 | tf_op jit(solution)/shard_map/ppermute | solution.py:531
  41.3 9.0 %collective-permute-start.9 = (f32[576,128]{1,0:T(8,128)}, f32[576,128]{1,0:T(8,128)S(1)}, u32[]{:S(2)}, u32[]{:S(2)}) collective-permute-start(f32[576,128]{1,0:T(8,128)} %bitcast_add_fusion.9), channel_id=1, source_target_pairs={{0,8},{8,16},{16,24},{24,28},{28,20},{20,12},{12,4},{4,0},{1,9},{9... | collective-permute-start | bytes 884744 | tf_op jit(solution)/shard_map/ppermute | solution.py:531
  51.3 16.9 %collective-permute-start.16 = (f32[576,128]{1,0:T(8,128)S(1)}, f32[576,128]{1,0:T(8,128)S(1)}, u32[]{:S(2)}, u32[]{:S(2)}) collective-permute-start(f32[576,128]{1,0:T(8,128)S(1)} %bitcast_add_fusion.6), channel_id=1, source_target_pairs={{8,0},{16,8},{24,16},{28,24},{20,28},{12,20},{4,12},{0,4},{9,1},{1... | collective-permute-start | bytes 884744 | tf_op jit(solution)/shard_map/ppermute | solution.py:531
  53.2 15.0 %collective-permute-start.15 = (f32[576,128]{1,0:T(8,128)}, f32[576,128]{1,0:T(8,128)S(1)}, u32[]{:S(2)}, u32[]{:S(2)}) collective-permute-start(f32[576,128]{1,0:T(8,128)} %bitcast_add_fusion.7), channel_id=1, source_target_pairs={{0,8},{8,16},{16,24},{24,28},{28,20},{20,12},{12,4},{4,0},{1,9},{9... | collective-permute-start | bytes 884744 | tf_op jit(solution)/shard_map/ppermute | solution.py:531
  69.2 11.3 %collective-permute-start.18 = (f32[576,128]{1,0:T(8,128)S(1)}, f32[576,128]{1,0:T(8,128)S(1)}, u32[]{:S(2)}, u32[]{:S(2)}) collective-permute-start(f32[576,128]{1,0:T(8,128)S(1)} %bitcast_add_fusion.4), channel_id=1, source_target_pairs={{8,0},{16,8},{24,16},{28,24},{20,28},{12,20},{4,12},{0,4},{9,1},{1... | collective-permute-start | bytes 884744 | tf_op jit(solution)/shard_map/ppermute | solution.py:531
  102.9 10.7 %collective-permute-start.27 = (f32[544,128]{1,0:T(8,128)S(1)}, f32[544,128]{1,0:T(8,128)S(1)}, u32[]{:S(2)}, u32[]{:S(2)}) collective-permute-start(f32[544,128]{1,0:T(8,128)S(1)} %get-tuple-element.160.up_ref.refs_0_), channel_id=1, source_target_pairs={{0,8},{8,16},{16,24},{24,28},{28,20},{20,12},{12,4},{4,0},{1,9},{9... | collective-permute-start | bytes 835592 | tf_op jit(solution)/shard_map/ppermute | solution.py:531
  104.2 9.4 %collective-permute-start.28 = (f32[544,128]{1,0:T(8,128)S(1)}, f32[544,128]{1,0:T(8,128)S(1)}, u32[]{:S(2)}, u32[]{:S(2)}) collective-permute-start(f32[544,128]{1,0:T(8,128)S(1)} %get-tuple-element.161.dn_ref.refs_1_.refs_8_), channel_id=1, source_target_pairs={{8,0},{16,8},{24,16},{28,24},{20,28},{12,20},{4,12},{0,4},{9,1},{1... | collective-permute-start | bytes 835592 | tf_op jit(solution)/shard_map/ppermute | solution.py:531
  113.6 10.0 %collective-permute-start.30 = (f32[544,128]{1,0:T(8,128)S(1)}, f32[544,128]{1,0:T(8,128)S(1)}, u32[]{:S(2)}, u32[]{:S(2)}) collective-permute-start(f32[544,128]{1,0:T(8,128)S(1)} %collective-permute-done.27.refs_1_), channel_id=1, source_target_pairs={{0,8},{8,16},{16,24},{24,28},{28,20},{20,12},{12,4},{4,0},{1,9},{9... | collective-permute-start | bytes 835592 | tf_op jit(solution)/shard_map/ppermute | solution.py:531
  114.3 9.3 %collective-permute-start.31 = (f32[544,128]{1,0:T(8,128)S(1)}, f32[544,128]{1,0:T(8,128)S(1)}, u32[]{:S(2)}, u32[]{:S(2)}) collective-permute-start(f32[544,128]{1,0:T(8,128)S(1)} %collective-permute-done.28.refs_9_), channel_id=1, source_target_pairs={{8,0},{16,8},{24,16},{28,24},{20,28},{12,20},{4,12},{0,4},{9,1},{1... | collective-permute-start | bytes 835592 | tf_op jit(solution)/shard_map/ppermute | solution.py:531
  123.6 17.8 %collective-permute-start.36 = (f32[544,128]{1,0:T(8,128)S(1)}, f32[544,128]{1,0:T(8,128)S(1)}, u32[]{:S(2)}, u32[]{:S(2)}) collective-permute-start(f32[544,128]{1,0:T(8,128)S(1)} %collective-permute-done.30.refs_2_), channel_id=1, source_target_pairs={{0,8},{8,16},{16,24},{24,28},{28,20},{20,12},{12,4},{4,0},{1,9},{9... | collective-permute-start | bytes 835592 | tf_op jit(solution)/shard_map/ppermute | solution.py:531
  123.9 17.5 %collective-permute-start.37 = (f32[544,128]{1,0:T(8,128)S(1)}, f32[544,128]{1,0:T(8,128)S(1)}, u32[]{:S(2)}, u32[]{:S(2)}) collective-permute-start(f32[544,128]{1,0:T(8,128)S(1)} %collective-permute-done.31.refs_10_), channel_id=1, source_target_pairs={{8,0},{16,8},{24,16},{28,24},{20,28},{12,20},{4,12},{0,4},{9,1},{1... | collective-permute-start | bytes 835592 | tf_op jit(solution)/shard_map/ppermute | solution.py:531
  125.7 10.2 %collective-permute-start.32 = (f32[80,256]{1,0:T(8,128)S(1)}, f32[80,256]{1,0:T(8,128)S(1)}, u32[]{:S(2)}, u32[]{:S(2)}) collective-permute-start(f32[80,256]{1,0:T(8,128)S(1)} %add.266), channel_id=1, source_target_pairs={{0,16},{4,20},{8,24},{12,28},{16,0},{20,4},{24,8},{28,12},{1,17},{... | collective-permute-start | bytes 245768 | tf_op jit(solution)/shard_map/ppermute | solution.py:483
  150.5 12.4 %collective-permute-start.43 = (f32[544,128]{1,0:T(8,128)S(1)}, f32[544,128]{1,0:T(8,128)S(1)}, u32[]{:S(2)}, u32[]{:S(2)}) collective-permute-start(f32[544,128]{1,0:T(8,128)S(1)} %collective-permute-done.38.refs_4_), channel_id=1, source_target_pairs={{0,8},{8,16},{16,24},{24,28},{28,20},{20,12},{12,4},{4,0},{1,9},{9... | collective-permute-start | bytes 835592 | tf_op jit(solution)/shard_map/ppermute | solution.py:531
  150.6 12.4 %collective-permute-start.44 = (f32[544,128]{1,0:T(8,128)S(1)}, f32[544,128]{1,0:T(8,128)S(1)}, u32[]{:S(2)}, u32[]{:S(2)}) collective-permute-start(f32[544,128]{1,0:T(8,128)S(1)} %collective-permute-done.39.refs_12_), channel_id=1, source_target_pairs={{8,0},{16,8},{24,16},{28,24},{20,28},{12,20},{4,12},{0,4},{9,1},{1... | collective-permute-start | bytes 835592 | tf_op jit(solution)/shard_map/ppermute | solution.py:531
  163.0 10.2 %collective-permute-start.48 = (f32[544,128]{1,0:T(8,128)S(1)}, f32[544,128]{1,0:T(8,128)S(1)}, u32[]{:S(2)}, u32[]{:S(2)}) collective-permute-start(f32[544,128]{1,0:T(8,128)S(1)} %collective-permute-done.43.refs_5_), channel_id=1, source_target_pairs={{0,8},{8,16},{16,24},{24,28},{28,20},{20,12},{12,4},{4,0},{1,9},{9... | collective-permute-start | bytes 835592 | tf_op jit(solution)/shard_map/ppermute | solution.py:531
  163.1 10.1 %collective-permute-start.49 = (f32[544,128]{1,0:T(8,128)S(1)}, f32[544,128]{1,0:T(8,128)S(1)}, u32[]{:S(2)}, u32[]{:S(2)}) collective-permute-start(f32[544,128]{1,0:T(8,128)S(1)} %collective-permute-done.44.refs_13_), channel_id=1, source_target_pairs={{8,0},{16,8},{24,16},{28,24},{20,28},{12,20},{4,12},{0,4},{9,1},{1... | collective-permute-start | bytes 835592 | tf_op jit(solution)/shard_map/ppermute | solution.py:531
  173.2 10.0 %collective-permute-start.51 = (f32[544,128]{1,0:T(8,128)S(1)}, f32[544,128]{1,0:T(8,128)S(1)}, u32[]{:S(2)}, u32[]{:S(2)}) collective-permute-start(f32[544,128]{1,0:T(8,128)S(1)} %collective-permute-done.48.refs_6_), channel_id=1, source_target_pairs={{0,8},{8,16},{16,24},{24,28},{28,20},{20,12},{12,4},{4,0},{1,9},{9... | collective-permute-start | bytes 835592 | tf_op jit(solution)/shard_map/ppermute | solution.py:531
  (41 other events, 304.7 us)

commit v2 on v0

--- a/solution.py
+++ b/solution.py
@@ -39,6 +39,10 @@
         return lax.dot_general(x, y, (((ca,), (cb,)), ((), ())), preferred_element_type=F32)
 
     return one(a[0], b[0]) + (one(a[0], b[1]) + one(a[1], b[0]))
+
+
+def grant(mib):
+    return pltpu.CompilerParams(vmem_limit_bytes=mib << 20)
 
 
 def cost(flops, moved):
@@ -173,6 +177,7 @@
         out_specs=[VMEM] * len(shapes),
         scratch_shapes=[pltpu.VMEM((rows, rank), F32)],
         cost_estimate=cost(6e9, 1e6),
+        compiler_params=grant(12),
         name="orth_first",
     )(me, *parts)
 
@@ -188,6 +193,7 @@
         in_specs=[VMEM] * 2,
         out_specs=[VMEM] * 2,
         cost_estimate=cost(6e9, 1e6),
+        compiler_params=grant(12),
         name="orth_second",
     )(left, rest)
 
@@ -201,14 +207,18 @@
     dn_ref[...] = chunk_rows(mom_dn[...], grads_dn[...])
 
 
-def lead(at, momentum, grads, n):
+def lead(place, momentum, grads, n):
     _, rows, cols = momentum.shape
     w = cols // n // 2
     part = jax.ShapeDtypeStruct((2 * rows, w), F32)
     specs = []
-    for side in range(2):
-        specs.append(pl.BlockSpec((1, rows, w), lambda i, at, side=side: (0, 0, 2 * at[side] + side)))
-        specs.append(pl.BlockSpec((2, 1, rows, w), lambda i, at, side=side: (0, 0, 0, 2 * at[side] + side)))
+    for side, offset in enumerate((n - 1, 1)):
+
+        def half(i, at, side=side, offset=offset):
+            return 2 * lax.rem(at[0] + offset, n) + side
+
+        specs.append(pl.BlockSpec((1, rows, w), lambda i, at, half=half: (0, 0, half(i, at))))
+        specs.append(pl.BlockSpec((2, 1, rows, w), lambda i, at, half=half: (0, 0, 0, half(i, at))))
     return pl.pallas_call(
         lead_kernel,
         out_shape=[part, part],
@@ -219,22 +229,24 @@
             out_specs=[whole((2 * rows, w))] * 2,
         ),
         cost_estimate=cost(4 * rows * w, 32 * rows * w),
+        compiler_params=grant(58),
         name="lead",
-    )(at, momentum, grads, momentum, grads)
+    )(place, momentum, grads, momentum, grads)
 
 
 def combine_kernel(count, inv, me_ref, mom_ref, grads_ref, right_ref, up_ref, dn_ref, both_ref, *refs):
     parts, acc_ref = refs[:count], refs[count]
     k = pl.program_id(0)
     rows = mom_ref.shape[1]
+    chunks, _, w = up_ref.shape
     total = mom_ref[0] + grads_ref[0, 0].astype(F32)
     later = grads_ref[1, 0].astype(F32)
-    both_ref[...] = total + later
-    w = total.shape[1] // 2
-    up_ref[0, :rows] = total[:, :w]
-    dn_ref[0, :rows] = total[:, w:]
-    up_ref[0, rows:] = later[:, :w]
-    dn_ref[0, rows:] = later[:, w:]
+    both_ref[0] = total + later
+    for c in range(chunks):
+        for side, ref in enumerate((up_ref, dn_ref)):
+            at = (2 * c + side) * w
+            ref[c, :rows] = total[:, at : at + w]
+            ref[c, rows:] = later[:, at : at + w]
     part = dot(total, right_ref[...])
 
     @pl.when(k == 0)
@@ -257,13 +269,14 @@
 def combine(me, momentum, grads, right_factor, n, count):
     _, rows, cols = momentum.shape
     rank = right_factor.shape[1]
-    w = cols // n
-    chunks = jax.ShapeDtypeStruct((n, 2 * rows, w // 2), F32)
+    steps = n // 2
+    w = cols // steps
+    chunks = jax.ShapeDtypeStruct((n, 2 * rows, w // 4), F32)
     part = jax.ShapeDtypeStruct((rows // count, rank), F32)
     out = pl.pallas_call(
         functools.partial(combine_kernel, count, 1.0 / n),
-        out_shape=[chunks, chunks, jax.ShapeDtypeStruct((rows, cols), F32)] + [part] * count,
-        grid=(n,),
+        out_shape=[chunks, chunks, jax.ShapeDtypeStruct((1, rows, cols), F32)] + [part] * count,
+        grid=(steps,),
         in_specs=[
             SMEM,
             pl.BlockSpec((1, rows, w), lambda k: (0, 0, k)),
@@ -271,16 +284,64 @@
             pl.BlockSpec((w, rank), lambda k: (k, 0)),
         ],
         out_specs=[
-            pl.BlockSpec((1, 2 * rows, w // 2), lambda k: (k, 0, 0)),
-            pl.BlockSpec((1, 2 * rows, w // 2), lambda k: (k, 0, 0)),
-            pl.BlockSpec((rows, w), lambda k: (0, k)),
+            pl.BlockSpec((2, 2 * rows, w // 4), lambda k: (k, 0, 0)),
+            pl.BlockSpec((2, 2 * rows, w // 4), lambda k: (k, 0, 0)),
+            pl.BlockSpec((1, rows, w), lambda k: (0, 0, k)),
         ]
         + [pl.BlockSpec((rows // count, rank), lambda k: (0, 0))] * count,
         scratch_shapes=[pltpu.VMEM((rows, rank), F32)],
-        cost_estimate=cost(12 * rows * cols * rank, 16 * rows * cols),
+        cost_estimate=cost(12 * rows * cols * rank, 28 * rows * cols),
+        compiler_params=grant(20),
         name="combine",
     )(me, momentum, grads, right_factor)
     return out[0], out[1], out[2], out[3:]
+
+
+def ring_add_kernel(at_ref, up_ref, dn_ref, up_all, dn_all, up_out, dn_out):
+    up_out[...] = up_ref[...] + up_all[0]
+    dn_out[...] = dn_ref[...] + dn_all[0]
+
+
+def ring_add(place, step, up, dn, up_all, dn_all):
+    n = up_all.shape[0]
+    shape = jax.ShapeDtypeStruct(up.shape, F32)
+    return pl.pallas_call(
+        ring_add_kernel,
+        out_shape=[shape, shape],
+        grid_spec=pltpu.PrefetchScalarGridSpec(
+            num_scalar_prefetch=1,
+            grid=(1,),
+            in_specs=[
+                whole(up.shape),
+                whole(dn.shape),
+                pl.BlockSpec((1,) + up.shape, lambda i, at: (lax.rem(at[0] + n - 1 - step, n), 0, 0)),
+                pl.BlockSpec((1,) + dn.shape, lambda i, at: (lax.rem(at[0] + 1 + step, n), 0, 0)),
+            ],
+            out_specs=[whole(up.shape), whole(dn.shape)],
+        ),
+        cost_estimate=cost(2 * up.size, 24 * up.size),
+        compiler_params=grant(8),
+        name="ring_add",
+    )(place, up, dn, up_all, dn_all)
+
+
+def alike_kernel(*refs):
+    terms = [ref[...] for ref in refs[:-1]]
+    while len(terms) > 1:
+        terms = [a + b for a, b in zip(terms[::2], terms[1::2])]
+    refs[-1][...] = terms[0]
+
+
+def alike(terms):
+    return pl.pallas_call(
+        alike_kernel,
+        out_shape=jax.ShapeDtypeStruct(terms[0].shape, F32),
+        in_specs=[VMEM] * len(terms),
+        out_specs=VMEM,
+        cost_estimate=cost(len(terms) * terms[0].size, 4 * (len(terms) + 1) * terms[0].size),
+        compiler_params=grant(4),
+        name="alike",
+    )(*terms)
 
 
 def reduced_kernel(inv, at_ref, up_ref, dn_ref, up_all, dn_all, left_ref, leftt_ref, up_out, dn_out):
@@ -312,6 +373,7 @@
             out_specs=[whole(ring.shape)] * 2,
         ),
         cost_estimate=cost(24 * rows * rank * rank, 4e6),
+        compiler_params=grant(12),
         name="reduced",
     )(place, up, dn, up_all, dn_all, left, leftt)
 
@@ -340,44 +402,27 @@
         out_specs=[VMEM] * count,
         scratch_shapes=[pltpu.VMEM((rows, rank), F32)],
         cost_estimate=cost(12 * rows * rank * rank, 2e6),
+        compiler_params=grant(8),
         name="partial",
     )(me, up, dn)
 
 
-def squares_kernel(rank, up_ref, dn_ref, leftt_ref, out_ref):
-    averaged = jnp.concatenate([up_ref[rank:], dn_ref[rank:]], axis=1)
-    right = dot(leftt_ref[...], averaged)
-    out_ref[...] = dot(jnp.ones((8, right.shape[1]), F32), right * right, 1, 1)
-
-
-def squares_of(up, dn, leftt):
-    rank = leftt.shape[0]
-    return pl.pallas_call(
-        functools.partial(squares_kernel, rank),
-        out_shape=jax.ShapeDtypeStruct((8, rank), F32),
-        in_specs=[VMEM] * 3,
-        out_specs=VMEM,
-        cost_estimate=cost(12 * rank * rank * rank, 2e6),
-        name="squares",
-    )(up, dn, leftt)
-
-
-def fetcher(n, ups, dns, buf, sem):
+def fetcher(pieces, buf, sem):
     k = pl.program_id(0)
-    w = buf.shape[2] // 2
 
     def copies(i, slot):
-        return (
-            pltpu.make_async_copy(ups[i], buf.at[slot, :, pl.ds(0, w)], sem.at[slot, 0]),
-            pltpu.make_async_copy(dns[(n - i) % n], buf.at[slot, :, pl.ds(w, w)], sem.at[slot, 1]),
-        )
+        out = []
+        for j, (ref, row, col) in enumerate(pieces[i]):
+            at = buf.at[slot, pl.ds(row, ref.shape[0]), pl.ds(col, ref.shape[1])]
+            out.append(pltpu.make_async_copy(ref, at, sem.at[slot, j]))
+        return out
 
     @pl.when(k == 0)
     def _():
         for c in copies(0, 0):
             c.start()
 
-    for i in range(1, n):
+    for i in range(1, len(pieces)):
 
         @pl.when(k == i - 1)
         def _():
@@ -390,64 +435,135 @@
     return buf[slot]
 
 
-def finish_kernel(n, rate, order_ref, *refs):
-    ups, dns = refs[:n], refs[n : 2 * n]
-    both_ref, w_ref, l1_ref, l2_ref, l2t_ref, norm_ref, total_ref = refs[2 * n : 2 * n + 7]
-    mom_out, w_out, right_out, buf, sem, project, update = refs[2 * n + 7 :]
-    rows, rank = l1_ref.shape
-    norm = jnp.sqrt(total_ref[0:1] + EPS)
+def advance_kernel(m, order_ref, *refs):
+    ups, dns = refs[:m], refs[m : 2 * m]
+    both_ref, l1_ref, l2_ref, l2t_ref, mom_out, y_out, sq_out, buf, sem, project, update = refs[2 * m :]
+    k = pl.program_id(0)
+    rank = l2t_ref.shape[0]
+    w = buf.shape[2] // 2
+
+    @pl.when(k == 0)
+    def _():
+        project[0], project[1] = halves(l2t_ref[...])
+        update[0], update[1] = halves(DAMPING * jnp.concatenate([l1_ref[...], l2_ref[...]], axis=1))
+
+    chunk = fetcher([[(ups[i], 0, 0), (dns[i], 0, w)] for i in range(m)], buf, sem)
+    y1, averaged = chunk[:rank], chunk[rank:]
+    y2 = dot3((project[0], project[1]), halves(averaged))
+    y_out[0] = y2
+    y = halves(jnp.concatenate([y1, y2], axis=0))
+    mom_out[0] = both_ref[0] - dot3((update[0], update[1]), y)
+    squares = dot(jnp.ones((8, 2 * w), F32), y2 * y2, 1, 1)
+
+    @pl.when(k == 0)
+    def _():
+        sq_out[...] = squares
+
+    @pl.when(k > 0)
+    def _():
+        sq_out[...] += squares
+
+
+def chunk_at(steps, n):
+    def at(k, place):
+        step = steps[0]
+        for i in range(1, len(steps)):
+            step = jnp.where(k == i, steps[i], step)
+        return lax.rem(place[0] + n - step, n)
+
+    return at
+
+
+def advance(place, steps, n, ups, dns, both, l1, l2, l2t):
+    m = len(ups)
+    _, rows, _ = both.shape
+    rank = l1.shape[1]
+    w = 2 * ups[0].shape[1]
+    at = chunk_at(steps, n)
+    block = pl.BlockSpec((1, rows, w), lambda k, place: (0, 0, at(k, place)))
+    return pl.pallas_call(
+        functools.partial(advance_kernel, m),
+        out_shape=[
+            jax.ShapeDtypeStruct(both.shape, F32),
+            jax.ShapeDtypeStruct((m, rank, w), F32),
+            jax.ShapeDtypeStruct((8, rank), F32),
+        ],
+        grid_spec=pltpu.PrefetchScalarGridSpec(
+            num_scalar_prefetch=1,
+            grid=(m,),
+            in_specs=[VMEM] * (2 * m) + [block, whole((rows, rank)), whole((rows, rank)), whole((rank, rows))],
+            out_specs=[block, pl.BlockSpec((1, rank, w), lambda k, order: (k, 0, 0)), whole((8, rank))],
+            scratch_shapes=[
+                pltpu.VMEM((2, rank + rows, w), F32),
+                pltpu.SemaphoreType.DMA((2, 2)),
+                pltpu.VMEM((2, rank, rows), BF16),
+                pltpu.VMEM((2, rows, 2 * rank), BF16),
+            ],
+        ),
+        input_output_aliases={1 + 2 * m: 0},
+        cost_estimate=cost(m * w * 30 * rows * rank, m * w * rows * 24),
+        compiler_params=grant(14),
+        name="advance",
+    )(place, *ups, *dns, both, l1, l2, l2t)
+
+
+def weights_kernel(n, groups, rate, order_ref, *refs):
+    ups, dns, ys = refs[:n], refs[n : 2 * n], refs[2 * n : 2 * n + len(groups)]
+    w_ref, l1_ref, l2_ref, norm_ref, *totals, w_out, right_out, buf, sem, update = refs[2 * n + len(groups) :]
+    rank = right_out.shape[1]
+    w = buf.shape[2] // 2
+    total = totals[0][0:1]
+    for ref in totals[1:]:
+        total = total + ref[0:1]
+    norm = jnp.sqrt(total + EPS)
 
     @pl.when(pl.program_id(0) == 0)
     def _():
-        project[0], project[1] = halves(l2t_ref[...])
-        l1, l2 = l1_ref[...], l2_ref[...]
-        moment = DAMPING * jnp.concatenate([l1, l2], axis=1)
-        weight = rate * jnp.concatenate([l1 / norm_ref[...], l2 / norm], axis=1)
-        update[0], update[1] = halves(jnp.concatenate([moment, weight], axis=0))
-
-    chunk = fetcher(n, ups, dns, buf, sem)
-    y1, averaged = chunk[:rank], chunk[rank:]
-    y2 = dot3((project[0], project[1]), halves(averaged))
-    change = dot3((update[0], update[1]), halves(jnp.concatenate([y1, y2], axis=0)))
-    mom_out[0] = both_ref[...] - change[:rows]
-    w_out[...] = w_ref[...] - change[rows:]
-    right_out[...] = y2.T / norm
-
-
-def finish(order, rings, both, weights, l1, l2, l2t, norm, totals, rate):
-    n = len(rings) // 2
-    rows, cols = both.shape
+        left = jnp.concatenate([l1_ref[...] / norm_ref[...], l2_ref[...] / norm], axis=1)
+        update[0], update[1] = halves(rate * left)
+
+    pieces = []
+    for y_ref, group in zip(ys, groups):
+        for j in range(group):
+            i = len(pieces)
+            rows = pl.ds(0, rank)
+            pieces.append([(ups[i].at[rows, :], 0, 0), (dns[i].at[rows, :], 0, w), (y_ref.at[j], rank, 0)])
+    y = fetcher(pieces, buf, sem)
+    w_out[...] = w_ref[...] - dot3((update[0], update[1]), halves(y))
+    right_out[...] = y[rank:].T / norm
+
+
+def finish(place, steps, ups, dns, ys, weights, l1, l2, norm, totals, rate):
+    n = len(ups)
+    rows, cols = weights.shape
     rank = l1.shape[1]
     w = cols // n
-    block = pl.BlockSpec((rows, w), lambda k, order: (0, order[k]))
-    return pl.pallas_call(
-        functools.partial(finish_kernel, n, rate),
+    groups = tuple(y.shape[0] for y in ys)
+    at = chunk_at(steps, n)
+    block = pl.BlockSpec((rows, w), lambda k, place: (0, at(k, place)))
+    return pl.pallas_call(
+        functools.partial(weights_kernel, n, groups, rate),
         out_shape=[
-            jax.ShapeDtypeStruct((1, rows, cols), F32),
             jax.ShapeDtypeStruct((rows, cols), F32),
             jax.ShapeDtypeStruct((cols, rank), F32),
         ],
         grid_spec=pltpu.PrefetchScalarGridSpec(
             num_scalar_prefetch=1,
             grid=(n,),
-            in_specs=[pl.BlockSpec(memory_space=pl.ANY)] * len(rings)
-            + [block, block, whole((rows, rank)), whole((rows, rank)), whole((rank, rows))]
-            + [whole((1, rank)), whole((8, rank))],
-            out_specs=[
-                pl.BlockSpec((1, rows, w), lambda k, order: (0, 0, order[k])),
-                block,
-                pl.BlockSpec((w, rank), lambda k, order: (order[k], 0)),
-            ],
+            in_specs=[VMEM] * (2 * n + len(ys))
+            + [block, whole((rows, rank)), whole((rows, rank)), whole((1, rank))]
+            + [whole((8, rank))] * len(totals),
+            out_specs=[block, pl.BlockSpec((w, rank), lambda k, place: (at(k, place), 0))],
             scratch_shapes=[
-                pltpu.VMEM((2, rank + rows, w), F32),
-                pltpu.SemaphoreType.DMA((2, 2)),
-                pltpu.VMEM((2, rank, rows), BF16),
-                pltpu.VMEM((2, 2 * rows, 2 * rank), BF16),
+                pltpu.VMEM((2, 2 * rank, w), F32),
+                pltpu.SemaphoreType.DMA((2, 3)),
+                pltpu.VMEM((2, rows, 2 * rank), BF16),
             ],
         ),
-        cost_estimate=cost(30 * rows * cols * rank, 32 * rows * cols),
+        cost_estimate=cost(12 * rows * cols * rank, 32 * rows * cols),
+        compiler_params=grant(28),
         name="finish",
-    )(order, *rings, both, weights, l1, l2, l2t, norm, totals)
+    )(place, *ups, *dns, *ys, weights, l1, l2, norm, *totals)
 
 
 def whole(shape):
@@ -464,15 +580,12 @@
 
     def scatter():
         got = [flip(box["parts"][d], "col", d) for d in range(1, cols)]
-        x = box["parts"][0]
-        for other in got:
-            x = x + other
-        box["x"] = x
+        box["x"] = alike([box["parts"][0]] + got)
 
     def exchange(bit):
         def stage():
             got = flip(box["x"], "rep", 1 << bit)
-            box["x"] = box["x"] + got
+            box["x"] = alike([box["x"], got])
 
         return stage
 
@@ -488,14 +601,10 @@
     rank = right_factor.shape[1]
     ring = list(range(0, n, 2)) + list(range(n - 1, 0, -2))
     rep = lax.axis_index("rep")
-    place = jnp.where(rep % 2 == 0, rep // 2, n - 1 - rep // 2).astype(jnp.int32)
+    place = jnp.where(rep % 2 == 0, rep // 2, n - 1 - rep // 2).astype(jnp.int32)[None]
     ahead = [(ring[i], ring[(i + 1) % n]) for i in range(n)]
     back = [(b, a) for a, b in ahead]
     me = lax.axis_index("col").astype(jnp.int32)[None]
-    order = lax.rem(place - jnp.arange(n, dtype=jnp.int32) + n, n)
-
-    def chunk(x, k):
-        return lax.dynamic_index_in_dim(x, lax.rem(place + k + 2 * n, n), 0, keepdims=False)
 
     def tie(box, *arrays):
         keys = list(box)
@@ -506,29 +615,30 @@
     def step(up, dn):
         return lax.ppermute(up, "rep", ahead), lax.ppermute(dn, "rep", back)
 
-    def windows(box, scaled):
-        stages = all_sum_stages(box)
-
-        def first():
+    def first(scaled):
+        def stage():
             out = orth_first(me, box.pop("parts"), rows, scaled)
             box.pop("x")
             box["left"], box["rest"] = out[:2]
             if scaled:
                 box["norm"] = out[2]
 
-        def second():
-            box["left"], box["leftt"] = orth_second(box.pop("left"), box.pop("rest"))
-
-        return [stages[:2]] + [[s] for s in stages[2:-2]] + [stages[-2:], [first], [second]]
+        return stage
 
     box = {}
-
-    def prepare():
-        up_all, dn_all, both, parts = combine(me, momentum, grads, right_factor, n, count)
-        box.update(up_all=up_all, dn_all=dn_all, both=both, parts=list(parts))
-
-    work = [[prepare]] + windows(box, False)
-    up, dn = lead(lax.rem(jnp.stack([place + n - 1, place + 1]), n), momentum, grads, n)
+    scatter, *bits, gather = all_sum_stages(box)
+
+    def begin():
+        out = combine(me, momentum, grads, right_factor, n, count)
+        box["up_all"], box["dn_all"], box["both"] = out[:3]
+        box["parts"] = list(out[3])
+
+    def second():
+        box["left"], box["leftt"] = orth_second(box.pop("left"), box.pop("rest"))
+
+    work = [[begin, scatter]] + [[bit] for bit in bits] + [[first(False)], [second]]
+    work[len(bits)].append(gather)
+    up, dn = lead(place, momentum, grads, n)
     for k in range(1, n):
         up, dn = step(up, dn)
         if work:
@@ -536,53 +646,58 @@
                 stage()
             up, dn = tie(box, up, dn)
         if k < n - 1:
-            up, dn = up + chunk(box["up_all"], -1 - k), dn + chunk(box["dn_all"], 1 + k)
-    for stage in sum(work, []):
-        stage()
+            up, dn = ring_add(place, k, up, dn, box["up_all"], box["dn_all"])
     l1 = box["left"]
     both = box["both"]
-    up, dn = reduced(place[None], up, dn, box["up_all"], box["dn_all"], l1, box["leftt"], n)
+    up, dn = reduced(place, up, dn, box["up_all"], box["dn_all"], l1, box["leftt"], n)
 
     box = {}
     mine = (up, dn)
-
-    def begin():
+    scatter, *bits, gather = all_sum_stages(box)
+
+    def begin_again():
         box["parts"] = list(partial_raw(me, *mine, rank, count))
 
-    def total_columns():
-        x = squares_of(*mine, box["leftt"])
-        got = [flip(x, "col", d) for d in range(1, count)]
-        terms = [x] + got
-        while len(terms) > 1:
-            terms = [a + b for a, b in zip(terms[::2], terms[1::2])]
-        box["total"] = terms[0]
-
-    def total_bit(bit):
-        def stage():
-            got = flip(box["total"], "rep", 1 << bit)
-            box["total"] = box["total"] + got
-
-        return stage
-
-    work = windows(box, True)
-    work[0].insert(0, begin)
-    bits = [total_bit(b) for b in range(n.bit_length() - 1)]
-    work += [[total_columns, bits[0]], bits[1:]]
     ups, dns = [up], [dn]
+    ready, ys, totals = [], [], []
+
+    def advance_ready():
+        new = [c for c in range(n) if c not in ready and c < len(ups) and (n - c) % n < len(dns)]
+        ready.extend(new)
+        sides = ([ups[c] for c in new], [dns[(n - c) % n] for c in new])
+        box["both"], y, squares = advance(place, new, n, *sides, box["both"], l1, box["left"], box["leftt"])
+        ys.append(y)
+        totals.append(squares)
+
+    work = [[begin_again, scatter, bits[0]]] + [[bit] for bit in bits[1:]]
+    work[-1].append(gather)
+    work += [[first(True)], [second]]
     for _ in range(1, n):
         up, dn = step(up, dn)
         if work:
             for stage in work.pop(0):
                 stage()
             up, dn = tie(box, up, dn)
+        else:
+            box.setdefault("both", both)
+            advance_ready()
+            up, dn = tie(box, up, dn)
         ups.append(up)
         dns.append(dn)
-    for stage in sum(work, []):
-        stage()
-    new_momentum, new_weights, new_right = finish(
-        order, ups + dns, both, weights, l1, box["left"], box["leftt"], box["norm"], box["total"], rate
-    )
-    return new_weights, new_momentum, new_right
+    box.setdefault("both", both)
+    advance_ready()
+    total = alike_total(totals, count)
+    sides = ([ups[c] for c in ready], [dns[(n - c) % n] for c in ready])
+    new_weights, new_right = finish(place, ready, *sides, ys, weights, l1, box["left"], box["norm"], [total], rate)
+    return new_weights, box["both"], new_right
+
+
+def alike_total(totals, count):
+    total = totals[0]
+    for other in totals[1:]:
+        total = alike([total, other])
+    got = [flip(total, "col", d) for d in range(1, count)]
+    return alike([total] + got)
 
 
 def plain_orthonormal(left_raw):

time: 212 us -> 178 us (0.84)
  other arithmetic: 16.1 us -> 0 us
  Pallas kernels: 66.9 us -> 52.7 us
    add x24 -> x0, other arithmetic: 15 us -> none  [the longest x6 5.96 us: ring_shards(): dn + chunk(box['dn_all'], 1 + k)]
    pallas_call x1, Pallas kernels: 9.48 us -> 4.63 us  [combine(): pl.pallas_call(functools.partial(combine_kernel, count, 1.0 / n), out_sha...]
    ppermute x24 -> x21, waiting for transfers between devices: 64.2 us -> 59.4 us  [flip(): return lax.ppermute(x, axis, [(i, i ^ bits) for i in range(size)])]
    pallas_call x2, Pallas kernels: 14.5 us -> 11 us  [orth_second(): pl.pallas_call(second_kernel, out_shape=[jax.ShapeDtypeStruct((rows, rank...]
    pallas_call x2, Pallas kernels: 15.8 us -> 12.5 us  [orth_first(): pl.pallas_call(functools.partial(first_kernel, scaled), out_shape=shapes,...]
    ppermute x28, waiting for transfers between devices: 7.65 us -> 10.7 us  [step(): return (lax.ppermute(up, 'rep', ahead), lax.ppermute(dn, 'rep', back))]
    ppermute x28, starting transfers between devices: 32.4 us -> 29.9 us  [step(): return (lax.ppermute(up, 'rep', ahead), lax.ppermute(dn, 'rep', back))]
    pallas_call x1, Pallas kernels: 3.65 us -> 1.39 us  [reduced(): pl.pallas_call(functools.partial(reduced_kernel, 1.0 / n), out_shape=[rin...]
  transfers between devices with their start and end apart: 52 -> 49, of which waited for: 22 -> 28; matrix products, arithmetic and copies ran while one was open for 5% -> 0% of each run, Pallas kernels for 20% -> 22%
where the time goes in v2:
time: 178 us
  waiting for transfers between devices  70.1 us (39%)
  Pallas kernels  52.7 us (30%)
  starting transfers between devices  50.5 us (28%)
  local copies, waits for them, and re-layouts  3.27 us (2%)
    ppermute x21, waiting for transfers between devices, flip(): return lax.ppermute(x, axis, [(i, i ^ bits) for i in range(size)])  59.4 us
    ppermute x28, starting transfers between devices, step(): return (lax.ppermute(up, 'rep', ahead), lax.ppermute(dn, 'rep', back))  29.9 us
    ppermute x21, starting transfers between devices, flip(): return lax.ppermute(x, axis, [(i, i ^ bits) for i in range(size)])  20.6 us
    pallas_call x3, Pallas kernels, advance(): pl.pallas_call(functools.partial(advance_kernel, m), out_shape=[jax.Shape...  14 us
    pallas_call x2, Pallas kernels, orth_first(): pl.pallas_call(functools.partial(first_kernel, scaled), out_shape=shapes,...  12.5 us
    pallas_call x2, Pallas kernels, orth_second(): pl.pallas_call(second_kernel, out_shape=[jax.ShapeDtypeStruct((rows, rank...  11 us
    ppermute x28, waiting for transfers between devices, step(): return (lax.ppermute(up, 'rep', ahead), lax.ppermute(dn, 'rep', back))  10.7 us
    pallas_call x1, Pallas kernels, finish(): pl.pallas_call(functools.partial(weights_kernel, n, groups, rate), out_sh...  5.85 us
  transfers between devices with their start and end apart: 49, of which 28 were waited for; matrix products, arithmetic and copies ran while one was open for 0% of the time, Pallas kernels for 22%

profile of v2, /device:TPU:0, one launch (start us, length us, event | category | flops | bytes accessed | tf_op | source)
XLA Modules:
  0.0 177.8 jit_solution(16502726351042320106)
XLA Ops:
  0.7 2.1 %lead.1 = (f32[576,128]{1,0:T(8,128)}, f32[576,128]{1,0:T(8,128)}) custom-call(s32[1]{0:T(128)} %bitcast.at_ref.order_ref, f32[1,288,2048]{2,1,0:T(8,128)} %mom_dn.1, bf16[2,1,288,2048]{3,2,1,0:T(8,128)(2,1)} %grads_dn.1, f32[1,288,2048]{2,1,0:T(8,128)} %mom_dn.1, bf16[2,1,288,2048]{3,2,1,0:T(8,128)(2,1)} %grads_dn.1), custom_call_target="tpu_custom_call" | custom-call | flops 147456 | bytes 1179648 | tf_op jit(solution)/shard_map/lead/pallas_call | solution.py:222
  2.8 3.1 %collective-permute-start.3 = (f32[576,128]{1,0:T(8,128)}, f32[576,128]{1,0:T(8,128)S(1)}, u32[]{:S(2)}, u32[]{:S(2)}) collective-permute-start(f32[576,128]{1,0:T(8,128)} %get-tuple-element.132), channel_id=1, source_target_pairs={{0,8},{8,16},{16,24},{24,28},{28,20},{20,12},{12,4},{4,0},{1,9},{9... | collective-permute-start | bytes 884744 | tf_op jit(solution)/shard_map/ppermute | solution.py:616
  9.1 4.6 %combine.1 = (f32[8,576,128]{2,1,0:T(8,128)S(1)}, f32[8,576,128]{2,1,0:T(8,128)S(1)}, f32[1,288,2048]{2,1,0:T(8,128)}, f32[72,256]{1,0:T(8,128)S(1)}, f32[72,256...) custom-call(s32[1]{0:T(128)} %bitcast.1.me_ref, f32[1,288,2048]{2,1,0:T(8,128)S(1)} %copy-done, ...), custom_call_target="tpu_custom_call" | custom-call | flops 1811939328 | bytes 16515072 | tf_op jit(solution)/shard_map/combine/pallas_call | solution.py:276
  15.8 2.8 %collective-permute-done.1.refs_2_ = f32[72,256]{1,0:T(8,128)S(1)} collective-permute-done((f32[72,256]{1,0:T(8,128)S(1)}, f32[72,256]{1,0:T(8,128)S(1)}, u32[]{:S(2)}, u32[]{:S(2)}) %collective-permute-start.1) | collective-permute-done | bytes 73760 | tf_op jit(solution)/shard_map/ppermute | solution.py:575
  20.0 2.0 %collective-permute-start.6 = (f32[576,128]{1,0:T(8,128)S(1)}, f32[576,128]{1,0:T(8,128)S(1)}, u32[]{:S(2)}, u32[]{:S(2)}) collective-permute-start(f32[576,128]{1,0:T(8,128)S(1)} %get-tuple-element.140), channel_id=1, source_target_pairs={{0,8},{8,16},{16,24},{24,28},{28,20},{20,12},{12,4},{4,0},{1,9},{9... | collective-permute-start | bytes 884744 | tf_op jit(solution)/shard_map/ppermute | solution.py:616
  24.0 6.8 %collective-permute-done.5.refs_1_ = f32[72,256]{1,0:T(8,128)S(1)} collective-permute-done((f32[72,256]{1,0:T(8,128)S(1)}, f32[72,256]{1,0:T(8,128)S(1)}, u32[]{:S(2)}, u32[]{:S(2)}) %collective-permute-start.5) | collective-permute-done | bytes 73760 | tf_op jit(solution)/shard_map/ppermute | solution.py:575
  34.5 7.2 %collective-permute-done.8.refs_1_ = f32[72,256]{1,0:T(8,128)S(1)} collective-permute-done((f32[72,256]{1,0:T(8,128)S(1)}, f32[72,256]{1,0:T(8,128)S(1)}, u32[]{:S(2)}, u32[]{:S(2)}) %collective-permute-start.8) | collective-permute-done | bytes 73760 | tf_op jit(solution)/shard_map/ppermute | solution.py:575
  43.8 4.2 %collective-permute-start.11 = (f32[72,256]{1,0:T(8,128)S(1)}, f32[72,256]{1,0:T(8,128)S(1)}, u32[]{:S(2)}, u32[]{:S(2)}) collective-permute-start(f32[72,256]{1,0:T(8,128)S(1)} %alike.13.refs_0_), channel_id=1, source_target_pairs={{0,16},{4,20},{8,24},{12,28},{16,0},{20,4},{24,8},{28,12},{1,17},{... | collective-permute-start | bytes 221192 | tf_op jit(solution)/shard_map/ppermute | solution.py:575
  48.0 7.6 %collective-permute-done.11.refs_1_ = f32[72,256]{1,0:T(8,128)S(1)} collective-permute-done((f32[72,256]{1,0:T(8,128)S(1)}, f32[72,256]{1,0:T(8,128)S(1)}, u32[]{:S(2)}, u32[]{:S(2)}) %collective-permute-start.11) | collective-permute-done | bytes 73760 | tf_op jit(solution)/shard_map/ppermute | solution.py:575
  57.5 2.4 %collective-permute-done.14.refs_3_ = f32[72,256]{1,0:T(8,128)S(1)} collective-permute-done((f32[72,256]{1,0:T(8,128)S(1)}, f32[72,256]{1,0:T(8,128)S(1)}, u32[]{:S(2)}, u32[]{:S(2)}) %collective-permute-start.14) | collective-permute-done | bytes 73760 | tf_op jit(solution)/shard_map/ppermute | solution.py:575
  64.0 6.2 %orth_first.2 = (f32[288,128]{1,0:T(8,128)S(1)}, f32[288,128]{1,0:T(8,128)S(1)}) custom-call(s32[1]{0:T(128)} %bitcast.1.me_ref, f32[72,256]{1,0:T(8,128)S(1)} %alike.14.refs_0_, f32[72,256]{1,0:T(8,128)S(1)} %collective-permute-done.12.refs_1_, f32[72,256]{1,0:T(8,128)S(1)} %collective-permute-done.13.refs_2_, f32[72,256]{1,0:T(8,128)S(1)} %collective-permute-done.14.refs_3_), custom_call_target="tpu_custom_call" | custom-call | flops 6000000000 | bytes 1000000 | tf_op jit(solution)/shard_map/orth_first/pallas_call | solution.py:173
  73.1 5.5 %orth_second.2 = (f32[288,256]{1,0:T(8,128)S(1)}, f32[256,288]{1,0:T(8,128)S(1)}) custom-call(f32[288,128]{1,0:T(8,128)S(1)} %get-tuple-element.174.left_ref, f32[288,128]{1,0:T(8,128)S(1)} %get-tuple-element.175.rest_ref), custom_call_target="tpu_custom_call" | custom-call | flops 6000000000 | bytes 1000000 | tf_op jit(solution)/shard_map/orth_second/pallas_call | solution.py:187
  81.5 5.2 %collective-permute-done.21.up_ref = f32[576,128]{1,0:T(8,128)S(1)} collective-permute-done((f32[576,128]{1,0:T(8,128)S(1)}, f32[576,128]{1,0:T(8,128)S(1)}, u32[]{:S(2)}, u32[]{:S(2)}) %collective-permute-start.21) | collective-permute-done | bytes 294944 | tf_op jit(solution)/shard_map/ppermute | solution.py:616
  93.4 3.5 %collective-permute-done.24.refs_2_ = f32[80,256]{1,0:T(8,128)S(1)} collective-permute-done((f32[80,256]{1,0:T(8,128)S(1)}, f32[80,256]{1,0:T(8,128)S(1)}, u32[]{:S(2)}, u32[]{:S(2)}) %collective-permute-start.24) | collective-permute-done | bytes 81952 | tf_op jit(solution)/shard_map/ppermute | solution.py:575
  98.8 3.6 %collective-permute-done.26.refs_1_ = f32[80,256]{1,0:T(8,128)S(1)} collective-permute-done((f32[80,256]{1,0:T(8,128)S(1)}, f32[80,256]{1,0:T(8,128)S(1)}, u32[]{:S(2)}, u32[]{:S(2)}) %collective-permute-start.26) | collective-permute-done | bytes 81952 | tf_op jit(solution)/shard_map/ppermute | solution.py:575
  105.2 7.5 %collective-permute-done.29.refs_1_ = f32[80,256]{1,0:T(8,128)S(1)} collective-permute-done((f32[80,256]{1,0:T(8,128)S(1)}, f32[80,256]{1,0:T(8,128)S(1)}, u32[]{:S(2)}, u32[]{:S(2)}) %collective-permute-start.29) | collective-permute-done | bytes 81952 | tf_op jit(solution)/shard_map/ppermute | solution.py:575
  116.4 8.1 %collective-permute-done.32.refs_1_ = f32[80,256]{1,0:T(8,128)S(1)} collective-permute-done((f32[80,256]{1,0:T(8,128)S(1)}, f32[80,256]{1,0:T(8,128)S(1)}, u32[]{:S(2)}, u32[]{:S(2)}) %collective-permute-start.32) | collective-permute-done | bytes 81952 | tf_op jit(solution)/shard_map/ppermute | solution.py:575
  126.5 2.9 %collective-permute-done.35.refs_3_ = f32[80,256]{1,0:T(8,128)S(1)} collective-permute-done((f32[80,256]{1,0:T(8,128)S(1)}, f32[80,256]{1,0:T(8,128)S(1)}, u32[]{:S(2)}, u32[]{:S(2)}) %collective-permute-start.35) | collective-permute-done | bytes 81952 | tf_op jit(solution)/shard_map/ppermute | solution.py:575
  132.6 6.3 %orth_first.3 = (f32[288,128]{1,0:T(8,128)S(1)}, f32[288,128]{1,0:T(8,128)S(1)}, f32[1,256]{1,0:T(1,128)S(1)}) custom-call(s32[1]{0:T(128)} %bitcast.1.me_ref, f32[80,256]{1,0:T(8,128)S(1)} %alike.18.refs_0_, f32[80,256]{1,0:T(8,128)S(1)} %collective-permute-done.33.refs_1_, f32[80,256]{1,0:T(8,128)S(1)} %collective-permute-done.34.refs_2_, ...), custom_call_target="tpu_custom_call" | custom-call | flops 6000000000 | bytes 1000000 | tf_op jit(solution)/shard_map/orth_first/pallas_call | solution.py:173
  141.6 5.5 %orth_second.3 = (f32[288,256]{1,0:T(8,128)S(1)}, f32[256,288]{1,0:T(8,128)S(1)}) custom-call(f32[288,128]{1,0:T(8,128)S(1)} %get-tuple-element.213.left_ref, f32[288,128]{1,0:T(8,128)S(1)} %get-tuple-element.214.rest_ref), custom_call_target="tpu_custom_call" | custom-call | flops 6000000000 | bytes 1000000 | tf_op jit(solution)/shard_map/orth_second/pallas_call | solution.py:187
  149.4 6.1 %advance.3 = (f32[1,288,2048]{2,1,0:T(8,128)}, f32[4,256,256]{2,1,0:T(8,128)S(1)}, f32[8,256]{1,0:T(8,128)S(1)}) custom-call(s32[1]{0:T(128)} %bitcast.at_ref.order_ref, f32[544,128]{1,0:T(8,128)S(1)} %get-tuple-element.190.up_ref.refs_0_, f32[544,128]{1,0:T(8,128)S(1)} %collective-permute-done.36.refs_1_, ...), custom_call_target="tpu_custom_call", output_to_operand_aliasing={{0}: (9, {})} | custom-call | flops 2264924160 | bytes 7077888 | tf_op jit(solution)/shard_map/advance/pallas_call | solution.py:484
  157.7 4.0 %advance.4 = (f32[1,288,2048]{2,1,0:T(8,128)}, f32[2,256,256]{2,1,0:T(8,128)S(1)}, f32[8,256]{1,0:T(8,128)S(1)}) custom-call(s32[1]{0:T(128)} %bitcast.at_ref.order_ref, f32[544,128]{1,0:T(8,128)S(1)} %collective-permute-done.30.refs_0_.refs_4_, f32[544,128]{1,0:T(8,128)S(1)} %collective-permute-done.42.refs_1_.refs_5_, ...), custom_call_target="tpu_custom_call", output_to_operand_aliasing={{0}: (5, {})} | custom-call | flops 1132462080 | bytes 3538944 | tf_op jit(solution)/shard_map/advance/pallas_call | solution.py:484
  163.9 4.0 %advance.5 = (f32[1,288,2048]{2,1,0:T(8,128)}, f32[2,256,256]{2,1,0:T(8,128)S(1)}, f32[8,256]{1,0:T(8,128)S(1)}) custom-call(s32[1]{0:T(128)} %bitcast.at_ref.order_ref, f32[544,128]{1,0:T(8,128)S(1)} %collective-permute-done.27.refs_0_.refs_6_, f32[544,128]{1,0:T(8,128)S(1)} %collective-permute-done.44.refs_1_.refs_7_, ...), custom_call_target="tpu_custom_call", output_to_operand_aliasing={{0}: (5, {})} | custom-call | flops 1132462080 | bytes 3538944 | tf_op jit(solution)/shard_map/advance/pallas_call | solution.py:484
  171.7 5.8 %finish.1 = (f32[288,2048]{1,0:T(8,128)}, f32[2048,256]{1,0:T(8,128)}) custom-call(s32[1]{0:T(128)} %bitcast.at_ref.order_ref, f32[544,128]{1,0:T(8,128)S(1)} %get-tuple-element.190.up_ref.refs_0_, f32[544,128]{1,0:T(8,128)S(1)} %collective-permute-done.36.refs_1_, f32[544,128]{1,0:T(8,128)S(1)} %collective-permute-done.38.refs_2_, ...), custom_call_target="tpu_custom_call" | custom-call | flops 1811939328 | bytes 18874368 | tf_op jit(solution)/shard_map/finish/pallas_call | solution.py:544
  (111 shorter events, 59.5 us)
Async XLA Ops:
  2.8 17.1 %collective-permute-start.3 = (f32[576,128]{1,0:T(8,128)}, f32[576,128]{1,0:T(8,128)S(1)}, u32[]{:S(2)}, u32[]{:S(2)}) collective-permute-start(f32[576,128]{1,0:T(8,128)} %get-tuple-element.132), channel_id=1, source_target_pairs={{0,8},{8,16},{16,24},{24,28},{28,20},{20,12},{12,4},{4,0},{1,9},{9... | collective-permute-start | bytes 884744 | tf_op jit(solution)/shard_map/ppermute | solution.py:616
  5.8 14.0 %collective-permute-start.4 = (f32[576,128]{1,0:T(8,128)}, f32[576,128]{1,0:T(8,128)S(1)}, u32[]{:S(2)}, u32[]{:S(2)}) collective-permute-start(f32[576,128]{1,0:T(8,128)} %get-tuple-element.133), channel_id=1, source_target_pairs={{8,0},{16,8},{24,16},{28,24},{20,28},{12,20},{4,12},{0,4},{9,1},{1... | collective-permute-start | bytes 884744 | tf_op jit(solution)/shard_map/ppermute | solution.py:616
  20.0 10.9 %collective-permute-start.6 = (f32[576,128]{1,0:T(8,128)S(1)}, f32[576,128]{1,0:T(8,128)S(1)}, u32[]{:S(2)}, u32[]{:S(2)}) collective-permute-start(f32[576,128]{1,0:T(8,128)S(1)} %get-tuple-element.140), channel_id=1, source_target_pairs={{0,8},{8,16},{16,24},{24,28},{28,20},{20,12},{12,4},{4,0},{1,9},{9... | collective-permute-start | bytes 884744 | tf_op jit(solution)/shard_map/ppermute | solution.py:616
  22.0 8.8 %collective-permute-start.7 = (f32[576,128]{1,0:T(8,128)S(1)}, f32[576,128]{1,0:T(8,128)S(1)}, u32[]{:S(2)}, u32[]{:S(2)}) collective-permute-start(f32[576,128]{1,0:T(8,128)S(1)} %get-tuple-element.141), channel_id=1, source_target_pairs={{8,0},{16,8},{24,16},{28,24},{20,28},{12,20},{4,12},{0,4},{9,1},{1... | collective-permute-start | bytes 884744 | tf_op jit(solution)/shard_map/ppermute | solution.py:616
  22.0 8.8 %collective-permute-start.5 = (f32[72,256]{1,0:T(8,128)S(1)}, f32[72,256]{1,0:T(8,128)S(1)}, u32[]{:S(2)}, u32[]{:S(2)}) collective-permute-start(f32[72,256]{1,0:T(8,128)S(1)} %alike.11.refs_0_), channel_id=1, source_target_pairs={{0,4},{4,0},{8,12},{12,8},{16,20},{20,16},{24,28},{28,24},{1,5},{5... | collective-permute-start | bytes 221192 | tf_op jit(solution)/shard_map/ppermute | solution.py:575
  30.9 10.7 %collective-permute-start.9 = (f32[576,128]{1,0:T(8,128)S(1)}, f32[576,128]{1,0:T(8,128)S(1)}, u32[]{:S(2)}, u32[]{:S(2)}) collective-permute-start(f32[576,128]{1,0:T(8,128)S(1)} %get-tuple-element.148), channel_id=1, source_target_pairs={{0,8},{8,16},{16,24},{24,28},{28,20},{20,12},{12,4},{4,0},{1,9},{9... | collective-permute-start | bytes 884744 | tf_op jit(solution)/shard_map/ppermute | solution.py:616
  32.4 9.2 %collective-permute-start.10 = (f32[576,128]{1,0:T(8,128)S(1)}, f32[576,128]{1,0:T(8,128)S(1)}, u32[]{:S(2)}, u32[]{:S(2)}) collective-permute-start(f32[576,128]{1,0:T(8,128)S(1)} %get-tuple-element.149), channel_id=1, source_target_pairs={{8,0},{16,8},{24,16},{28,24},{20,28},{12,20},{4,12},{0,4},{9,1},{1... | collective-permute-start | bytes 884744 | tf_op jit(solution)/shard_map/ppermute | solution.py:616
  33.0 8.6 %collective-permute-start.8 = (f32[72,256]{1,0:T(8,128)S(1)}, f32[72,256]{1,0:T(8,128)S(1)}, u32[]{:S(2)}, u32[]{:S(2)}) collective-permute-start(f32[72,256]{1,0:T(8,128)S(1)} %alike.12.refs_0_), channel_id=1, source_target_pairs={{0,8},{4,12},{8,0},{12,4},{16,24},{20,28},{24,16},{28,20},{1,9},{5... | collective-permute-start | bytes 221192 | tf_op jit(solution)/shard_map/ppermute | solution.py:575
  41.7 20.1 %collective-permute-start.15 = (f32[576,128]{1,0:T(8,128)S(1)}, f32[576,128]{1,0:T(8,128)S(1)}, u32[]{:S(2)}, u32[]{:S(2)}) collective-permute-start(f32[576,128]{1,0:T(8,128)S(1)} %get-tuple-element.156), channel_id=1, source_target_pairs={{0,8},{8,16},{16,24},{24,28},{28,20},{20,12},{12,4},{4,0},{1,9},{9... | collective-permute-start | bytes 884744 | tf_op jit(solution)/shard_map/ppermute | solution.py:616
  43.2 18.7 %collective-permute-start.16 = (f32[576,128]{1,0:T(8,128)S(1)}, f32[576,128]{1,0:T(8,128)S(1)}, u32[]{:S(2)}, u32[]{:S(2)}) collective-permute-start(f32[576,128]{1,0:T(8,128)S(1)} %get-tuple-element.157), channel_id=1, source_target_pairs={{8,0},{16,8},{24,16},{28,24},{20,28},{12,20},{4,12},{0,4},{9,1},{1... | collective-permute-start | bytes 884744 | tf_op jit(solution)/shard_map/ppermute | solution.py:616
  43.8 11.8 %collective-permute-start.11 = (f32[72,256]{1,0:T(8,128)S(1)}, f32[72,256]{1,0:T(8,128)S(1)}, u32[]{:S(2)}, u32[]{:S(2)}) collective-permute-start(f32[72,256]{1,0:T(8,128)S(1)} %alike.13.refs_0_), channel_id=1, source_target_pairs={{0,16},{4,20},{8,24},{12,28},{16,0},{20,4},{24,8},{28,12},{1,17},{... | collective-permute-start | bytes 221192 | tf_op jit(solution)/shard_map/ppermute | solution.py:575
  61.9 9.0 %collective-permute-start.17 = (f32[576,128]{1,0:T(8,128)S(1)}, f32[576,128]{1,0:T(8,128)S(1)}, u32[]{:S(2)}, u32[]{:S(2)}) collective-permute-start(f32[576,128]{1,0:T(8,128)S(1)} %get-tuple-element.169), channel_id=1, source_target_pairs={{0,8},{8,16},{16,24},{24,28},{28,20},{20,12},{12,4},{4,0},{1,9},{9... | collective-permute-start | bytes 884744 | tf_op jit(solution)/shard_map/ppermute | solution.py:616
  62.0 9.0 %collective-permute-start.18 = (f32[576,128]{1,0:T(8,128)S(1)}, f32[576,128]{1,0:T(8,128)S(1)}, u32[]{:S(2)}, u32[]{:S(2)}) collective-permute-start(f32[576,128]{1,0:T(8,128)S(1)} %get-tuple-element.170), channel_id=1, source_target_pairs={{8,0},{16,8},{24,16},{28,24},{20,28},{12,20},{4,12},{0,4},{9,1},{1... | collective-permute-start | bytes 884744 | tf_op jit(solution)/shard_map/ppermute | solution.py:616
  88.8 13.7 %collective-permute-start.27 = (f32[544,128]{1,0:T(8,128)S(1)}, f32[544,128]{1,0:T(8,128)S(1)}, u32[]{:S(2)}, u32[]{:S(2)}) collective-permute-start(f32[544,128]{1,0:T(8,128)S(1)} %get-tuple-element.190.up_ref.refs_0_), channel_id=1, source_target_pairs={{0,8},{8,16},{16,24},{24,28},{28,20},{20,12},{12,4},{4,0},{1,9},{9... | collective-permute-start | bytes 835592 | tf_op jit(solution)/shard_map/ppermute | solution.py:616
  89.4 13.0 %collective-permute-start.28 = (f32[544,128]{1,0:T(8,128)S(1)}, f32[544,128]{1,0:T(8,128)S(1)}, u32[]{:S(2)}, u32[]{:S(2)}) collective-permute-start(f32[544,128]{1,0:T(8,128)S(1)} %get-tuple-element.191.dn_ref.refs_4_.refs_8_), channel_id=1, source_target_pairs={{8,0},{16,8},{24,16},{28,24},{20,28},{12,20},{4,12},{0,4},{9,1},{1... | collective-permute-start | bytes 835592 | tf_op jit(solution)/shard_map/ppermute | solution.py:616
  102.5 10.2 %collective-permute-start.30 = (f32[544,128]{1,0:T(8,128)S(1)}, f32[544,128]{1,0:T(8,128)S(1)}, u32[]{:S(2)}, u32[]{:S(2)}) collective-permute-start(f32[544,128]{1,0:T(8,128)S(1)} %collective-permute-done.27.refs_0_.refs_6_), channel_id=1, source_target_pairs={{0,8},{8,16},{16,24},{24,28},{28,20},{20,12},{12,4},{4,0},{1,9},{9... | collective-permute-start | bytes 835592 | tf_op jit(solution)/shard_map/ppermute | solution.py:616
  103.1 9.6 %collective-permute-start.31 = (f32[544,128]{1,0:T(8,128)S(1)}, f32[544,128]{1,0:T(8,128)S(1)}, u32[]{:S(2)}, u32[]{:S(2)}) collective-permute-start(f32[544,128]{1,0:T(8,128)S(1)} %collective-permute-done.28.refs_3_.refs_15_), channel_id=1, source_target_pairs={{8,0},{16,8},{24,16},{28,24},{20,28},{12,20},{4,12},{0,4},{9,1},{1... | collective-permute-start | bytes 835592 | tf_op jit(solution)/shard_map/ppermute | solution.py:616
  104.5 8.1 %collective-permute-start.29 = (f32[80,256]{1,0:T(8,128)S(1)}, f32[80,256]{1,0:T(8,128)S(1)}, u32[]{:S(2)}, u32[]{:S(2)}) collective-permute-start(f32[80,256]{1,0:T(8,128)S(1)} %alike.16.refs_0_), channel_id=1, source_target_pairs={{0,8},{4,12},{8,0},{12,4},{16,24},{20,28},{24,16},{28,20},{1,9},{5... | collective-permute-start | bytes 245768 | tf_op jit(solution)/shard_map/ppermute | solution.py:575
  112.7 17.8 %collective-permute-start.36 = (f32[544,128]{1,0:T(8,128)S(1)}, f32[544,128]{1,0:T(8,128)S(1)}, u32[]{:S(2)}, u32[]{:S(2)}) collective-permute-start(f32[544,128]{1,0:T(8,128)S(1)} %collective-permute-done.30.refs_0_.refs_4_), channel_id=1, source_target_pairs={{0,8},{8,16},{16,24},{24,28},{28,20},{20,12},{12,4},{4,0},{1,9},{9... | collective-permute-start | bytes 835592 | tf_op jit(solution)/shard_map/ppermute | solution.py:616
  113.1 17.5 %collective-permute-start.37 = (f32[544,128]{1,0:T(8,128)S(1)}, f32[544,128]{1,0:T(8,128)S(1)}, u32[]{:S(2)}, u32[]{:S(2)}) collective-permute-start(f32[544,128]{1,0:T(8,128)S(1)} %collective-permute-done.31.refs_3_.refs_13_), channel_id=1, source_target_pairs={{8,0},{16,8},{24,16},{28,24},{20,28},{12,20},{4,12},{0,4},{9,1},{1... | collective-permute-start | bytes 835592 | tf_op jit(solution)/shard_map/ppermute | solution.py:616
  114.8 9.7 %collective-permute-start.32 = (f32[80,256]{1,0:T(8,128)S(1)}, f32[80,256]{1,0:T(8,128)S(1)}, u32[]{:S(2)}, u32[]{:S(2)}) collective-permute-start(f32[80,256]{1,0:T(8,128)S(1)} %alike.17.refs_0_), channel_id=1, source_target_pairs={{0,16},{4,20},{8,24},{12,28},{16,0},{20,4},{24,8},{28,12},{1,17},{... | collective-permute-start | bytes 245768 | tf_op jit(solution)/shard_map/ppermute | solution.py:575
  130.6 8.7 %collective-permute-start.38 = (f32[544,128]{1,0:T(8,128)S(1)}, f32[544,128]{1,0:T(8,128)S(1)}, u32[]{:S(2)}, u32[]{:S(2)}) collective-permute-start(f32[544,128]{1,0:T(8,128)S(1)} %collective-permute-done.36.refs_1_), channel_id=1, source_target_pairs={{0,8},{8,16},{16,24},{24,28},{28,20},{20,12},{12,4},{4,0},{1,9},{9... | collective-permute-start | bytes 835592 | tf_op jit(solution)/shard_map/ppermute | solution.py:616
  130.6 8.9 %collective-permute-start.39 = (f32[544,128]{1,0:T(8,128)S(1)}, f32[544,128]{1,0:T(8,128)S(1)}, u32[]{:S(2)}, u32[]{:S(2)}) collective-permute-start(f32[544,128]{1,0:T(8,128)S(1)} %collective-permute-done.37.refs_7_.refs_11_), channel_id=1, source_target_pairs={{8,0},{16,8},{24,16},{28,24},{20,28},{12,20},{4,12},{0,4},{9,1},{1... | collective-permute-start | bytes 835592 | tf_op jit(solution)/shard_map/ppermute | solution.py:616
  147.4 8.1 %collective-permute-start.42 = (f32[544,128]{1,0:T(8,128)S(1)}, f32[544,128]{1,0:T(8,128)S(1)}, u32[]{:S(2)}, u32[]{:S(2)}) collective-permute-start(f32[544,128]{1,0:T(8,128)S(1)} %collective-permute-done.40.refs_3_), channel_id=1, source_target_pairs={{0,8},{8,16},{16,24},{24,28},{28,20},{20,12},{12,4},{4,0},{1,9},{9... | collective-permute-start | bytes 835592 | tf_op jit(solution)/shard_map/ppermute | solution.py:616
  (29 other events, 151.7 us)

commit v3 on v2

--- a/solution.py
+++ b/solution.py
@@ -202,36 +202,45 @@
     return jnp.concatenate([mom[0] + grads[0, 0].astype(F32), grads[1, 0].astype(F32)], axis=0)
 
 
-def lead_kernel(at_ref, mom_up, grads_up, mom_dn, grads_dn, up_ref, dn_ref):
-    up_ref[...] = chunk_rows(mom_up[...], grads_up[...])
-    dn_ref[...] = chunk_rows(mom_dn[...], grads_dn[...])
+def lead_kernel(n, place_ref, mom, grads, up_ref, dn_ref, mom_buf, grads_buf, sem):
+    w = up_ref.shape[1]
+    copies = []
+    for side, offset in enumerate((n - 1, 1)):
+        chunk = lax.rem(place_ref[0] + offset, n)
+        at = pl.ds(pl.multiple_of((2 * chunk + side) * w, w), w)
+        copies.append(
+            (
+                pltpu.make_async_copy(mom.at[:, :, at], mom_buf.at[side], sem.at[side, 0]),
+                pltpu.make_async_copy(grads.at[:, :, :, at], grads_buf.at[side], sem.at[side, 1]),
+            )
+        )
+    for pair in copies:
+        for copy in pair:
+            copy.start()
+    for side, ref in enumerate((up_ref, dn_ref)):
+        for copy in copies[side]:
+            copy.wait()
+        ref[...] = chunk_rows(mom_buf[side], grads_buf[side])
 
 
 def lead(place, momentum, grads, n):
     _, rows, cols = momentum.shape
     w = cols // n // 2
     part = jax.ShapeDtypeStruct((2 * rows, w), F32)
-    specs = []
-    for side, offset in enumerate((n - 1, 1)):
-
-        def half(i, at, side=side, offset=offset):
-            return 2 * lax.rem(at[0] + offset, n) + side
-
-        specs.append(pl.BlockSpec((1, rows, w), lambda i, at, half=half: (0, 0, half(i, at))))
-        specs.append(pl.BlockSpec((2, 1, rows, w), lambda i, at, half=half: (0, 0, 0, half(i, at))))
-    return pl.pallas_call(
-        lead_kernel,
+    return pl.pallas_call(
+        functools.partial(lead_kernel, n),
         out_shape=[part, part],
-        grid_spec=pltpu.PrefetchScalarGridSpec(
-            num_scalar_prefetch=1,
-            grid=(1,),
-            in_specs=specs,
-            out_specs=[whole((2 * rows, w))] * 2,
-        ),
+        in_specs=[SMEM, pl.BlockSpec(memory_space=pltpu.HBM), pl.BlockSpec(memory_space=pltpu.HBM)],
+        out_specs=[VMEM] * 2,
+        scratch_shapes=[
+            pltpu.VMEM((2, 1, rows, w), F32),
+            pltpu.VMEM((2, 2, 1, rows, w), BF16),
+            pltpu.SemaphoreType.DMA((2, 2)),
+        ],
         cost_estimate=cost(4 * rows * w, 32 * rows * w),
         compiler_params=grant(58),
         name="lead",
-    )(place, momentum, grads, momentum, grads)
+    )(place, momentum, grads)
 
 
 def combine_kernel(count, inv, me_ref, mom_ref, grads_ref, right_ref, up_ref, dn_ref, both_ref, *refs):
@@ -577,22 +586,27 @@
 
 def all_sum_stages(box):
     cols, reps = lax.axis_size("col"), lax.axis_size("rep")
+    last = reps.bit_length() - 2
+
+    def send(bit):
+        box["pending"] = flip(box["x"], "rep", 1 << bit)
 
     def scatter():
         got = [flip(box["parts"][d], "col", d) for d in range(1, cols)]
         box["x"] = alike([box["parts"][0]] + got)
+        send(0)
 
     def exchange(bit):
         def stage():
-            got = flip(box["x"], "rep", 1 << bit)
-            box["x"] = alike([box["x"], got])
+            box["x"] = alike([box["x"], box.pop("pending")])
+            if bit < last:
+                send(bit + 1)
+                return
+            box["parts"] = [box["x"]] + [flip(box["x"], "col", d) for d in range(1, cols)]
 
         return stage
 
-    def gather():
-        box["parts"] = [box["x"]] + [flip(box["x"], "col", d) for d in range(1, cols)]
-
-    return [scatter] + [exchange(b) for b in range(reps.bit_length() - 1)] + [gather]
+    return [scatter] + [exchange(b) for b in range(last + 1)]
 
 
 def ring_shards(rate, momentum, grads, weights, right_factor):
@@ -607,7 +621,7 @@
     me = lax.axis_index("col").astype(jnp.int32)[None]
 
     def tie(box, *arrays):
-        keys = list(box)
+        keys = [k for k in box if k != "pending"]
         tied = lax.optimization_barrier(([box[k] for k in keys], list(arrays)))
         box.update(zip(keys, tied[0]))
         return tied[1]
@@ -626,7 +640,7 @@
         return stage
 
     box = {}
-    scatter, *bits, gather = all_sum_stages(box)
+    stages = all_sum_stages(box)
 
     def begin():
         out = combine(me, momentum, grads, right_factor, n, count)
@@ -636,8 +650,7 @@
     def second():
         box["left"], box["leftt"] = orth_second(box.pop("left"), box.pop("rest"))
 
-    work = [[begin, scatter]] + [[bit] for bit in bits] + [[first(False)], [second]]
-    work[len(bits)].append(gather)
+    work = [[begin]] + [[stage] for stage in stages] + [[first(False)], [second]]
     up, dn = lead(place, momentum, grads, n)
     for k in range(1, n):
         up, dn = step(up, dn)
@@ -653,7 +666,7 @@
 
     box = {}
     mine = (up, dn)
-    scatter, *bits, gather = all_sum_stages(box)
+    stages = all_sum_stages(box)
 
     def begin_again():
         box["parts"] = list(partial_raw(me, *mine, rank, count))
@@ -669,9 +682,7 @@
         ys.append(y)
         totals.append(squares)
 
-    work = [[begin_again, scatter, bits[0]]] + [[bit] for bit in bits[1:]]
-    work[-1].append(gather)
-    work += [[first(True)], [second]]
+    work = [[begin_again, stages[0]]] + [[stage] for stage in stages[1:]] + [[first(True)], [second]]
     for _ in range(1, n):
         up, dn = step(up, dn)
         if work:

time: 178 us -> 172 us (0.966)
  waiting for transfers between devices: 70.1 us -> 66.8 us
    ppermute x28, waiting for transfers between devices: 10.7 us -> 4.5 us  [step(): return (lax.ppermute(up, 'rep', ahead), lax.ppermute(dn, 'rep', back))]
    ppermute x21, waiting for transfers between devices: 59.4 us -> 62.3 us  [flip(): return lax.ppermute(x, axis, [(i, i ^ bits) for i in range(size)])]
    pallas_call x3 -> x2, Pallas kernels: 14 us -> 12.4 us  [advance(): pl.pallas_call(functools.partial(advance_kernel, m), out_shape=[jax.Shape...]
  transfers between devices with their start and end apart: 49 -> 49, of which waited for: 28 -> 25; matrix products, arithmetic and copies ran while one was open for 0% -> 0% of each run, Pallas kernels for 22% -> 22%
where the time goes in v3:
time: 172 us
  waiting for transfers between devices  66.8 us (39%)
  Pallas kernels  51 us (30%)
  starting transfers between devices  49.5 us (29%)
  local copies, waits for them, and re-layouts  3.27 us (2%)
    ppermute x21, waiting for transfers between devices, flip(): return lax.ppermute(x, axis, [(i, i ^ bits) for i in range(size)])  62.3 us
    ppermute x28, starting transfers between devices, step(): return (lax.ppermute(up, 'rep', ahead), lax.ppermute(dn, 'rep', back))  30 us
    ppermute x21, starting transfers between devices, flip(): return lax.ppermute(x, axis, [(i, i ^ bits) for i in range(size)])  19.5 us
    pallas_call x2, Pallas kernels, orth_first(): pl.pallas_call(functools.partial(first_kernel, scaled), out_shape=shapes,...  12.5 us
    pallas_call x2, Pallas kernels, advance(): pl.pallas_call(functools.partial(advance_kernel, m), out_shape=[jax.Shape...  12.4 us
    pallas_call x2, Pallas kernels, orth_second(): pl.pallas_call(second_kernel, out_shape=[jax.ShapeDtypeStruct((rows, rank...  11 us
    pallas_call x1, Pallas kernels, finish(): pl.pallas_call(functools.partial(weights_kernel, n, groups, rate), out_sh...  5.85 us
    pallas_call x1, Pallas kernels, combine(): pl.pallas_call(functools.partial(combine_kernel, count, 1.0 / n), out_sha...  4.63 us
  transfers between devices with their start and end apart: 49, of which 25 were waited for; matrix products, arithmetic and copies ran while one was open for 0% of the time, Pallas kernels for 22%

profile of v3, /device:TPU:0, one launch (start us, length us, event | category | flops | bytes accessed | tf_op | source)
XLA Modules:
  0.0 171.9 jit_solution(10990174881638620389)
XLA Ops:
  0.7 2.1 %lead.1 = (f32[576,128]{1,0:T(8,128)}, f32[576,128]{1,0:T(8,128)}) custom-call(s32[1]{0:T(128)} %bitcast.place_ref.at_ref.order_ref, f32[1,288,2048]{2,1,0:T(8,128)} %mom.1, bf16[2,1,288,2048]{3,2,1,0:T(8,128)(2,1)} %grads.1), custom_call_target="tpu_custom_call" | custom-call | flops 147456 | bytes 1179648 | tf_op jit(solution)/shard_map/lead/pallas_call | solution.py:230
  2.8 3.1 %collective-permute-start = (f32[576,128]{1,0:T(8,128)}, f32[576,128]{1,0:T(8,128)S(1)}, u32[]{:S(2)}, u32[]{:S(2)}) collective-permute-start(f32[576,128]{1,0:T(8,128)} %get-tuple-element.135), channel_id=1, source_target_pairs={{0,8},{8,16},{16,24},{24,28},{28,20},{20,12},{12,4},{4,0},{1,9},{9... | collective-permute-start | bytes 884744 | tf_op jit(solution)/shard_map/ppermute | solution.py:630
  9.2 4.6 %combine.1 = (f32[8,576,128]{2,1,0:T(8,128)S(1)}, f32[8,576,128]{2,1,0:T(8,128)S(1)}, f32[1,288,2048]{2,1,0:T(8,128)}, f32[72,256]{1,0:T(8,128)S(1)}, f32[72,256...) custom-call(s32[1]{0:T(128)} %bitcast.1.me_ref, f32[1,288,2048]{2,1,0:T(8,128)S(1)} %copy-done, ...), custom_call_target="tpu_custom_call" | custom-call | flops 1811939328 | bytes 16515072 | tf_op jit(solution)/shard_map/combine/pallas_call | solution.py:285
  18.6 3.0 %collective-permute-done.3.refs_2_ = f32[72,256]{1,0:T(8,128)S(1)} collective-permute-done((f32[72,256]{1,0:T(8,128)S(1)}, f32[72,256]{1,0:T(8,128)S(1)}, u32[]{:S(2)}, u32[]{:S(2)}) %collective-permute-start.3) | collective-permute-done | bytes 73760 | tf_op jit(solution)/shard_map/ppermute | solution.py:584
  26.3 7.5 %collective-permute-done.7.refs_1_ = f32[72,256]{1,0:T(8,128)S(1)} collective-permute-done((f32[72,256]{1,0:T(8,128)S(1)}, f32[72,256]{1,0:T(8,128)S(1)}, u32[]{:S(2)}, u32[]{:S(2)}) %collective-permute-start.7) | collective-permute-done | bytes 73760 | tf_op jit(solution)/shard_map/ppermute | solution.py:584
  37.2 6.4 %collective-permute-done.10.refs_1_ = f32[72,256]{1,0:T(8,128)S(1)} collective-permute-done((f32[72,256]{1,0:T(8,128)S(1)}, f32[72,256]{1,0:T(8,128)S(1)}, u32[]{:S(2)}, u32[]{:S(2)}) %collective-permute-start.10) | collective-permute-done | bytes 73760 | tf_op jit(solution)/shard_map/ppermute | solution.py:584
  45.8 4.6 %collective-permute-start.13 = (f32[72,256]{1,0:T(8,128)S(1)}, f32[72,256]{1,0:T(8,128)S(1)}, u32[]{:S(2)}, u32[]{:S(2)}) collective-permute-start(f32[72,256]{1,0:T(8,128)S(1)} %alike.12.refs_0_), channel_id=1, source_target_pairs={{0,16},{4,20},{8,24},{12,28},{16,0},{20,4},{24,8},{28,12},{1,17},{... | collective-permute-start | bytes 221192 | tf_op jit(solution)/shard_map/ppermute | solution.py:584
  50.4 7.6 %collective-permute-done.13.refs_1_ = f32[72,256]{1,0:T(8,128)S(1)} collective-permute-done((f32[72,256]{1,0:T(8,128)S(1)}, f32[72,256]{1,0:T(8,128)S(1)}, u32[]{:S(2)}, u32[]{:S(2)}) %collective-permute-start.13) | collective-permute-done | bytes 73760 | tf_op jit(solution)/shard_map/ppermute | solution.py:584
  59.9 2.7 %collective-permute-done.16.refs_3_ = f32[72,256]{1,0:T(8,128)S(1)} collective-permute-done((f32[72,256]{1,0:T(8,128)S(1)}, f32[72,256]{1,0:T(8,128)S(1)}, u32[]{:S(2)}, u32[]{:S(2)}) %collective-permute-start.16) | collective-permute-done | bytes 73760 | tf_op jit(solution)/shard_map/ppermute | solution.py:584
  66.4 6.2 %orth_first.2 = (f32[288,128]{1,0:T(8,128)S(1)}, f32[288,128]{1,0:T(8,128)S(1)}) custom-call(s32[1]{0:T(128)} %bitcast.1.me_ref, f32[72,256]{1,0:T(8,128)S(1)} %alike.13.refs_0_, f32[72,256]{1,0:T(8,128)S(1)} %collective-permute-done.14.refs_1_, f32[72,256]{1,0:T(8,128)S(1)} %collective-permute-done.15.refs_2_, f32[72,256]{1,0:T(8,128)S(1)} %collective-permute-done.16.refs_3_), custom_call_target="tpu_custom_call" | custom-call | flops 6000000000 | bytes 1000000 | tf_op jit(solution)/shard_map/orth_first/pallas_call | solution.py:173
  75.5 5.5 %orth_second.2 = (f32[288,256]{1,0:T(8,128)S(1)}, f32[256,288]{1,0:T(8,128)S(1)}) custom-call(f32[288,128]{1,0:T(8,128)S(1)} %get-tuple-element.188.left_ref, f32[288,128]{1,0:T(8,128)S(1)} %get-tuple-element.189.rest_ref), custom_call_target="tpu_custom_call" | custom-call | flops 6000000000 | bytes 1000000 | tf_op jit(solution)/shard_map/orth_second/pallas_call | solution.py:187
  87.9 3.5 %collective-permute-done.24.refs_2_ = f32[80,256]{1,0:T(8,128)S(1)} collective-permute-done((f32[80,256]{1,0:T(8,128)S(1)}, f32[80,256]{1,0:T(8,128)S(1)}, u32[]{:S(2)}, u32[]{:S(2)}) %collective-permute-start.24) | collective-permute-done | bytes 81952 | tf_op jit(solution)/shard_map/ppermute | solution.py:584
  95.8 7.2 %collective-permute-done.28.refs_1_ = f32[80,256]{1,0:T(8,128)S(1)} collective-permute-done((f32[80,256]{1,0:T(8,128)S(1)}, f32[80,256]{1,0:T(8,128)S(1)}, u32[]{:S(2)}, u32[]{:S(2)}) %collective-permute-start.28) | collective-permute-done | bytes 81952 | tf_op jit(solution)/shard_map/ppermute | solution.py:584
  105.1 7.8 %collective-permute-done.31.refs_1_ = f32[80,256]{1,0:T(8,128)S(1)} collective-permute-done((f32[80,256]{1,0:T(8,128)S(1)}, f32[80,256]{1,0:T(8,128)S(1)}, u32[]{:S(2)}, u32[]{:S(2)}) %collective-permute-start.31) | collective-permute-done | bytes 81952 | tf_op jit(solution)/shard_map/ppermute | solution.py:584
  115.0 2.3 %collective-permute-start.34 = (f32[80,256]{1,0:T(8,128)S(1)}, f32[80,256]{1,0:T(8,128)S(1)}, u32[]{:S(2)}, u32[]{:S(2)}) collective-permute-start(f32[80,256]{1,0:T(8,128)S(1)} %alike.16.refs_0_), channel_id=1, source_target_pairs={{0,16},{4,20},{8,24},{12,28},{16,0},{20,4},{24,8},{28,12},{1,17},{... | collective-permute-start | bytes 245768 | tf_op jit(solution)/shard_map/ppermute | solution.py:584
  117.3 7.9 %collective-permute-done.34.refs_1_ = f32[80,256]{1,0:T(8,128)S(1)} collective-permute-done((f32[80,256]{1,0:T(8,128)S(1)}, f32[80,256]{1,0:T(8,128)S(1)}, u32[]{:S(2)}, u32[]{:S(2)}) %collective-permute-start.34) | collective-permute-done | bytes 81952 | tf_op jit(solution)/shard_map/ppermute | solution.py:584
  127.1 2.2 %collective-permute-done.37.refs_3_ = f32[80,256]{1,0:T(8,128)S(1)} collective-permute-done((f32[80,256]{1,0:T(8,128)S(1)}, f32[80,256]{1,0:T(8,128)S(1)}, u32[]{:S(2)}, u32[]{:S(2)}) %collective-permute-start.37) | collective-permute-done | bytes 81952 | tf_op jit(solution)/shard_map/ppermute | solution.py:584
  130.7 2.0 %collective-permute-start.41 = (f32[544,128]{1,0:T(8,128)S(1)}, f32[544,128]{1,0:T(8,128)S(1)}, u32[]{:S(2)}, u32[]{:S(2)}) collective-permute-start(f32[544,128]{1,0:T(8,128)S(1)} %collective-permute-done.39.refs_9_.refs_11_), channel_id=1, source_target_pairs={{8,0},{16,8},{24,16},{28,24},{20,28},{12,20},{4,12},{0,4},{9,1},{1... | collective-permute-start | bytes 835592 | tf_op jit(solution)/shard_map/ppermute | solution.py:630
  132.7 6.3 %orth_first.3 = (f32[288,128]{1,0:T(8,128)S(1)}, f32[288,128]{1,0:T(8,128)S(1)}, f32[1,256]{1,0:T(1,128)S(1)}) custom-call(s32[1]{0:T(128)} %bitcast.1.me_ref, f32[80,256]{1,0:T(8,128)S(1)} %alike.17.refs_0_, f32[80,256]{1,0:T(8,128)S(1)} %collective-permute-done.35.refs_1_, f32[80,256]{1,0:T(8,128)S(1)} %collective-permute-done.36.refs_2_, ...), custom_call_target="tpu_custom_call" | custom-call | flops 6000000000 | bytes 1000000 | tf_op jit(solution)/shard_map/orth_first/pallas_call | solution.py:173
  139.7 2.0 %collective-permute-start.43 = (f32[544,128]{1,0:T(8,128)S(1)}, f32[544,128]{1,0:T(8,128)S(1)}, u32[]{:S(2)}, u32[]{:S(2)}) collective-permute-start(f32[544,128]{1,0:T(8,128)S(1)} %collective-permute-done.41.refs_8_.refs_10_), channel_id=1, source_target_pairs={{8,0},{16,8},{24,16},{28,24},{20,28},{12,20},{4,12},{0,4},{9,1},{1... | collective-permute-start | bytes 835592 | tf_op jit(solution)/shard_map/ppermute | solution.py:630
  141.7 5.5 %orth_second.3 = (f32[288,256]{1,0:T(8,128)S(1)}, f32[256,288]{1,0:T(8,128)S(1)}) custom-call(f32[288,128]{1,0:T(8,128)S(1)} %get-tuple-element.228.left_ref, f32[288,128]{1,0:T(8,128)S(1)} %get-tuple-element.229.rest_ref), custom_call_target="tpu_custom_call" | custom-call | flops 6000000000 | bytes 1000000 | tf_op jit(solution)/shard_map/orth_second/pallas_call | solution.py:187
  149.5 8.3 %advance.2 = (f32[1,288,2048]{2,1,0:T(8,128)}, f32[6,256,256]{2,1,0:T(8,128)S(1)}, f32[8,256]{1,0:T(8,128)S(1)}) custom-call(s32[1]{0:T(128)} %bitcast.place_ref.at_ref.order_ref, f32[544,128]{1,0:T(8,128)S(1)} %get-tuple-element.202.up_ref.refs_0_, f32[544,128]{1,0:T(8,128)S(1)} %collective-permute-done.29.refs_1_, ...), custom_call_target="tpu_custom_call", output_to_operand_aliasing={{0}: (13, {})} | custom-call | flops 3397386240 | bytes 10616832 | tf_op jit(solution)/shard_map/advance/pallas_call | solution.py:493
  157.8 4.2 %advance.3 = (f32[1,288,2048]{2,1,0:T(8,128)}, f32[2,256,256]{2,1,0:T(8,128)S(1)}, f32[8,256]{1,0:T(8,128)S(1)}) custom-call(s32[1]{0:T(128)} %bitcast.place_ref.at_ref.order_ref, f32[544,128]{1,0:T(8,128)S(1)} %collective-permute-done.26.refs_0_.refs_6_, f32[544,128]{1,0:T(8,128)S(1)} %collective-permute-done.44.refs_1_.refs_7_, ...), custom_call_target="tpu_custom_call", output_to_operand_aliasing={{0}: (5, {})} | custom-call | flops 1132462080 | bytes 3538944 | tf_op jit(solution)/shard_map/advance/pallas_call | solution.py:493
  165.8 5.8 %finish.1 = (f32[288,2048]{1,0:T(8,128)}, f32[2048,256]{1,0:T(8,128)}) custom-call(s32[1]{0:T(128)} %bitcast.place_ref.at_ref.order_ref, f32[544,128]{1,0:T(8,128)S(1)} %get-tuple-element.202.up_ref.refs_0_, f32[544,128]{1,0:T(8,128)S(1)} %collective-permute-done.29.refs_1_, f32[544,128]{1,0:T(8,128)S(1)} %collective-permute-done.32.refs_2_, ...), custom_call_target="tpu_custom_call" | custom-call | flops 1811939328 | bytes 18874368 | tf_op jit(solution)/shard_map/finish/pallas_call | solution.py:553
  (109 shorter events, 52.5 us)
Async XLA Ops:
  2.8 11.0 %collective-permute-start = (f32[576,128]{1,0:T(8,128)}, f32[576,128]{1,0:T(8,128)S(1)}, u32[]{:S(2)}, u32[]{:S(2)}) collective-permute-start(f32[576,128]{1,0:T(8,128)} %get-tuple-element.135), channel_id=1, source_target_pairs={{0,8},{8,16},{16,24},{24,28},{28,20},{20,12},{12,4},{4,0},{1,9},{9... | collective-permute-start | bytes 884744 | tf_op jit(solution)/shard_map/ppermute | solution.py:630
  5.9 8.7 %collective-permute-start.1 = (f32[576,128]{1,0:T(8,128)}, f32[576,128]{1,0:T(8,128)S(1)}, u32[]{:S(2)}, u32[]{:S(2)}) collective-permute-start(f32[576,128]{1,0:T(8,128)} %get-tuple-element.136), channel_id=1, source_target_pairs={{8,0},{16,8},{24,16},{28,24},{20,28},{12,20},{4,12},{0,4},{9,1},{1... | collective-permute-start | bytes 884744 | tf_op jit(solution)/shard_map/ppermute | solution.py:630
  23.9 9.9 %collective-permute-start.8 = (f32[576,128]{1,0:T(8,128)S(1)}, f32[576,128]{1,0:T(8,128)S(1)}, u32[]{:S(2)}, u32[]{:S(2)}) collective-permute-start(f32[576,128]{1,0:T(8,128)S(1)} %get-tuple-element.154), channel_id=1, source_target_pairs={{0,8},{8,16},{16,24},{24,28},{28,20},{20,12},{12,4},{4,0},{1,9},{9... | collective-permute-start | bytes 884744 | tf_op jit(solution)/shard_map/ppermute | solution.py:630
  25.6 8.2 %collective-permute-start.9 = (f32[576,128]{1,0:T(8,128)S(1)}, f32[576,128]{1,0:T(8,128)S(1)}, u32[]{:S(2)}, u32[]{:S(2)}) collective-permute-start(f32[576,128]{1,0:T(8,128)S(1)} %get-tuple-element.155), channel_id=1, source_target_pairs={{8,0},{16,8},{24,16},{28,24},{20,28},{12,20},{4,12},{0,4},{9,1},{1... | collective-permute-start | bytes 884744 | tf_op jit(solution)/shard_map/ppermute | solution.py:630
  33.9 9.7 %collective-permute-start.11 = (f32[576,128]{1,0:T(8,128)S(1)}, f32[576,128]{1,0:T(8,128)S(1)}, u32[]{:S(2)}, u32[]{:S(2)}) collective-permute-start(f32[576,128]{1,0:T(8,128)S(1)} %get-tuple-element.162), channel_id=1, source_target_pairs={{0,8},{8,16},{16,24},{24,28},{28,20},{20,12},{12,4},{4,0},{1,9},{9... | collective-permute-start | bytes 884744 | tf_op jit(solution)/shard_map/ppermute | solution.py:630
  35.2 8.4 %collective-permute-start.12 = (f32[576,128]{1,0:T(8,128)S(1)}, f32[576,128]{1,0:T(8,128)S(1)}, u32[]{:S(2)}, u32[]{:S(2)}) collective-permute-start(f32[576,128]{1,0:T(8,128)S(1)} %get-tuple-element.163), channel_id=1, source_target_pairs={{8,0},{16,8},{24,16},{28,24},{20,28},{12,20},{4,12},{0,4},{9,1},{1... | collective-permute-start | bytes 884744 | tf_op jit(solution)/shard_map/ppermute | solution.py:630
  43.7 20.5 %collective-permute-start.17 = (f32[576,128]{1,0:T(8,128)S(1)}, f32[576,128]{1,0:T(8,128)S(1)}, u32[]{:S(2)}, u32[]{:S(2)}) collective-permute-start(f32[576,128]{1,0:T(8,128)S(1)} %get-tuple-element.170), channel_id=1, source_target_pairs={{0,8},{8,16},{16,24},{24,28},{28,20},{20,12},{12,4},{4,0},{1,9},{9... | collective-permute-start | bytes 884744 | tf_op jit(solution)/shard_map/ppermute | solution.py:630
  45.6 18.7 %collective-permute-start.18 = (f32[576,128]{1,0:T(8,128)S(1)}, f32[576,128]{1,0:T(8,128)S(1)}, u32[]{:S(2)}, u32[]{:S(2)}) collective-permute-start(f32[576,128]{1,0:T(8,128)S(1)} %get-tuple-element.171), channel_id=1, source_target_pairs={{8,0},{16,8},{24,16},{28,24},{20,28},{12,20},{4,12},{0,4},{9,1},{1... | collective-permute-start | bytes 884744 | tf_op jit(solution)/shard_map/ppermute | solution.py:630
  45.8 12.2 %collective-permute-start.13 = (f32[72,256]{1,0:T(8,128)S(1)}, f32[72,256]{1,0:T(8,128)S(1)}, u32[]{:S(2)}, u32[]{:S(2)}) collective-permute-start(f32[72,256]{1,0:T(8,128)S(1)} %alike.12.refs_0_), channel_id=1, source_target_pairs={{0,16},{4,20},{8,24},{12,28},{16,0},{20,4},{24,8},{28,12},{1,17},{... | collective-permute-start | bytes 221192 | tf_op jit(solution)/shard_map/ppermute | solution.py:584
  64.3 9.0 %collective-permute-start.19 = (f32[576,128]{1,0:T(8,128)S(1)}, f32[576,128]{1,0:T(8,128)S(1)}, u32[]{:S(2)}, u32[]{:S(2)}) collective-permute-start(f32[576,128]{1,0:T(8,128)S(1)} %get-tuple-element.183), channel_id=1, source_target_pairs={{0,8},{8,16},{16,24},{24,28},{28,20},{20,12},{12,4},{4,0},{1,9},{9... | collective-permute-start | bytes 884744 | tf_op jit(solution)/shard_map/ppermute | solution.py:630
  64.4 9.0 %collective-permute-start.20 = (f32[576,128]{1,0:T(8,128)S(1)}, f32[576,128]{1,0:T(8,128)S(1)}, u32[]{:S(2)}, u32[]{:S(2)}) collective-permute-start(f32[576,128]{1,0:T(8,128)S(1)} %get-tuple-element.184), channel_id=1, source_target_pairs={{8,0},{16,8},{24,16},{28,24},{20,28},{12,20},{4,12},{0,4},{9,1},{1... | collective-permute-start | bytes 884744 | tf_op jit(solution)/shard_map/ppermute | solution.py:630
  83.3 8.9 %collective-permute-start.26 = (f32[544,128]{1,0:T(8,128)S(1)}, f32[544,128]{1,0:T(8,128)S(1)}, u32[]{:S(2)}, u32[]{:S(2)}) collective-permute-start(f32[544,128]{1,0:T(8,128)S(1)} %get-tuple-element.202.up_ref.refs_0_), channel_id=1, source_target_pairs={{0,8},{8,16},{16,24},{24,28},{28,20},{20,12},{12,4},{4,0},{1,9},{9... | collective-permute-start | bytes 835592 | tf_op jit(solution)/shard_map/ppermute | solution.py:630
  92.2 10.8 %collective-permute-start.29 = (f32[544,128]{1,0:T(8,128)S(1)}, f32[544,128]{1,0:T(8,128)S(1)}, u32[]{:S(2)}, u32[]{:S(2)}) collective-permute-start(f32[544,128]{1,0:T(8,128)S(1)} %collective-permute-done.26.refs_0_.refs_6_), channel_id=1, source_target_pairs={{0,8},{8,16},{16,24},{24,28},{28,20},{20,12},{12,4},{4,0},{1,9},{9... | collective-permute-start | bytes 835592 | tf_op jit(solution)/shard_map/ppermute | solution.py:630
  93.4 9.6 %collective-permute-start.30 = (f32[544,128]{1,0:T(8,128)S(1)}, f32[544,128]{1,0:T(8,128)S(1)}, u32[]{:S(2)}, u32[]{:S(2)}) collective-permute-start(f32[544,128]{1,0:T(8,128)S(1)} %collective-permute-done.27.refs_3_.refs_15_), channel_id=1, source_target_pairs={{8,0},{16,8},{24,16},{28,24},{20,28},{12,20},{4,12},{0,4},{9,1},{1... | collective-permute-start | bytes 835592 | tf_op jit(solution)/shard_map/ppermute | solution.py:630
  94.3 8.7 %collective-permute-start.28 = (f32[80,256]{1,0:T(8,128)S(1)}, f32[80,256]{1,0:T(8,128)S(1)}, u32[]{:S(2)}, u32[]{:S(2)}) collective-permute-start(f32[80,256]{1,0:T(8,128)S(1)} %alike.14.refs_0_), channel_id=1, source_target_pairs={{0,4},{4,0},{8,12},{12,8},{16,20},{20,16},{24,28},{28,24},{1,5},{5... | collective-permute-start | bytes 245768 | tf_op jit(solution)/shard_map/ppermute | solution.py:584
  103.0 10.0 %collective-permute-start.32 = (f32[544,128]{1,0:T(8,128)S(1)}, f32[544,128]{1,0:T(8,128)S(1)}, u32[]{:S(2)}, u32[]{:S(2)}) collective-permute-start(f32[544,128]{1,0:T(8,128)S(1)} %collective-permute-done.29.refs_1_), channel_id=1, source_target_pairs={{0,8},{8,16},{16,24},{24,28},{28,20},{20,12},{12,4},{4,0},{1,9},{9... | collective-permute-start | bytes 835592 | tf_op jit(solution)/shard_map/ppermute | solution.py:630
  103.0 9.9 %collective-permute-start.33 = (f32[544,128]{1,0:T(8,128)S(1)}, f32[544,128]{1,0:T(8,128)S(1)}, u32[]{:S(2)}, u32[]{:S(2)}) collective-permute-start(f32[544,128]{1,0:T(8,128)S(1)} %collective-permute-done.30.refs_11_.refs_13_), channel_id=1, source_target_pairs={{8,0},{16,8},{24,16},{28,24},{20,28},{12,20},{4,12},{0,4},{9,1},{1... | collective-permute-start | bytes 835592 | tf_op jit(solution)/shard_map/ppermute | solution.py:630
  112.9 17.7 %collective-permute-start.38 = (f32[544,128]{1,0:T(8,128)S(1)}, f32[544,128]{1,0:T(8,128)S(1)}, u32[]{:S(2)}, u32[]{:S(2)}) collective-permute-start(f32[544,128]{1,0:T(8,128)S(1)} %collective-permute-done.32.refs_2_), channel_id=1, source_target_pairs={{0,8},{8,16},{16,24},{24,28},{28,20},{20,12},{12,4},{4,0},{1,9},{9... | collective-permute-start | bytes 835592 | tf_op jit(solution)/shard_map/ppermute | solution.py:630
  113.2 17.4 %collective-permute-start.39 = (f32[544,128]{1,0:T(8,128)S(1)}, f32[544,128]{1,0:T(8,128)S(1)}, u32[]{:S(2)}, u32[]{:S(2)}) collective-permute-start(f32[544,128]{1,0:T(8,128)S(1)} %collective-permute-done.33.refs_10_.refs_12_), channel_id=1, source_target_pairs={{8,0},{16,8},{24,16},{28,24},{20,28},{12,20},{4,12},{0,4},{9,1},{1... | collective-permute-start | bytes 835592 | tf_op jit(solution)/shard_map/ppermute | solution.py:630
  115.0 10.1 %collective-permute-start.34 = (f32[80,256]{1,0:T(8,128)S(1)}, f32[80,256]{1,0:T(8,128)S(1)}, u32[]{:S(2)}, u32[]{:S(2)}) collective-permute-start(f32[80,256]{1,0:T(8,128)S(1)} %alike.16.refs_0_), channel_id=1, source_target_pairs={{0,16},{4,20},{8,24},{12,28},{16,0},{20,4},{24,8},{28,12},{1,17},{... | collective-permute-start | bytes 245768 | tf_op jit(solution)/shard_map/ppermute | solution.py:584
  130.6 8.7 %collective-permute-start.40 = (f32[544,128]{1,0:T(8,128)S(1)}, f32[544,128]{1,0:T(8,128)S(1)}, u32[]{:S(2)}, u32[]{:S(2)}) collective-permute-start(f32[544,128]{1,0:T(8,128)S(1)} %collective-permute-done.38.refs_3_), channel_id=1, source_target_pairs={{0,8},{8,16},{16,24},{24,28},{28,20},{20,12},{12,4},{4,0},{1,9},{9... | collective-permute-start | bytes 835592 | tf_op jit(solution)/shard_map/ppermute | solution.py:630
  130.7 8.9 %collective-permute-start.41 = (f32[544,128]{1,0:T(8,128)S(1)}, f32[544,128]{1,0:T(8,128)S(1)}, u32[]{:S(2)}, u32[]{:S(2)}) collective-permute-start(f32[544,128]{1,0:T(8,128)S(1)} %collective-permute-done.39.refs_9_.refs_11_), channel_id=1, source_target_pairs={{8,0},{16,8},{24,16},{28,24},{20,28},{12,20},{4,12},{0,4},{9,1},{1... | collective-permute-start | bytes 835592 | tf_op jit(solution)/shard_map/ppermute | solution.py:630
  147.5 10.3 %collective-permute-start.44 = (f32[544,128]{1,0:T(8,128)S(1)}, f32[544,128]{1,0:T(8,128)S(1)}, u32[]{:S(2)}, u32[]{:S(2)}) collective-permute-start(f32[544,128]{1,0:T(8,128)S(1)} %collective-permute-done.42.refs_5_), channel_id=1, source_target_pairs={{0,8},{8,16},{16,24},{24,28},{28,20},{20,12},{12,4},{4,0},{1,9},{9... | collective-permute-start | bytes 835592 | tf_op jit(solution)/shard_map/ppermute | solution.py:630
  149.3 8.6 %collective-permute-start.45 = (f32[544,128]{1,0:T(8,128)S(1)}, f32[544,128]{1,0:T(8,128)S(1)}, u32[]{:S(2)}, u32[]{:S(2)}) collective-permute-start(f32[544,128]{1,0:T(8,128)S(1)} %collective-permute-done.43.refs_7_.refs_9_), channel_id=1, source_target_pairs={{8,0},{16,8},{24,16},{28,24},{20,28},{12,20},{4,12},{0,4},{9,1},{1... | collective-permute-start | bytes 835592 | tf_op jit(solution)/shard_map/ppermute | solution.py:630
  (29 other events, 158.0 us)

commit v4 on v3

--- a/solution.py
+++ b/solution.py
@@ -300,7 +300,7 @@
         + [pl.BlockSpec((rows // count, rank), lambda k: (0, 0))] * count,
         scratch_shapes=[pltpu.VMEM((rows, rank), F32)],
         cost_estimate=cost(12 * rows * cols * rank, 28 * rows * cols),
-        compiler_params=grant(20),
+        compiler_params=grant(47),
         name="combine",
     )(me, momentum, grads, right_factor)
     return out[0], out[1], out[2], out[3:]
@@ -462,15 +462,53 @@
     y_out[0] = y2
     y = halves(jnp.concatenate([y1, y2], axis=0))
     mom_out[0] = both_ref[0] - dot3((update[0], update[1]), y)
-    squares = dot(jnp.ones((8, 2 * w), F32), y2 * y2, 1, 1)
+    add_squares(k, y2, sq_out)
+
+
+def add_squares(k, y, out):
+    squares = dot(jnp.ones((8, y.shape[1]), F32), y * y, 1, 1)
 
     @pl.when(k == 0)
     def _():
-        sq_out[...] = squares
+        out[...] = squares
 
     @pl.when(k > 0)
     def _():
-        sq_out[...] += squares
+        out[...] += squares
+
+
+def project_kernel(m, order_ref, *refs):
+    ups, dns = refs[:m], refs[m : 2 * m]
+    l2t_ref, y_out, sq_out, buf, sem, project = refs[2 * m :]
+    k = pl.program_id(0)
+    rank, rows = l2t_ref.shape
+    w = buf.shape[2] // 2
+
+    @pl.when(k == 0)
+    def _():
+        project[0], project[1] = halves(l2t_ref[...])
+
+    at = pl.ds(rank, rows)
+    averaged = fetcher([[(ups[i].at[at, :], 0, 0), (dns[i].at[at, :], 0, w)] for i in range(m)], buf, sem)
+    y2 = dot3((project[0], project[1]), halves(averaged))
+    y_out[0] = y2
+    add_squares(k, y2, sq_out)
+
+
+def moment_kernel(m, order_ref, *refs):
+    ups, dns = refs[:m], refs[m : 2 * m]
+    both_ref, y_ref, l1_ref, l2_ref, mom_out, buf, sem, update = refs[2 * m :]
+    rank = y_ref.shape[1]
+    w = buf.shape[2] // 2
+
+    @pl.when(pl.program_id(0) == 0)
+    def _():
+        update[0], update[1] = halves(DAMPING * jnp.concatenate([l1_ref[...], l2_ref[...]], axis=1))
+
+    at = pl.ds(0, rank)
+    y1 = fetcher([[(ups[i].at[at, :], 0, 0), (dns[i].at[at, :], 0, w)] for i in range(m)], buf, sem)
+    y = halves(jnp.concatenate([y1, y_ref[0]], axis=0))
+    mom_out[0] = both_ref[0] - dot3((update[0], update[1]), y)
 
 
 def chunk_at(steps, n):
@@ -483,37 +521,48 @@
     return at
 
 
-def advance(place, steps, n, ups, dns, both, l1, l2, l2t):
+def advance(mode, place, steps, n, ups, dns, both, y, l1, l2, l2t):
     m = len(ups)
     _, rows, _ = both.shape
     rank = l1.shape[1]
     w = 2 * ups[0].shape[1]
     at = chunk_at(steps, n)
     block = pl.BlockSpec((1, rows, w), lambda k, place: (0, 0, at(k, place)))
+    y_block = pl.BlockSpec((1, rank, w), lambda k, place: (k, 0, 0))
+    factors = [whole((rows, rank)), whole((rows, rank))]
+    projected = [jax.ShapeDtypeStruct((m, rank, w), F32), jax.ShapeDtypeStruct((8, rank), F32)]
+    moment = [jax.ShapeDtypeStruct(both.shape, F32)]
+    project_scratch = pltpu.VMEM((2, rank, rows), BF16)
+    moment_scratch = pltpu.VMEM((2, rows, 2 * rank), BF16)
+    kernel, args, specs, outs, out_specs, scratch, fetched, aliases = {
+        "both": (
+            advance_kernel, [both, l1, l2, l2t], [block] + factors + [whole((rank, rows))],
+            moment + projected, [block, y_block, whole((8, rank))],
+            [project_scratch, moment_scratch], rank + rows, {1 + 2 * m: 0},
+        ),
+        "project": (
+            project_kernel, [l2t], [whole((rank, rows))],
+            projected, [y_block, whole((8, rank))], [project_scratch], rows, {},
+        ),
+        "moment": (
+            moment_kernel, [both, y, l1, l2], [block, y_block] + factors,
+            moment, [block], [moment_scratch], rank, {1 + 2 * m: 0},
+        ),
+    }[mode]
     return pl.pallas_call(
-        functools.partial(advance_kernel, m),
-        out_shape=[
-            jax.ShapeDtypeStruct(both.shape, F32),
-            jax.ShapeDtypeStruct((m, rank, w), F32),
-            jax.ShapeDtypeStruct((8, rank), F32),
-        ],
+        functools.partial(kernel, m),
+        out_shape=outs,
         grid_spec=pltpu.PrefetchScalarGridSpec(
             num_scalar_prefetch=1,
             grid=(m,),
-            in_specs=[VMEM] * (2 * m) + [block, whole((rows, rank)), whole((rows, rank)), whole((rank, rows))],
-            out_specs=[block, pl.BlockSpec((1, rank, w), lambda k, order: (k, 0, 0)), whole((8, rank))],
-            scratch_shapes=[
-                pltpu.VMEM((2, rank + rows, w), F32),
-                pltpu.SemaphoreType.DMA((2, 2)),
-                pltpu.VMEM((2, rank, rows), BF16),
-                pltpu.VMEM((2, rows, 2 * rank), BF16),
-            ],
+            in_specs=[VMEM] * (2 * m) + specs,
+            out_specs=out_specs,
+            scratch_shapes=[pltpu.VMEM((2, fetched, w), F32), pltpu.SemaphoreType.DMA((2, 2))] + scratch,
         ),
-        input_output_aliases={1 + 2 * m: 0},
-        cost_estimate=cost(m * w * 30 * rows * rank, m * w * rows * 24),
+        input_output_aliases=aliases,
+        cost_estimate=cost(m * w * 20 * rows * rank, m * w * rows * 24),
         compiler_params=grant(14),
-        name="advance",
-    )(place, *ups, *dns, both, l1, l2, l2t)
+    )(place, *ups, *dns, *args)
 
 
 def weights_kernel(n, groups, rate, order_ref, *refs):
@@ -584,29 +633,33 @@
     return lax.ppermute(x, axis, [(i, i ^ bits) for i in range(size)])
 
 
+def rep_masks(reps):
+    return [[1, 2, 3]] + [[1 << b] for b in range(2, reps.bit_length() - 1)]
+
+
 def all_sum_stages(box):
-    cols, reps = lax.axis_size("col"), lax.axis_size("rep")
-    last = reps.bit_length() - 2
-
-    def send(bit):
-        box["pending"] = flip(box["x"], "rep", 1 << bit)
+    cols = lax.axis_size("col")
+    masks = rep_masks(lax.axis_size("rep"))
+
+    def send(x, axis, partners):
+        return [flip(part, axis, p) for part, p in zip(x, partners)]
 
     def scatter():
-        got = [flip(box["parts"][d], "col", d) for d in range(1, cols)]
-        box["x"] = alike([box["parts"][0]] + got)
-        send(0)
-
-    def exchange(bit):
+        parts = box.pop("parts")
+        box["x"] = parts[0]
+        box["pending"] = send(parts[1:], "col", range(1, cols))
+
+    def exchange(i):
         def stage():
-            box["x"] = alike([box["x"], box.pop("pending")])
-            if bit < last:
-                send(bit + 1)
-                return
-            box["parts"] = [box["x"]] + [flip(box["x"], "col", d) for d in range(1, cols)]
+            x = box["x"] = alike([box["x"]] + box.pop("pending"))
+            if i < len(masks):
+                box["pending"] = send([x] * len(masks[i]), "rep", masks[i])
+            else:
+                box["pending"] = send([x] * (cols - 1), "col", range(1, cols))
 
         return stage
 
-    return [scatter] + [exchange(b) for b in range(last + 1)]
+    return [scatter] + [exchange(i) for i in range(len(masks) + 1)]
 
 
 def ring_shards(rate, momentum, grads, weights, right_factor):
@@ -631,8 +684,7 @@
 
     def first(scaled):
         def stage():
-            out = orth_first(me, box.pop("parts"), rows, scaled)
-            box.pop("x")
+            out = orth_first(me, [box.pop("x")] + box.pop("pending"), rows, scaled)
             box["left"], box["rest"] = out[:2]
             if scaled:
                 box["norm"] = out[2]
@@ -674,13 +726,22 @@
     ups, dns = [up], [dn]
     ready, ys, totals = [], [], []
 
-    def advance_ready():
+    def advance_ready(last=False):
         new = [c for c in range(n) if c not in ready and c < len(ups) and (n - c) % n < len(dns)]
         ready.extend(new)
         sides = ([ups[c] for c in new], [dns[(n - c) % n] for c in new])
-        box["both"], y, squares = advance(place, new, n, *sides, box["both"], l1, box["left"], box["leftt"])
+        factors = (l1, box["left"], box["leftt"])
+        if not last:
+            box["both"], y, squares = advance("both", place, new, n, *sides, box["both"], None, *factors)
+            ys.append(y)
+            totals.append(squares)
+            return None
+        y, squares = advance("project", place, new, n, *sides, box["both"], None, *factors)
         ys.append(y)
         totals.append(squares)
+        total = alike_total(totals, count)
+        (box["both"],) = advance("moment", place, new, n, *sides, box["both"], y, *factors)
+        return total
 
     work = [[begin_again, stages[0]]] + [[stage] for stage in stages[1:]] + [[first(True)], [second]]
     for _ in range(1, n):
@@ -696,8 +757,7 @@
         ups.append(up)
         dns.append(dn)
     box.setdefault("both", both)
-    advance_ready()
-    total = alike_total(totals, count)
+    total = advance_ready(last=True)
     sides = ([ups[c] for c in ready], [dns[(n - c) % n] for c in ready])
     new_weights, new_right = finish(place, ready, *sides, ys, weights, l1, box["left"], box["norm"], [total], rate)
     return new_weights, box["both"], new_right

time: 172 us -> 167 us (0.971)
  waiting for transfers between devices: 66.8 us -> 62.8 us
  local copies, waits for them, and re-layouts: 3.27 us -> 0.01 us
  Pallas kernels: 51 us -> 53.4 us
    ppermute x21 -> x23, waiting for transfers between devices: 62.3 us -> 44.9 us  [flip(): return lax.ppermute(x, axis, [(i, i ^ bits) for i in range(size)])]
    ppermute x28, waiting for transfers between devices: 4.5 us -> 18 us  [step(): return (lax.ppermute(up, 'rep', ahead), lax.ppermute(dn, 'rep', back))]
    unnamed x8 -> x4, local copies, waits for them, and re-layouts: 3.27 us -> 0.01 us
    pallas_call x2 -> x3, Pallas kernels: 12.4 us -> 13.2 us  [advance(): pl.pallas_call(functools.partial(kernel, m), out_shape=outs, grid_spec=pl...]
    ppermute x21 -> x23, starting transfers between devices: 19.5 us -> 19.3 us  [flip(): return lax.ppermute(x, axis, [(i, i ^ bits) for i in range(size)])]
  transfers between devices with their start and end apart: 49 -> 51, of which waited for: 25 -> 25; matrix products, arithmetic and copies ran while one was open for 0% -> 0% of each run, Pallas kernels for 22% -> 25%
where the time goes in v4:
time: 167 us
  waiting for transfers between devices  62.8 us (38%)
  Pallas kernels  53.4 us (32%)
  starting transfers between devices  49.3 us (30%)
    ppermute x23, waiting for transfers between devices, flip(): return lax.ppermute(x, axis, [(i, i ^ bits) for i in range(size)])  44.9 us
    ppermute x28, starting transfers between devices, step(): return (lax.ppermute(up, 'rep', ahead), lax.ppermute(dn, 'rep', back))  29.9 us
    ppermute x23, starting transfers between devices, flip(): return lax.ppermute(x, axis, [(i, i ^ bits) for i in range(size)])  19.3 us
    ppermute x28, waiting for transfers between devices, step(): return (lax.ppermute(up, 'rep', ahead), lax.ppermute(dn, 'rep', back))  18 us
    pallas_call x3, Pallas kernels, advance(): pl.pallas_call(functools.partial(kernel, m), out_shape=outs, grid_spec=pl...  13.2 us
    pallas_call x2, Pallas kernels, orth_first(): pl.pallas_call(functools.partial(first_kernel, scaled), out_shape=shapes,...  12.5 us
    pallas_call x2, Pallas kernels, orth_second(): pl.pallas_call(second_kernel, out_shape=[jax.ShapeDtypeStruct((rows, rank...  11 us
    pallas_call x1, Pallas kernels, combine(): pl.pallas_call(functools.partial(combine_kernel, count, 1.0 / n), out_sha...  6.21 us
  transfers between devices with their start and end apart: 51, of which 25 were waited for; matrix products, arithmetic and copies ran while one was open for 0% of the time, Pallas kernels for 25%

profile of v4, /device:TPU:0, one launch (start us, length us, event | category | flops | bytes accessed | tf_op | source)
XLA Modules:
  0.0 166.7 jit_solution(1707200459586826289)
XLA Ops:
  0.7 2.1 %lead.1 = (f32[576,128]{1,0:T(8,128)}, f32[576,128]{1,0:T(8,128)}) custom-call(s32[1]{0:T(128)} %bitcast.place_ref.at_ref.order_ref, f32[1,288,2048]{2,1,0:T(8,128)} %mom.1, bf16[2,1,288,2048]{3,2,1,0:T(8,128)(2,1)} %grads.1), custom_call_target="tpu_custom_call" | custom-call | flops 147456 | bytes 1179648 | tf_op jit(solution)/shard_map/lead/pallas_call | solution.py:230
  2.8 3.1 %collective-permute-start = (f32[576,128]{1,0:T(8,128)}, f32[576,128]{1,0:T(8,128)S(1)}, u32[]{:S(2)}, u32[]{:S(2)}) collective-permute-start(f32[576,128]{1,0:T(8,128)} %get-tuple-element.128), channel_id=1, source_target_pairs={{0,8},{8,16},{16,24},{24,28},{28,20},{20,12},{12,4},{4,0},{1,9},{9... | collective-permute-start | bytes 884744 | tf_op jit(solution)/shard_map/ppermute | solution.py:683
  5.9 6.2 %combine.1 = (f32[8,576,128]{2,1,0:T(8,128)S(1)}, f32[8,576,128]{2,1,0:T(8,128)S(1)}, f32[1,288,2048]{2,1,0:T(8,128)}, f32[72,256]{1,0:T(8,128)S(1)}, f32[72,256...) custom-call(s32[1]{0:T(128)} %bitcast.1.me_ref, f32[1,288,2048]{2,1,0:T(8,128)} %mom.1, ...), custom_call_target="tpu_custom_call" | custom-call | flops 1811939328 | bytes 16515072 | tf_op jit(solution)/shard_map/combine/pallas_call | solution.py:285
  16.7 5.6 %collective-permute-done.2.up_ref = f32[576,128]{1,0:T(8,128)S(1)} collective-permute-done((f32[576,128]{1,0:T(8,128)S(1)}, f32[576,128]{1,0:T(8,128)S(1)}, u32[]{:S(2)}, u32[]{:S(2)}) %collective-permute-start.2) | collective-permute-done | bytes 294944 | tf_op jit(solution)/shard_map/ppermute | solution.py:683
  27.6 3.0 %collective-permute-done.5.refs_2_ = f32[72,256]{1,0:T(8,128)S(1)} collective-permute-done((f32[72,256]{1,0:T(8,128)S(1)}, f32[72,256]{1,0:T(8,128)S(1)}, u32[]{:S(2)}, u32[]{:S(2)}) %collective-permute-start.5) | collective-permute-done | bytes 73760 | tf_op jit(solution)/shard_map/ppermute | solution.py:633
  37.7 5.9 %collective-permute-done.11.refs_3_ = f32[72,256]{1,0:T(8,128)S(1)} collective-permute-done((f32[72,256]{1,0:T(8,128)S(1)}, f32[72,256]{1,0:T(8,128)S(1)}, u32[]{:S(2)}, u32[]{:S(2)}) %collective-permute-start.11) | collective-permute-done | bytes 73760 | tf_op jit(solution)/shard_map/ppermute | solution.py:633
  43.6 2.1 %collective-permute-done.10.refs_2_ = f32[72,256]{1,0:T(8,128)S(1)} collective-permute-done((f32[72,256]{1,0:T(8,128)S(1)}, f32[72,256]{1,0:T(8,128)S(1)}, u32[]{:S(2)}, u32[]{:S(2)}) %collective-permute-start.10) | collective-permute-done | bytes 73760 | tf_op jit(solution)/shard_map/ppermute | solution.py:633
  49.2 8.5 %collective-permute-done.14.refs_1_ = f32[72,256]{1,0:T(8,128)S(1)} collective-permute-done((f32[72,256]{1,0:T(8,128)S(1)}, f32[72,256]{1,0:T(8,128)S(1)}, u32[]{:S(2)}, u32[]{:S(2)}) %collective-permute-start.14) | collective-permute-done | bytes 73760 | tf_op jit(solution)/shard_map/ppermute | solution.py:633
  59.7 2.0 %collective-permute-start.21 = (f32[576,128]{1,0:T(8,128)S(1)}, f32[576,128]{1,0:T(8,128)S(1)}, u32[]{:S(2)}, u32[]{:S(2)}) collective-permute-start(f32[576,128]{1,0:T(8,128)S(1)} %get-tuple-element.174), channel_id=1, source_target_pairs={{8,0},{16,8},{24,16},{28,24},{20,28},{12,20},{4,12},{0,4},{9,1},{1... | collective-permute-start | bytes 884744 | tf_op jit(solution)/shard_map/ppermute | solution.py:683
  63.9 6.2 %orth_first.2 = (f32[288,128]{1,0:T(8,128)S(1)}, f32[288,128]{1,0:T(8,128)S(1)}) custom-call(s32[1]{0:T(128)} %bitcast.1.me_ref, f32[72,256]{1,0:T(8,128)S(1)} %alike.10.refs_0_, f32[72,256]{1,0:T(8,128)S(1)} %collective-permute-done.17.refs_1_, f32[72,256]{1,0:T(8,128)S(1)} %collective-permute-done.18.refs_2_, f32[72,256]{1,0:T(8,128)S(1)} %collective-permute-done.19.refs_3_), custom_call_target="tpu_custom_call" | custom-call | flops 6000000000 | bytes 1000000 | tf_op jit(solution)/shard_map/orth_first/pallas_call | solution.py:173
  70.3 2.0 %collective-permute-start.23 = (f32[576,128]{1,0:T(8,128)S(1)}, f32[576,128]{1,0:T(8,128)S(1)}, u32[]{:S(2)}, u32[]{:S(2)}) collective-permute-start(f32[576,128]{1,0:T(8,128)S(1)} %get-tuple-element.185), channel_id=1, source_target_pairs={{8,0},{16,8},{24,16},{28,24},{20,28},{12,20},{4,12},{0,4},{9,1},{1... | collective-permute-start | bytes 884744 | tf_op jit(solution)/shard_map/ppermute | solution.py:683
  72.3 5.5 %orth_second.2 = (f32[288,256]{1,0:T(8,128)S(1)}, f32[256,288]{1,0:T(8,128)S(1)}) custom-call(f32[288,128]{1,0:T(8,128)S(1)} %get-tuple-element.178.left_ref, f32[288,128]{1,0:T(8,128)S(1)} %get-tuple-element.179.rest_ref), custom_call_target="tpu_custom_call" | custom-call | flops 6000000000 | bytes 1000000 | tf_op jit(solution)/shard_map/orth_second/pallas_call | solution.py:187
  83.6 5.0 %collective-permute-done.24.refs_0_.refs_6_ = f32[544,128]{1,0:T(8,128)S(1)} collective-permute-done((f32[544,128]{1,0:T(8,128)S(1)}, f32[544,128]{1,0:T(8,128)S(1)}, u32[]{:S(2)}, u32[]{:S(2)}) %collective-permute-start.24) | collective-permute-done | bytes 278560 | tf_op jit(solution)/shard_map/ppermute | solution.py:683
  92.5 3.5 %collective-permute-done.27.refs_2_ = f32[80,256]{1,0:T(8,128)S(1)} collective-permute-done((f32[80,256]{1,0:T(8,128)S(1)}, f32[80,256]{1,0:T(8,128)S(1)}, u32[]{:S(2)}, u32[]{:S(2)}) %collective-permute-start.27) | collective-permute-done | bytes 81952 | tf_op jit(solution)/shard_map/ppermute | solution.py:633
  98.9 2.3 %collective-permute-start.33 = (f32[80,256]{1,0:T(8,128)S(1)}, f32[80,256]{1,0:T(8,128)S(1)}, u32[]{:S(2)}, u32[]{:S(2)}) collective-permute-start(f32[80,256]{1,0:T(8,128)S(1)} %alike.11.refs_0_), channel_id=1, source_target_pairs={{0,12},{4,8},{8,4},{12,0},{16,28},{20,24},{24,20},{28,16},{1,13},{... | collective-permute-start | bytes 245768 | tf_op jit(solution)/shard_map/ppermute | solution.py:633
  102.4 6.9 %collective-permute-done.33.refs_3_ = f32[80,256]{1,0:T(8,128)S(1)} collective-permute-done((f32[80,256]{1,0:T(8,128)S(1)}, f32[80,256]{1,0:T(8,128)S(1)}, u32[]{:S(2)}, u32[]{:S(2)}) %collective-permute-start.33) | collective-permute-done | bytes 81952 | tf_op jit(solution)/shard_map/ppermute | solution.py:633
  113.8 8.6 %collective-permute-done.36.refs_1_ = f32[80,256]{1,0:T(8,128)S(1)} collective-permute-done((f32[80,256]{1,0:T(8,128)S(1)}, f32[80,256]{1,0:T(8,128)S(1)}, u32[]{:S(2)}, u32[]{:S(2)}) %collective-permute-start.36) | collective-permute-done | bytes 81952 | tf_op jit(solution)/shard_map/ppermute | solution.py:633
  124.4 2.0 %collective-permute-start.43 = (f32[544,128]{1,0:T(8,128)S(1)}, f32[544,128]{1,0:T(8,128)S(1)}, u32[]{:S(2)}, u32[]{:S(2)}) collective-permute-start(f32[544,128]{1,0:T(8,128)S(1)} %collective-permute-done.38.refs_9_.refs_11_), channel_id=1, source_target_pairs={{8,0},{16,8},{24,16},{28,24},{20,28},{12,20},{4,12},{0,4},{9,1},{1... | collective-permute-start | bytes 835592 | tf_op jit(solution)/shard_map/ppermute | solution.py:683
  127.9 6.3 %orth_first.3 = (f32[288,128]{1,0:T(8,128)S(1)}, f32[288,128]{1,0:T(8,128)S(1)}, f32[1,256]{1,0:T(1,128)S(1)}) custom-call(s32[1]{0:T(128)} %bitcast.1.me_ref, f32[80,256]{1,0:T(8,128)S(1)} %alike.13.refs_0_, f32[80,256]{1,0:T(8,128)S(1)} %collective-permute-done.39.refs_1_, f32[80,256]{1,0:T(8,128)S(1)} %collective-permute-done.40.refs_2_, ...), custom_call_target="tpu_custom_call" | custom-call | flops 6000000000 | bytes 1000000 | tf_op jit(solution)/shard_map/orth_first/pallas_call | solution.py:173
  134.2 2.0 %collective-permute-start.45 = (f32[544,128]{1,0:T(8,128)S(1)}, f32[544,128]{1,0:T(8,128)S(1)}, u32[]{:S(2)}, u32[]{:S(2)}) collective-permute-start(f32[544,128]{1,0:T(8,128)S(1)} %collective-permute-done.43.refs_8_.refs_10_), channel_id=1, source_target_pairs={{8,0},{16,8},{24,16},{28,24},{20,28},{12,20},{4,12},{0,4},{9,1},{1... | collective-permute-start | bytes 835592 | tf_op jit(solution)/shard_map/ppermute | solution.py:683
  136.3 5.5 %orth_second.3 = (f32[288,256]{1,0:T(8,128)S(1)}, f32[256,288]{1,0:T(8,128)S(1)}) custom-call(f32[288,128]{1,0:T(8,128)S(1)} %get-tuple-element.215.left_ref, f32[288,128]{1,0:T(8,128)S(1)} %get-tuple-element.216.rest_ref), custom_call_target="tpu_custom_call" | custom-call | flops 6000000000 | bytes 1000000 | tf_op jit(solution)/shard_map/orth_second/pallas_call | solution.py:187
  145.4 8.3 %shard_map.67 = (f32[1,288,2048]{2,1,0:T(8,128)}, f32[6,256,256]{2,1,0:T(8,128)S(1)}, f32[8,256]{1,0:T(8,128)S(1)}) custom-call(s32[1]{0:T(128)} %bitcast.place_ref.at_ref.order_ref, f32[544,128]{1,0:T(8,128)S(1)} %get-tuple-element.192.up_ref.refs_0_, f32[544,128]{1,0:T(8,128)S(1)} %collective-permute-done.29.refs_1_, ...), custom_call_target="tpu_custom_call", output_to_operand_aliasing={{0}: (13, {})} | custom-call | flops 2264924160 | bytes 10616832 | tf_op jit(solution)/shard_map/pallas_call | solution.py:552
  157.7 2.9 %shard_map.69 = f32[1,288,2048]{2,1,0:T(8,128)} custom-call(s32[1]{0:T(128)} %bitcast.place_ref.at_ref.order_ref, f32[544,128]{1,0:T(8,128)S(1)} %collective-permute-done.24.refs_0_.refs_6_, f32[544,128]{1,0:T(8,128)S(1)} %collective-permute-done.46.refs_1_.refs_7_, ...), custom_call_target="tpu_custom_call", output_to_operand_aliasing={{}: (5, {})} | custom-call | flops 754974720 | bytes 3538944 | tf_op jit(solution)/shard_map/pallas_call | solution.py:552
  160.6 5.8 %finish.1 = (f32[288,2048]{1,0:T(8,128)}, f32[2048,256]{1,0:T(8,128)}) custom-call(s32[1]{0:T(128)} %bitcast.place_ref.at_ref.order_ref, f32[544,128]{1,0:T(8,128)S(1)} %get-tuple-element.192.up_ref.refs_0_, f32[544,128]{1,0:T(8,128)S(1)} %collective-permute-done.29.refs_1_, f32[544,128]{1,0:T(8,128)S(1)} %collective-permute-done.34.refs_2_, ...), custom_call_target="tpu_custom_call" | custom-call | flops 1811939328 | bytes 18874368 | tf_op jit(solution)/shard_map/finish/pallas_call | solution.py:602
  (108 shorter events, 54.1 us)
Async XLA Ops:
  2.8 10.3 %collective-permute-start = (f32[576,128]{1,0:T(8,128)}, f32[576,128]{1,0:T(8,128)S(1)}, u32[]{:S(2)}, u32[]{:S(2)}) collective-permute-start(f32[576,128]{1,0:T(8,128)} %get-tuple-element.128), channel_id=1, source_target_pairs={{0,8},{8,16},{16,24},{24,28},{28,20},{20,12},{12,4},{4,0},{1,9},{9... | collective-permute-start | bytes 884744 | tf_op jit(solution)/shard_map/ppermute | solution.py:683
  32.1 13.6 %collective-permute-start.12 = (f32[576,128]{1,0:T(8,128)S(1)}, f32[576,128]{1,0:T(8,128)S(1)}, u32[]{:S(2)}, u32[]{:S(2)}) collective-permute-start(f32[576,128]{1,0:T(8,128)S(1)} %get-tuple-element.155), channel_id=1, source_target_pairs={{0,8},{8,16},{16,24},{24,28},{28,20},{20,12},{12,4},{4,0},{1,9},{9... | collective-permute-start | bytes 884744 | tf_op jit(solution)/shard_map/ppermute | solution.py:683
  33.7 12.0 %collective-permute-start.13 = (f32[576,128]{1,0:T(8,128)S(1)}, f32[576,128]{1,0:T(8,128)S(1)}, u32[]{:S(2)}, u32[]{:S(2)}) collective-permute-start(f32[576,128]{1,0:T(8,128)S(1)} %get-tuple-element.156), channel_id=1, source_target_pairs={{8,0},{16,8},{24,16},{28,24},{20,28},{12,20},{4,12},{0,4},{9,1},{1... | collective-permute-start | bytes 884744 | tf_op jit(solution)/shard_map/ppermute | solution.py:683
  34.2 9.4 %collective-permute-start.11 = (f32[72,256]{1,0:T(8,128)S(1)}, f32[72,256]{1,0:T(8,128)S(1)}, u32[]{:S(2)}, u32[]{:S(2)}) collective-permute-start(f32[72,256]{1,0:T(8,128)S(1)} %alike.8.refs_0_), channel_id=1, source_target_pairs={{0,12},{4,8},{8,4},{12,0},{16,28},{20,24},{24,20},{28,16},{1,13},{... | collective-permute-start | bytes 221192 | tf_op jit(solution)/shard_map/ppermute | solution.py:633
  34.5 11.1 %collective-permute-start.10 = (f32[72,256]{1,0:T(8,128)S(1)}, f32[72,256]{1,0:T(8,128)S(1)}, u32[]{:S(2)}, u32[]{:S(2)}) collective-permute-start(f32[72,256]{1,0:T(8,128)S(1)} %alike.8.refs_0_), channel_id=1, source_target_pairs={{0,8},{4,12},{8,0},{12,4},{16,24},{20,28},{24,16},{28,20},{1,9},{5... | collective-permute-start | bytes 221192 | tf_op jit(solution)/shard_map/ppermute | solution.py:633
  36.1 9.5 %collective-permute-start.9 = (f32[72,256]{1,0:T(8,128)S(1)}, f32[72,256]{1,0:T(8,128)S(1)}, u32[]{:S(2)}, u32[]{:S(2)}) collective-permute-start(f32[72,256]{1,0:T(8,128)S(1)} %alike.8.refs_0_), channel_id=1, source_target_pairs={{0,4},{4,0},{8,12},{12,8},{16,20},{20,16},{24,28},{28,24},{1,5},{5... | collective-permute-start | bytes 221192 | tf_op jit(solution)/shard_map/ppermute | solution.py:633
  45.8 13.8 %collective-permute-start.15 = (f32[576,128]{1,0:T(8,128)S(1)}, f32[576,128]{1,0:T(8,128)S(1)}, u32[]{:S(2)}, u32[]{:S(2)}) collective-permute-start(f32[576,128]{1,0:T(8,128)S(1)} %get-tuple-element.163), channel_id=1, source_target_pairs={{0,8},{8,16},{16,24},{24,28},{28,20},{20,12},{12,4},{4,0},{1,9},{9... | collective-permute-start | bytes 884744 | tf_op jit(solution)/shard_map/ppermute | solution.py:683
  46.1 13.5 %collective-permute-start.16 = (f32[576,128]{1,0:T(8,128)S(1)}, f32[576,128]{1,0:T(8,128)S(1)}, u32[]{:S(2)}, u32[]{:S(2)}) collective-permute-start(f32[576,128]{1,0:T(8,128)S(1)} %get-tuple-element.164), channel_id=1, source_target_pairs={{8,0},{16,8},{24,16},{28,24},{20,28},{12,20},{4,12},{0,4},{9,1},{1... | collective-permute-start | bytes 884744 | tf_op jit(solution)/shard_map/ppermute | solution.py:683
  47.9 9.8 %collective-permute-start.14 = (f32[72,256]{1,0:T(8,128)S(1)}, f32[72,256]{1,0:T(8,128)S(1)}, u32[]{:S(2)}, u32[]{:S(2)}) collective-permute-start(f32[72,256]{1,0:T(8,128)S(1)} %alike.9.refs_0_), channel_id=1, source_target_pairs={{0,16},{4,20},{8,24},{12,28},{16,0},{20,4},{24,8},{28,12},{1,17},{... | collective-permute-start | bytes 221192 | tf_op jit(solution)/shard_map/ppermute | solution.py:633
  59.7 10.5 %collective-permute-start.20 = (f32[576,128]{1,0:T(8,128)S(1)}, f32[576,128]{1,0:T(8,128)S(1)}, u32[]{:S(2)}, u32[]{:S(2)}) collective-permute-start(f32[576,128]{1,0:T(8,128)S(1)} %get-tuple-element.173), channel_id=1, source_target_pairs={{0,8},{8,16},{16,24},{24,28},{28,20},{20,12},{12,4},{4,0},{1,9},{9... | collective-permute-start | bytes 884744 | tf_op jit(solution)/shard_map/ppermute | solution.py:683
  59.7 10.4 %collective-permute-start.21 = (f32[576,128]{1,0:T(8,128)S(1)}, f32[576,128]{1,0:T(8,128)S(1)}, u32[]{:S(2)}, u32[]{:S(2)}) collective-permute-start(f32[576,128]{1,0:T(8,128)S(1)} %get-tuple-element.174), channel_id=1, source_target_pairs={{8,0},{16,8},{24,16},{28,24},{20,28},{12,20},{4,12},{0,4},{9,1},{1... | collective-permute-start | bytes 884744 | tf_op jit(solution)/shard_map/ppermute | solution.py:683
  70.3 9.1 %collective-permute-start.23 = (f32[576,128]{1,0:T(8,128)S(1)}, f32[576,128]{1,0:T(8,128)S(1)}, u32[]{:S(2)}, u32[]{:S(2)}) collective-permute-start(f32[576,128]{1,0:T(8,128)S(1)} %get-tuple-element.185), channel_id=1, source_target_pairs={{8,0},{16,8},{24,16},{28,24},{20,28},{12,20},{4,12},{0,4},{9,1},{1... | collective-permute-start | bytes 884744 | tf_op jit(solution)/shard_map/ppermute | solution.py:683
  96.9 13.3 %collective-permute-start.34 = (f32[544,128]{1,0:T(8,128)S(1)}, f32[544,128]{1,0:T(8,128)S(1)}, u32[]{:S(2)}, u32[]{:S(2)}) collective-permute-start(f32[544,128]{1,0:T(8,128)S(1)} %collective-permute-done.29.refs_1_), channel_id=1, source_target_pairs={{0,8},{8,16},{16,24},{24,28},{28,20},{20,12},{12,4},{4,0},{1,9},{9... | collective-permute-start | bytes 835592 | tf_op jit(solution)/shard_map/ppermute | solution.py:683
  98.1 12.1 %collective-permute-start.35 = (f32[544,128]{1,0:T(8,128)S(1)}, f32[544,128]{1,0:T(8,128)S(1)}, u32[]{:S(2)}, u32[]{:S(2)}) collective-permute-start(f32[544,128]{1,0:T(8,128)S(1)} %collective-permute-done.30.refs_11_.refs_13_), channel_id=1, source_target_pairs={{8,0},{16,8},{24,16},{28,24},{20,28},{12,20},{4,12},{0,4},{9,1},{1... | collective-permute-start | bytes 835592 | tf_op jit(solution)/shard_map/ppermute | solution.py:683
  98.9 10.4 %collective-permute-start.33 = (f32[80,256]{1,0:T(8,128)S(1)}, f32[80,256]{1,0:T(8,128)S(1)}, u32[]{:S(2)}, u32[]{:S(2)}) collective-permute-start(f32[80,256]{1,0:T(8,128)S(1)} %alike.11.refs_0_), channel_id=1, source_target_pairs={{0,12},{4,8},{8,4},{12,0},{16,28},{20,24},{24,20},{28,16},{1,13},{... | collective-permute-start | bytes 245768 | tf_op jit(solution)/shard_map/ppermute | solution.py:633
  110.2 14.2 %collective-permute-start.37 = (f32[544,128]{1,0:T(8,128)S(1)}, f32[544,128]{1,0:T(8,128)S(1)}, u32[]{:S(2)}, u32[]{:S(2)}) collective-permute-start(f32[544,128]{1,0:T(8,128)S(1)} %collective-permute-done.34.refs_2_), channel_id=1, source_target_pairs={{0,8},{8,16},{16,24},{24,28},{28,20},{20,12},{12,4},{4,0},{1,9},{9... | collective-permute-start | bytes 835592 | tf_op jit(solution)/shard_map/ppermute | solution.py:683
  111.4 13.0 %collective-permute-start.38 = (f32[544,128]{1,0:T(8,128)S(1)}, f32[544,128]{1,0:T(8,128)S(1)}, u32[]{:S(2)}, u32[]{:S(2)}) collective-permute-start(f32[544,128]{1,0:T(8,128)S(1)} %collective-permute-done.35.refs_10_.refs_12_), channel_id=1, source_target_pairs={{8,0},{16,8},{24,16},{28,24},{20,28},{12,20},{4,12},{0,4},{9,1},{1... | collective-permute-start | bytes 835592 | tf_op jit(solution)/shard_map/ppermute | solution.py:683
  112.3 10.1 %collective-permute-start.36 = (f32[80,256]{1,0:T(8,128)S(1)}, f32[80,256]{1,0:T(8,128)S(1)}, u32[]{:S(2)}, u32[]{:S(2)}) collective-permute-start(f32[80,256]{1,0:T(8,128)S(1)} %alike.12.refs_0_), channel_id=1, source_target_pairs={{0,16},{4,20},{8,24},{12,28},{16,0},{20,4},{24,8},{28,12},{1,17},{... | collective-permute-start | bytes 245768 | tf_op jit(solution)/shard_map/ppermute | solution.py:633
  124.4 9.8 %collective-permute-start.42 = (f32[544,128]{1,0:T(8,128)S(1)}, f32[544,128]{1,0:T(8,128)S(1)}, u32[]{:S(2)}, u32[]{:S(2)}) collective-permute-start(f32[544,128]{1,0:T(8,128)S(1)} %collective-permute-done.37.refs_3_), channel_id=1, source_target_pairs={{0,8},{8,16},{16,24},{24,28},{28,20},{20,12},{12,4},{4,0},{1,9},{9... | collective-permute-start | bytes 835592 | tf_op jit(solution)/shard_map/ppermute | solution.py:683
  124.4 9.8 %collective-permute-start.43 = (f32[544,128]{1,0:T(8,128)S(1)}, f32[544,128]{1,0:T(8,128)S(1)}, u32[]{:S(2)}, u32[]{:S(2)}) collective-permute-start(f32[544,128]{1,0:T(8,128)S(1)} %collective-permute-done.38.refs_9_.refs_11_), channel_id=1, source_target_pairs={{8,0},{16,8},{24,16},{28,24},{20,28},{12,20},{4,12},{0,4},{9,1},{1... | collective-permute-start | bytes 835592 | tf_op jit(solution)/shard_map/ppermute | solution.py:683
  134.2 9.2 %collective-permute-start.44 = (f32[544,128]{1,0:T(8,128)S(1)}, f32[544,128]{1,0:T(8,128)S(1)}, u32[]{:S(2)}, u32[]{:S(2)}) collective-permute-start(f32[544,128]{1,0:T(8,128)S(1)} %collective-permute-done.42.refs_4_), channel_id=1, source_target_pairs={{0,8},{8,16},{16,24},{24,28},{28,20},{20,12},{12,4},{4,0},{1,9},{9... | collective-permute-start | bytes 835592 | tf_op jit(solution)/shard_map/ppermute | solution.py:683
  134.2 9.2 %collective-permute-start.45 = (f32[544,128]{1,0:T(8,128)S(1)}, f32[544,128]{1,0:T(8,128)S(1)}, u32[]{:S(2)}, u32[]{:S(2)}) collective-permute-start(f32[544,128]{1,0:T(8,128)S(1)} %collective-permute-done.43.refs_8_.refs_10_), channel_id=1, source_target_pairs={{8,0},{16,8},{24,16},{28,24},{20,28},{12,20},{4,12},{0,4},{9,1},{1... | collective-permute-start | bytes 835592 | tf_op jit(solution)/shard_map/ppermute | solution.py:683
  143.4 10.3 %collective-permute-start.46 = (f32[544,128]{1,0:T(8,128)S(1)}, f32[544,128]{1,0:T(8,128)S(1)}, u32[]{:S(2)}, u32[]{:S(2)}) collective-permute-start(f32[544,128]{1,0:T(8,128)S(1)} %collective-permute-done.44.refs_5_), channel_id=1, source_target_pairs={{0,8},{8,16},{16,24},{24,28},{28,20},{20,12},{12,4},{4,0},{1,9},{9... | collective-permute-start | bytes 835592 | tf_op jit(solution)/shard_map/ppermute | solution.py:683
  143.6 10.1 %collective-permute-start.47 = (f32[544,128]{1,0:T(8,128)S(1)}, f32[544,128]{1,0:T(8,128)S(1)}, u32[]{:S(2)}, u32[]{:S(2)}) collective-permute-start(f32[544,128]{1,0:T(8,128)S(1)} %collective-permute-done.45.refs_7_.refs_9_), channel_id=1, source_target_pairs={{8,0},{16,8},{24,16},{28,24},{20,28},{12,20},{4,12},{0,4},{9,1},{1... | collective-permute-start | bytes 835592 | tf_op jit(solution)/shard_map/ppermute | solution.py:683
  (29 other events, 169.9 us)

commit v5 on v4

--- a/solution.py
+++ b/solution.py
@@ -306,32 +306,28 @@
     return out[0], out[1], out[2], out[3:]
 
 
-def ring_add_kernel(at_ref, up_ref, dn_ref, up_all, dn_all, up_out, dn_out):
-    up_out[...] = up_ref[...] + up_all[0]
-    dn_out[...] = dn_ref[...] + dn_all[0]
-
-
-def ring_add(place, step, up, dn, up_all, dn_all):
-    n = up_all.shape[0]
-    shape = jax.ShapeDtypeStruct(up.shape, F32)
+def ring_add_kernel(place_ref, x_ref, chunks_ref, out_ref):
+    out_ref[...] = x_ref[...] + chunks_ref[0]
+
+
+def ring_add(place, offset, x, chunks):
+    n = chunks.shape[0]
     return pl.pallas_call(
         ring_add_kernel,
-        out_shape=[shape, shape],
+        out_shape=jax.ShapeDtypeStruct(x.shape, F32),
         grid_spec=pltpu.PrefetchScalarGridSpec(
             num_scalar_prefetch=1,
             grid=(1,),
             in_specs=[
-                whole(up.shape),
-                whole(dn.shape),
-                pl.BlockSpec((1,) + up.shape, lambda i, at: (lax.rem(at[0] + n - 1 - step, n), 0, 0)),
-                pl.BlockSpec((1,) + dn.shape, lambda i, at: (lax.rem(at[0] + 1 + step, n), 0, 0)),
+                whole(x.shape),
+                pl.BlockSpec((1,) + x.shape, lambda i, place: (lax.rem(place[0] + offset, n), 0, 0)),
             ],
-            out_specs=[whole(up.shape), whole(dn.shape)],
+            out_specs=whole(x.shape),
         ),
-        cost_estimate=cost(2 * up.size, 24 * up.size),
-        compiler_params=grant(8),
+        cost_estimate=cost(x.size, 12 * x.size),
+        compiler_params=grant(6),
         name="ring_add",
-    )(place, up, dn, up_all, dn_all)
+    )(place, x, chunks)
 
 
 def alike_kernel(*refs):
@@ -466,7 +462,9 @@
 
 
 def add_squares(k, y, out):
-    squares = dot(jnp.ones((8, y.shape[1]), F32), y * y, 1, 1)
+    ones = jnp.ones((8, y.shape[1]), BF16)
+    high, low = [lax.dot_general(ones, part, (((1,), (1,)), ((), ())), preferred_element_type=F32) for part in halves(y * y)]
+    squares = high + low
 
     @pl.when(k == 0)
     def _():
@@ -680,7 +678,9 @@
         return tied[1]
 
     def step(up, dn):
-        return lax.ppermute(up, "rep", ahead), lax.ppermute(dn, "rep", back)
+        up = lax.ppermute(up, "rep", ahead)
+        dn = lax.ppermute(dn, "rep", back)
+        return up, dn
 
     def first(scaled):
         def stage():
@@ -709,9 +709,10 @@
         if work:
             for stage in work.pop(0):
                 stage()
-            up, dn = tie(box, up, dn)
+            (up,) = tie(box, up)
         if k < n - 1:
-            up, dn = ring_add(place, k, up, dn, box["up_all"], box["dn_all"])
+            up = ring_add(place, n - 1 - k, up, box["up_all"])
+            dn = ring_add(place, 1 + k, dn, box["dn_all"])
     l1 = box["left"]
     both = box["both"]
     up, dn = reduced(place, up, dn, box["up_all"], box["dn_all"], l1, box["leftt"], n)
@@ -749,11 +750,11 @@
         if work:
             for stage in work.pop(0):
                 stage()
-            up, dn = tie(box, up, dn)
+            (up,) = tie(box, up)
         else:
             box.setdefault("both", both)
             advance_ready()
-            up, dn = tie(box, up, dn)
+            (up,) = tie(box, up)
         ups.append(up)
         dns.append(dn)
     box.setdefault("both", both)

time: 167 us -> 166 us (level)
  waiting for transfers between devices: 62.8 us -> 59.9 us
    ppermute x28, waiting for transfers between devices: 18 us -> 15.6 us  [the longest x14 15.3 us: step(): up = lax.ppermute(up, 'rep', ahead)]
  transfers between devices with their start and end apart: 51 -> 51, of which waited for: 25 -> 19; matrix products, arithmetic and copies ran while one was open for 0% -> 0% of each run, Pallas kernels for 25% -> 26%
where the time goes in v5:
time: 166 us; the launch traced here: 165 us
  waiting for transfers between devices  59.9 us (36%)
  Pallas kernels  53.3 us (32%)
  starting transfers between devices  50.9 us (31%)
    ppermute x23, waiting for transfers between devices, flip(): return lax.ppermute(x, axis, [(i, i ^ bits) for i in range(size)])  44.2 us
    ppermute x23, starting transfers between devices, flip(): return lax.ppermute(x, axis, [(i, i ^ bits) for i in range(size)])  20.5 us
    ppermute x14, starting transfers between devices, step(): dn = lax.ppermute(dn, 'rep', back)  18.8 us
    ppermute x14, waiting for transfers between devices, step(): up = lax.ppermute(up, 'rep', ahead)  15.3 us
    pallas_call x3, Pallas kernels, advance(): pl.pallas_call(functools.partial(kernel, m), out_shape=outs, grid_spec=pl...  13.1 us
    pallas_call x2, Pallas kernels, orth_first(): pl.pallas_call(functools.partial(first_kernel, scaled), out_shape=shapes,...  12.5 us
    ppermute x14, starting transfers between devices, step(): up = lax.ppermute(up, 'rep', ahead)  11.6 us
    pallas_call x2, Pallas kernels, orth_second(): pl.pallas_call(second_kernel, out_shape=[jax.ShapeDtypeStruct((rows, rank...  11 us
  transfers between devices with their start and end apart: 51, of which 19 were waited for; matrix products, arithmetic and copies ran while one was open for 0% of the time, Pallas kernels for 26%

profile of v5, /device:TPU:0, one launch (start us, length us, event | category | flops | bytes accessed | tf_op | source)
XLA Modules:
  0.0 165.3 jit_solution(17074038467903184416)
XLA Ops:
  0.7 2.1 %lead.1 = (f32[576,128]{1,0:T(8,128)}, f32[576,128]{1,0:T(8,128)}) custom-call(s32[1]{0:T(128)} %bitcast.place_ref.at_ref.order_ref, f32[1,288,2048]{2,1,0:T(8,128)} %mom.1, bf16[2,1,288,2048]{3,2,1,0:T(8,128)(2,1)} %grads.1), custom_call_target="tpu_custom_call" | custom-call | flops 147456 | bytes 1179648 | tf_op jit(solution)/shard_map/lead/pallas_call | solution.py:230
  2.8 3.1 %collective-permute-start = (f32[576,128]{1,0:T(8,128)}, f32[576,128]{1,0:T(8,128)S(1)}, u32[]{:S(2)}, u32[]{:S(2)}) collective-permute-start(f32[576,128]{1,0:T(8,128)} %get-tuple-element.102), channel_id=1, source_target_pairs={{0,8},{8,16},{16,24},{24,28},{28,20},{20,12},{12,4},{4,0},{1,9},{9... | collective-permute-start | bytes 884744 | tf_op jit(solution)/shard_map/ppermute | solution.py:681
  5.9 6.2 %combine.1 = (f32[8,576,128]{2,1,0:T(8,128)S(1)}, f32[8,576,128]{2,1,0:T(8,128)S(1)}, f32[1,288,2048]{2,1,0:T(8,128)}, f32[72,256]{1,0:T(8,128)S(1)}, f32[72,256...) custom-call(s32[1]{0:T(128)} %bitcast.1.me_ref, f32[1,288,2048]{2,1,0:T(8,128)} %mom.1, ...), custom_call_target="tpu_custom_call" | custom-call | flops 1811939328 | bytes 16515072 | tf_op jit(solution)/shard_map/combine/pallas_call | solution.py:285
  15.3 6.0 %collective-permute-done.1.x_ref = f32[576,128]{1,0:T(8,128)S(1)} collective-permute-done((f32[576,128]{1,0:T(8,128)S(1)}, f32[576,128]{1,0:T(8,128)S(1)}, u32[]{:S(2)}, u32[]{:S(2)}) %collective-permute-start.1) | collective-permute-done | bytes 294944 | tf_op jit(solution)/shard_map/ppermute | solution.py:681
  25.4 3.1 %collective-permute-done.3.refs_2_ = f32[72,256]{1,0:T(8,128)S(1)} collective-permute-done((f32[72,256]{1,0:T(8,128)S(1)}, f32[72,256]{1,0:T(8,128)S(1)}, u32[]{:S(2)}, u32[]{:S(2)}) %collective-permute-start.3) | collective-permute-done | bytes 73760 | tf_op jit(solution)/shard_map/ppermute | solution.py:631
  31.8 2.5 %collective-permute-start.8 = (f32[72,256]{1,0:T(8,128)S(1)}, f32[72,256]{1,0:T(8,128)S(1)}, u32[]{:S(2)}, u32[]{:S(2)}) collective-permute-start(f32[72,256]{1,0:T(8,128)S(1)} %alike.8.refs_0_), channel_id=1, source_target_pairs={{0,12},{4,8},{8,4},{12,0},{16,28},{20,24},{24,20},{28,16},{1,13},{... | collective-permute-start | bytes 221192 | tf_op jit(solution)/shard_map/ppermute | solution.py:631
  35.3 6.8 %collective-permute-done.8.refs_3_ = f32[72,256]{1,0:T(8,128)S(1)} collective-permute-done((f32[72,256]{1,0:T(8,128)S(1)}, f32[72,256]{1,0:T(8,128)S(1)}, u32[]{:S(2)}, u32[]{:S(2)}) %collective-permute-start.8) | collective-permute-done | bytes 73760 | tf_op jit(solution)/shard_map/ppermute | solution.py:631
  45.7 2.6 %collective-permute-start.10 = (f32[72,256]{1,0:T(8,128)S(1)}, f32[72,256]{1,0:T(8,128)S(1)}, u32[]{:S(2)}, u32[]{:S(2)}) collective-permute-start(f32[72,256]{1,0:T(8,128)S(1)} %alike.9.refs_0_), channel_id=1, source_target_pairs={{0,16},{4,20},{8,24},{12,28},{16,0},{20,4},{24,8},{28,12},{1,17},{... | collective-permute-start | bytes 221192 | tf_op jit(solution)/shard_map/ppermute | solution.py:631
  48.3 8.6 %collective-permute-done.10.refs_1_ = f32[72,256]{1,0:T(8,128)S(1)} collective-permute-done((f32[72,256]{1,0:T(8,128)S(1)}, f32[72,256]{1,0:T(8,128)S(1)}, u32[]{:S(2)}, u32[]{:S(2)}) %collective-permute-start.10) | collective-permute-done | bytes 73760 | tf_op jit(solution)/shard_map/ppermute | solution.py:631
  57.0 2.1 %collective-permute-start.13 = (f32[72,256]{1,0:T(8,128)S(1)}, f32[72,256]{1,0:T(8,128)S(1)}, u32[]{:S(2)}, u32[]{:S(2)}) collective-permute-start(f32[72,256]{1,0:T(8,128)S(1)} %alike.10.refs_0_), channel_id=1, source_target_pairs={{0,2},{1,3},{2,0},{3,1},{4,6},{5,7},{6,4},{7,5},{8,10},{9,11},{10,... | collective-permute-start | bytes 221192 | tf_op jit(solution)/shard_map/ppermute | solution.py:631
  59.3 2.0 %collective-permute-start.22 = (f32[576,128]{1,0:T(8,128)S(1)}, f32[576,128]{1,0:T(8,128)S(1)}, u32[]{:S(2)}, u32[]{:S(2)}) collective-permute-start(f32[576,128]{1,0:T(8,128)S(1)} %ring_add.22), channel_id=1, source_target_pairs={{8,0},{16,8},{24,16},{28,24},{20,28},{12,20},{4,12},{0,4},{9,1},{1... | collective-permute-start | bytes 884744 | tf_op jit(solution)/shard_map/ppermute | solution.py:682
  63.0 6.2 %orth_first.2 = (f32[288,128]{1,0:T(8,128)S(1)}, f32[288,128]{1,0:T(8,128)S(1)}) custom-call(s32[1]{0:T(128)} %bitcast.1.me_ref, f32[72,256]{1,0:T(8,128)S(1)} %alike.10.refs_0_, f32[72,256]{1,0:T(8,128)S(1)} %collective-permute-done.12.refs_1_, f32[72,256]{1,0:T(8,128)S(1)} %collective-permute-done.13.refs_2_, f32[72,256]{1,0:T(8,128)S(1)} %collective-permute-done.14.refs_3_), custom_call_target="tpu_custom_call" | custom-call | flops 6000000000 | bytes 1000000 | tf_op jit(solution)/shard_map/orth_first/pallas_call | solution.py:173
  69.4 2.2 %collective-permute-start.23 = (f32[576,128]{1,0:T(8,128)S(1)}, f32[576,128]{1,0:T(8,128)S(1)}, u32[]{:S(2)}, u32[]{:S(2)}) collective-permute-start(f32[576,128]{1,0:T(8,128)S(1)} %ring_add.23), channel_id=1, source_target_pairs={{8,0},{16,8},{24,16},{28,24},{20,28},{12,20},{4,12},{0,4},{9,1},{1... | collective-permute-start | bytes 884744 | tf_op jit(solution)/shard_map/ppermute | solution.py:682
  71.6 5.5 %orth_second.2 = (f32[288,256]{1,0:T(8,128)S(1)}, f32[256,288]{1,0:T(8,128)S(1)}) custom-call(f32[288,128]{1,0:T(8,128)S(1)} %get-tuple-element.136.left_ref, f32[288,128]{1,0:T(8,128)S(1)} %get-tuple-element.137.rest_ref), custom_call_target="tpu_custom_call" | custom-call | flops 6000000000 | bytes 1000000 | tf_op jit(solution)/shard_map/orth_second/pallas_call | solution.py:187
  83.0 5.3 %collective-permute-done.24.refs_0_.refs_6_ = f32[544,128]{1,0:T(8,128)S(1)} collective-permute-done((f32[544,128]{1,0:T(8,128)S(1)}, f32[544,128]{1,0:T(8,128)S(1)}, u32[]{:S(2)}, u32[]{:S(2)}) %collective-permute-start.24) | collective-permute-done | bytes 278560 | tf_op jit(solution)/shard_map/ppermute | solution.py:681
  92.2 3.5 %collective-permute-done.26.refs_2_ = f32[80,256]{1,0:T(8,128)S(1)} collective-permute-done((f32[80,256]{1,0:T(8,128)S(1)}, f32[80,256]{1,0:T(8,128)S(1)}, u32[]{:S(2)}, u32[]{:S(2)}) %collective-permute-start.26) | collective-permute-done | bytes 81952 | tf_op jit(solution)/shard_map/ppermute | solution.py:631
  102.1 6.6 %collective-permute-done.31.refs_3_ = f32[80,256]{1,0:T(8,128)S(1)} collective-permute-done((f32[80,256]{1,0:T(8,128)S(1)}, f32[80,256]{1,0:T(8,128)S(1)}, u32[]{:S(2)}, u32[]{:S(2)}) %collective-permute-start.31) | collective-permute-done | bytes 81952 | tf_op jit(solution)/shard_map/ppermute | solution.py:631
  112.3 8.6 %collective-permute-done.33.refs_1_ = f32[80,256]{1,0:T(8,128)S(1)} collective-permute-done((f32[80,256]{1,0:T(8,128)S(1)}, f32[80,256]{1,0:T(8,128)S(1)}, u32[]{:S(2)}, u32[]{:S(2)}) %collective-permute-start.33) | collective-permute-done | bytes 81952 | tf_op jit(solution)/shard_map/ppermute | solution.py:631
  122.8 2.0 %collective-permute-start.44 = (f32[544,128]{1,0:T(8,128)S(1)}, f32[544,128]{1,0:T(8,128)S(1)}, u32[]{:S(2)}, u32[]{:S(2)}) collective-permute-start(f32[544,128]{1,0:T(8,128)S(1)} %collective-permute-done.43.refs_9_.refs_11_), channel_id=1, source_target_pairs={{8,0},{16,8},{24,16},{28,24},{20,28},{12,20},{4,12},{0,4},{9,1},{1... | collective-permute-start | bytes 835592 | tf_op jit(solution)/shard_map/ppermute | solution.py:682
  126.8 6.3 %orth_first.3 = (f32[288,128]{1,0:T(8,128)S(1)}, f32[288,128]{1,0:T(8,128)S(1)}, f32[1,256]{1,0:T(1,128)S(1)}) custom-call(s32[1]{0:T(128)} %bitcast.1.me_ref, f32[80,256]{1,0:T(8,128)S(1)} %alike.13.refs_0_, f32[80,256]{1,0:T(8,128)S(1)} %collective-permute-done.35.refs_1_, f32[80,256]{1,0:T(8,128)S(1)} %collective-permute-done.36.refs_2_, ...), custom_call_target="tpu_custom_call" | custom-call | flops 6000000000 | bytes 1000000 | tf_op jit(solution)/shard_map/orth_first/pallas_call | solution.py:173
  135.1 5.5 %orth_second.3 = (f32[288,256]{1,0:T(8,128)S(1)}, f32[256,288]{1,0:T(8,128)S(1)}) custom-call(f32[288,128]{1,0:T(8,128)S(1)} %get-tuple-element.166.left_ref, f32[288,128]{1,0:T(8,128)S(1)} %get-tuple-element.167.rest_ref), custom_call_target="tpu_custom_call" | custom-call | flops 6000000000 | bytes 1000000 | tf_op jit(solution)/shard_map/orth_second/pallas_call | solution.py:187
  144.2 8.8 %shard_map.67 = (f32[1,288,2048]{2,1,0:T(8,128)}, f32[6,256,256]{2,1,0:T(8,128)S(1)}, f32[8,256]{1,0:T(8,128)S(1)}) custom-call(s32[1]{0:T(128)} %bitcast.place_ref.at_ref.order_ref, f32[544,128]{1,0:T(8,128)S(1)} %get-tuple-element.147.up_ref.refs_0_, f32[544,128]{1,0:T(8,128)S(1)} %collective-permute-done.28.refs_1_, ...), custom_call_target="tpu_custom_call", output_to_operand_aliasing={{0}: (13, {})} | custom-call | flops 2264924160 | bytes 10616832 | tf_op jit(solution)/shard_map/pallas_call | solution.py:550
  156.3 2.9 %shard_map.69 = f32[1,288,2048]{2,1,0:T(8,128)} custom-call(s32[1]{0:T(128)} %bitcast.place_ref.at_ref.order_ref, f32[544,128]{1,0:T(8,128)S(1)} %collective-permute-done.24.refs_0_.refs_6_, f32[544,128]{1,0:T(8,128)S(1)} %collective-permute-done.46.refs_1_.refs_7_, ...), custom_call_target="tpu_custom_call", output_to_operand_aliasing={{}: (5, {})} | custom-call | flops 754974720 | bytes 3538944 | tf_op jit(solution)/shard_map/pallas_call | solution.py:550
  159.3 5.8 %finish.1 = (f32[288,2048]{1,0:T(8,128)}, f32[2048,256]{1,0:T(8,128)}) custom-call(s32[1]{0:T(128)} %bitcast.place_ref.at_ref.order_ref, f32[544,128]{1,0:T(8,128)S(1)} %get-tuple-element.147.up_ref.refs_0_, f32[544,128]{1,0:T(8,128)S(1)} %collective-permute-done.28.refs_1_, f32[544,128]{1,0:T(8,128)S(1)} %collective-permute-done.32.refs_2_, ...), custom_call_target="tpu_custom_call" | custom-call | flops 1811939328 | bytes 18874368 | tf_op jit(solution)/shard_map/finish/pallas_call | solution.py:600
  (114 shorter events, 49.5 us)
Async XLA Ops:
  2.8 10.3 %collective-permute-start = (f32[576,128]{1,0:T(8,128)}, f32[576,128]{1,0:T(8,128)S(1)}, u32[]{:S(2)}, u32[]{:S(2)}) collective-permute-start(f32[576,128]{1,0:T(8,128)} %get-tuple-element.102), channel_id=1, source_target_pairs={{0,8},{8,16},{16,24},{24,28},{28,20},{20,12},{12,4},{4,0},{1,9},{9... | collective-permute-start | bytes 884744 | tf_op jit(solution)/shard_map/ppermute | solution.py:681
  29.6 13.9 %collective-permute-start.9 = (f32[576,128]{1,0:T(8,128)S(1)}, f32[576,128]{1,0:T(8,128)S(1)}, u32[]{:S(2)}, u32[]{:S(2)}) collective-permute-start(f32[576,128]{1,0:T(8,128)S(1)} %ring_add.14), channel_id=1, source_target_pairs={{0,8},{8,16},{16,24},{24,28},{28,20},{20,12},{12,4},{4,0},{1,9},{9... | collective-permute-start | bytes 884744 | tf_op jit(solution)/shard_map/ppermute | solution.py:681
  31.3 12.7 %collective-permute-start.20 = (f32[576,128]{1,0:T(8,128)S(1)}, f32[576,128]{1,0:T(8,128)S(1)}, u32[]{:S(2)}, u32[]{:S(2)}) collective-permute-start(f32[576,128]{1,0:T(8,128)S(1)} %ring_add.20), channel_id=1, source_target_pairs={{8,0},{16,8},{24,16},{28,24},{20,28},{12,20},{4,12},{0,4},{9,1},{1... | collective-permute-start | bytes 884744 | tf_op jit(solution)/shard_map/ppermute | solution.py:682
  31.8 10.3 %collective-permute-start.8 = (f32[72,256]{1,0:T(8,128)S(1)}, f32[72,256]{1,0:T(8,128)S(1)}, u32[]{:S(2)}, u32[]{:S(2)}) collective-permute-start(f32[72,256]{1,0:T(8,128)S(1)} %alike.8.refs_0_), channel_id=1, source_target_pairs={{0,12},{4,8},{8,4},{12,0},{16,28},{20,24},{24,20},{28,16},{1,13},{... | collective-permute-start | bytes 221192 | tf_op jit(solution)/shard_map/ppermute | solution.py:631
  34.3 9.1 %collective-permute-start.7 = (f32[72,256]{1,0:T(8,128)S(1)}, f32[72,256]{1,0:T(8,128)S(1)}, u32[]{:S(2)}, u32[]{:S(2)}) collective-permute-start(f32[72,256]{1,0:T(8,128)S(1)} %alike.8.refs_0_), channel_id=1, source_target_pairs={{0,8},{4,12},{8,0},{12,4},{16,24},{20,28},{24,16},{28,20},{1,9},{5... | collective-permute-start | bytes 221192 | tf_op jit(solution)/shard_map/ppermute | solution.py:631
  43.5 15.6 %collective-permute-start.11 = (f32[576,128]{1,0:T(8,128)S(1)}, f32[576,128]{1,0:T(8,128)S(1)}, u32[]{:S(2)}, u32[]{:S(2)}) collective-permute-start(f32[576,128]{1,0:T(8,128)S(1)} %ring_add.15), channel_id=1, source_target_pairs={{0,8},{8,16},{16,24},{24,28},{28,20},{20,12},{12,4},{4,0},{1,9},{9... | collective-permute-start | bytes 884744 | tf_op jit(solution)/shard_map/ppermute | solution.py:681
  44.0 15.2 %collective-permute-start.21 = (f32[576,128]{1,0:T(8,128)S(1)}, f32[576,128]{1,0:T(8,128)S(1)}, u32[]{:S(2)}, u32[]{:S(2)}) collective-permute-start(f32[576,128]{1,0:T(8,128)S(1)} %ring_add.21), channel_id=1, source_target_pairs={{8,0},{16,8},{24,16},{28,24},{20,28},{12,20},{4,12},{0,4},{9,1},{1... | collective-permute-start | bytes 884744 | tf_op jit(solution)/shard_map/ppermute | solution.py:682
  45.7 11.2 %collective-permute-start.10 = (f32[72,256]{1,0:T(8,128)S(1)}, f32[72,256]{1,0:T(8,128)S(1)}, u32[]{:S(2)}, u32[]{:S(2)}) collective-permute-start(f32[72,256]{1,0:T(8,128)S(1)} %alike.9.refs_0_), channel_id=1, source_target_pairs={{0,16},{4,20},{8,24},{12,28},{16,0},{20,4},{24,8},{28,12},{1,17},{... | collective-permute-start | bytes 221192 | tf_op jit(solution)/shard_map/ppermute | solution.py:631
  59.2 10.0 %collective-permute-start.15 = (f32[576,128]{1,0:T(8,128)S(1)}, f32[576,128]{1,0:T(8,128)S(1)}, u32[]{:S(2)}, u32[]{:S(2)}) collective-permute-start(f32[576,128]{1,0:T(8,128)S(1)} %ring_add.16), channel_id=1, source_target_pairs={{0,8},{8,16},{16,24},{24,28},{28,20},{20,12},{12,4},{4,0},{1,9},{9... | collective-permute-start | bytes 884744 | tf_op jit(solution)/shard_map/ppermute | solution.py:681
  59.3 10.0 %collective-permute-start.22 = (f32[576,128]{1,0:T(8,128)S(1)}, f32[576,128]{1,0:T(8,128)S(1)}, u32[]{:S(2)}, u32[]{:S(2)}) collective-permute-start(f32[576,128]{1,0:T(8,128)S(1)} %ring_add.22), channel_id=1, source_target_pairs={{8,0},{16,8},{24,16},{28,24},{20,28},{12,20},{4,12},{0,4},{9,1},{1... | collective-permute-start | bytes 884744 | tf_op jit(solution)/shard_map/ppermute | solution.py:682
  69.3 9.3 %collective-permute-start.16 = (f32[576,128]{1,0:T(8,128)S(1)}, f32[576,128]{1,0:T(8,128)S(1)}, u32[]{:S(2)}, u32[]{:S(2)}) collective-permute-start(f32[576,128]{1,0:T(8,128)S(1)} %ring_add.17), channel_id=1, source_target_pairs={{0,8},{8,16},{16,24},{24,28},{28,20},{20,12},{12,4},{4,0},{1,9},{9... | collective-permute-start | bytes 884744 | tf_op jit(solution)/shard_map/ppermute | solution.py:681
  69.4 9.4 %collective-permute-start.23 = (f32[576,128]{1,0:T(8,128)S(1)}, f32[576,128]{1,0:T(8,128)S(1)}, u32[]{:S(2)}, u32[]{:S(2)}) collective-permute-start(f32[576,128]{1,0:T(8,128)S(1)} %ring_add.23), channel_id=1, source_target_pairs={{8,0},{16,8},{24,16},{28,24},{20,28},{12,20},{4,12},{0,4},{9,1},{1... | collective-permute-start | bytes 884744 | tf_op jit(solution)/shard_map/ppermute | solution.py:682
  96.5 12.5 %collective-permute-start.32 = (f32[544,128]{1,0:T(8,128)S(1)}, f32[544,128]{1,0:T(8,128)S(1)}, u32[]{:S(2)}, u32[]{:S(2)}) collective-permute-start(f32[544,128]{1,0:T(8,128)S(1)} %collective-permute-done.28.refs_1_), channel_id=1, source_target_pairs={{0,8},{8,16},{16,24},{24,28},{28,20},{20,12},{12,4},{4,0},{1,9},{9... | collective-permute-start | bytes 835592 | tf_op jit(solution)/shard_map/ppermute | solution.py:681
  96.9 13.9 %collective-permute-start.42 = (f32[544,128]{1,0:T(8,128)S(1)}, f32[544,128]{1,0:T(8,128)S(1)}, u32[]{:S(2)}, u32[]{:S(2)}) collective-permute-start(f32[544,128]{1,0:T(8,128)S(1)} %collective-permute-done.41.refs_11_.refs_13_), channel_id=1, source_target_pairs={{8,0},{16,8},{24,16},{28,24},{20,28},{12,20},{4,12},{0,4},{9,1},{1... | collective-permute-start | bytes 835592 | tf_op jit(solution)/shard_map/ppermute | solution.py:682
  98.6 10.1 %collective-permute-start.31 = (f32[80,256]{1,0:T(8,128)S(1)}, f32[80,256]{1,0:T(8,128)S(1)}, u32[]{:S(2)}, u32[]{:S(2)}) collective-permute-start(f32[80,256]{1,0:T(8,128)S(1)} %alike.11.refs_0_), channel_id=1, source_target_pairs={{0,12},{4,8},{8,4},{12,0},{16,28},{20,24},{24,20},{28,16},{1,13},{... | collective-permute-start | bytes 245768 | tf_op jit(solution)/shard_map/ppermute | solution.py:631
  109.1 13.8 %collective-permute-start.34 = (f32[544,128]{1,0:T(8,128)S(1)}, f32[544,128]{1,0:T(8,128)S(1)}, u32[]{:S(2)}, u32[]{:S(2)}) collective-permute-start(f32[544,128]{1,0:T(8,128)S(1)} %collective-permute-done.32.refs_2_), channel_id=1, source_target_pairs={{0,8},{8,16},{16,24},{24,28},{28,20},{20,12},{12,4},{4,0},{1,9},{9... | collective-permute-start | bytes 835592 | tf_op jit(solution)/shard_map/ppermute | solution.py:681
  110.8 12.1 %collective-permute-start.43 = (f32[544,128]{1,0:T(8,128)S(1)}, f32[544,128]{1,0:T(8,128)S(1)}, u32[]{:S(2)}, u32[]{:S(2)}) collective-permute-start(f32[544,128]{1,0:T(8,128)S(1)} %collective-permute-done.42.refs_10_.refs_12_), channel_id=1, source_target_pairs={{8,0},{16,8},{24,16},{28,24},{20,28},{12,20},{4,12},{0,4},{9,1},{1... | collective-permute-start | bytes 835592 | tf_op jit(solution)/shard_map/ppermute | solution.py:682
  111.1 9.7 %collective-permute-start.33 = (f32[80,256]{1,0:T(8,128)S(1)}, f32[80,256]{1,0:T(8,128)S(1)}, u32[]{:S(2)}, u32[]{:S(2)}) collective-permute-start(f32[80,256]{1,0:T(8,128)S(1)} %alike.12.refs_0_), channel_id=1, source_target_pairs={{0,16},{4,20},{8,24},{12,28},{16,0},{20,4},{24,8},{28,12},{1,17},{... | collective-permute-start | bytes 245768 | tf_op jit(solution)/shard_map/ppermute | solution.py:631
  122.8 10.2 %collective-permute-start.38 = (f32[544,128]{1,0:T(8,128)S(1)}, f32[544,128]{1,0:T(8,128)S(1)}, u32[]{:S(2)}, u32[]{:S(2)}) collective-permute-start(f32[544,128]{1,0:T(8,128)S(1)} %collective-permute-done.34.refs_3_), channel_id=1, source_target_pairs={{0,8},{8,16},{16,24},{24,28},{28,20},{20,12},{12,4},{4,0},{1,9},{9... | collective-permute-start | bytes 835592 | tf_op jit(solution)/shard_map/ppermute | solution.py:681
  122.8 10.3 %collective-permute-start.44 = (f32[544,128]{1,0:T(8,128)S(1)}, f32[544,128]{1,0:T(8,128)S(1)}, u32[]{:S(2)}, u32[]{:S(2)}) collective-permute-start(f32[544,128]{1,0:T(8,128)S(1)} %collective-permute-done.43.refs_9_.refs_11_), channel_id=1, source_target_pairs={{8,0},{16,8},{24,16},{28,24},{20,28},{12,20},{4,12},{0,4},{9,1},{1... | collective-permute-start | bytes 835592 | tf_op jit(solution)/shard_map/ppermute | solution.py:682
  133.1 9.1 %collective-permute-start.39 = (f32[544,128]{1,0:T(8,128)S(1)}, f32[544,128]{1,0:T(8,128)S(1)}, u32[]{:S(2)}, u32[]{:S(2)}) collective-permute-start(f32[544,128]{1,0:T(8,128)S(1)} %collective-permute-done.38.refs_4_), channel_id=1, source_target_pairs={{0,8},{8,16},{16,24},{24,28},{28,20},{20,12},{12,4},{4,0},{1,9},{9... | collective-permute-start | bytes 835592 | tf_op jit(solution)/shard_map/ppermute | solution.py:681
  133.1 9.3 %collective-permute-start.45 = (f32[544,128]{1,0:T(8,128)S(1)}, f32[544,128]{1,0:T(8,128)S(1)}, u32[]{:S(2)}, u32[]{:S(2)}) collective-permute-start(f32[544,128]{1,0:T(8,128)S(1)} %collective-permute-done.44.refs_8_.refs_10_), channel_id=1, source_target_pairs={{8,0},{16,8},{24,16},{28,24},{20,28},{12,20},{4,12},{0,4},{9,1},{1... | collective-permute-start | bytes 835592 | tf_op jit(solution)/shard_map/ppermute | solution.py:682
  142.1 10.8 %collective-permute-start.46 = (f32[544,128]{1,0:T(8,128)S(1)}, f32[544,128]{1,0:T(8,128)S(1)}, u32[]{:S(2)}, u32[]{:S(2)}) collective-permute-start(f32[544,128]{1,0:T(8,128)S(1)} %collective-permute-done.39.refs_5_), channel_id=1, source_target_pairs={{0,8},{8,16},{16,24},{24,28},{28,20},{20,12},{12,4},{4,0},{1,9},{9... | collective-permute-start | bytes 835592 | tf_op jit(solution)/shard_map/ppermute | solution.py:681
  142.4 10.6 %collective-permute-start.47 = (f32[544,128]{1,0:T(8,128)S(1)}, f32[544,128]{1,0:T(8,128)S(1)}, u32[]{:S(2)}, u32[]{:S(2)}) collective-permute-start(f32[544,128]{1,0:T(8,128)S(1)} %collective-permute-done.45.refs_7_.refs_9_), channel_id=1, source_target_pairs={{8,0},{16,8},{24,16},{28,24},{20,28},{12,20},{4,12},{0,4},{9,1},{1... | collective-permute-start | bytes 835592 | tf_op jit(solution)/shard_map/ppermute | solution.py:682
  (29 other events, 174.4 us)

commit v6 on v5

--- a/solution.py
+++ b/solution.py
@@ -34,11 +34,14 @@
     return high, (x - high.astype(F32)).astype(BF16)
 
 
-def dot3(a, b, ca=1, cb=0):
-    def one(x, y):
-        return lax.dot_general(x, y, (((ca,), (cb,)), ((), ())), preferred_element_type=F32)
-
-    return one(a[0], b[0]) + (one(a[0], b[1]) + one(a[1], b[0]))
+def stacked(x):
+    return jnp.concatenate(halves(x), axis=0)
+
+
+def dot3(a, b):
+    m = a.shape[0] // 2
+    top = jnp.dot(a, b[0], preferred_element_type=F32)
+    return top[:m] + (top[m:] + jnp.dot(a[:m], b[1], preferred_element_type=F32))
 
 
 def grant(mib):
@@ -442,55 +445,58 @@
 
 def advance_kernel(m, order_ref, *refs):
     ups, dns = refs[:m], refs[m : 2 * m]
-    both_ref, l1_ref, l2_ref, l2t_ref, mom_out, y_out, sq_out, buf, sem, project, update = refs[2 * m :]
+    both_ref, l1_ref, l2_ref, l2t_ref, mom_out, y_out, sq_out, buf, sem, project, update, acc = refs[2 * m :]
     k = pl.program_id(0)
     rank = l2t_ref.shape[0]
     w = buf.shape[2] // 2
 
     @pl.when(k == 0)
     def _():
-        project[0], project[1] = halves(l2t_ref[...])
-        update[0], update[1] = halves(DAMPING * jnp.concatenate([l1_ref[...], l2_ref[...]], axis=1))
+        project[...] = stacked(l2t_ref[...])
+        update[...] = stacked(DAMPING * jnp.concatenate([l1_ref[...], l2_ref[...]], axis=1))
 
     chunk = fetcher([[(ups[i], 0, 0), (dns[i], 0, w)] for i in range(m)], buf, sem)
     y1, averaged = chunk[:rank], chunk[rank:]
-    y2 = dot3((project[0], project[1]), halves(averaged))
+    y2 = dot3(project[...], halves(averaged))
     y_out[0] = y2
     y = halves(jnp.concatenate([y1, y2], axis=0))
-    mom_out[0] = both_ref[0] - dot3((update[0], update[1]), y)
-    add_squares(k, y2, sq_out)
-
-
-def add_squares(k, y, out):
-    ones = jnp.ones((8, y.shape[1]), BF16)
-    high, low = [lax.dot_general(ones, part, (((1,), (1,)), ((), ())), preferred_element_type=F32) for part in halves(y * y)]
-    squares = high + low
+    mom_out[0] = both_ref[0] - dot3(update[...], y)
+    add_squares(k, m, y2, acc, sq_out)
+
+
+def add_squares(k, m, y, acc, out):
+    ones = jnp.ones((y.shape[1], LANES), BF16)
+    high, low = [jnp.dot(part, ones, preferred_element_type=F32) for part in halves(y * y)]
 
     @pl.when(k == 0)
     def _():
-        out[...] = squares
+        acc[...] = high + low
 
     @pl.when(k > 0)
     def _():
-        out[...] += squares
+        acc[...] += high + low
+
+    @pl.when(k == m - 1)
+    def _():
+        out[...] = acc[...].T[:8]
 
 
 def project_kernel(m, order_ref, *refs):
     ups, dns = refs[:m], refs[m : 2 * m]
-    l2t_ref, y_out, sq_out, buf, sem, project = refs[2 * m :]
+    l2t_ref, y_out, sq_out, buf, sem, project, acc = refs[2 * m :]
     k = pl.program_id(0)
     rank, rows = l2t_ref.shape
     w = buf.shape[2] // 2
 
     @pl.when(k == 0)
     def _():
-        project[0], project[1] = halves(l2t_ref[...])
+        project[...] = stacked(l2t_ref[...])
 
     at = pl.ds(rank, rows)
     averaged = fetcher([[(ups[i].at[at, :], 0, 0), (dns[i].at[at, :], 0, w)] for i in range(m)], buf, sem)
-    y2 = dot3((project[0], project[1]), halves(averaged))
+    y2 = dot3(project[...], halves(averaged))
     y_out[0] = y2
-    add_squares(k, y2, sq_out)
+    add_squares(k, m, y2, acc, sq_out)
 
 
 def moment_kernel(m, order_ref, *refs):
@@ -501,12 +507,12 @@
 
     @pl.when(pl.program_id(0) == 0)
     def _():
-        update[0], update[1] = halves(DAMPING * jnp.concatenate([l1_ref[...], l2_ref[...]], axis=1))
+        update[...] = stacked(DAMPING * jnp.concatenate([l1_ref[...], l2_ref[...]], axis=1))
 
     at = pl.ds(0, rank)
     y1 = fetcher([[(ups[i].at[at, :], 0, 0), (dns[i].at[at, :], 0, w)] for i in range(m)], buf, sem)
     y = halves(jnp.concatenate([y1, y_ref[0]], axis=0))
-    mom_out[0] = both_ref[0] - dot3((update[0], update[1]), y)
+    mom_out[0] = both_ref[0] - dot3(update[...], y)
 
 
 def chunk_at(steps, n):
@@ -530,17 +536,18 @@
     factors = [whole((rows, rank)), whole((rows, rank))]
     projected = [jax.ShapeDtypeStruct((m, rank, w), F32), jax.ShapeDtypeStruct((8, rank), F32)]
     moment = [jax.ShapeDtypeStruct(both.shape, F32)]
-    project_scratch = pltpu.VMEM((2, rank, rows), BF16)
-    moment_scratch = pltpu.VMEM((2, rows, 2 * rank), BF16)
+    project_scratch = pltpu.VMEM((2 * rank, rows), BF16)
+    squares_scratch = pltpu.VMEM((rank, LANES), F32)
+    moment_scratch = pltpu.VMEM((2 * rows, 2 * rank), BF16)
     kernel, args, specs, outs, out_specs, scratch, fetched, aliases = {
         "both": (
             advance_kernel, [both, l1, l2, l2t], [block] + factors + [whole((rank, rows))],
             moment + projected, [block, y_block, whole((8, rank))],
-            [project_scratch, moment_scratch], rank + rows, {1 + 2 * m: 0},
+            [project_scratch, moment_scratch, squares_scratch], rank + rows, {1 + 2 * m: 0},
         ),
         "project": (
             project_kernel, [l2t], [whole((rank, rows))],
-            projected, [y_block, whole((8, rank))], [project_scratch], rows, {},
+            projected, [y_block, whole((8, rank))], [project_scratch, squares_scratch], rows, {},
         ),
         "moment": (
             moment_kernel, [both, y, l1, l2], [block, y_block] + factors,
@@ -576,7 +583,7 @@
     @pl.when(pl.program_id(0) == 0)
     def _():
         left = jnp.concatenate([l1_ref[...] / norm_ref[...], l2_ref[...] / norm], axis=1)
-        update[0], update[1] = halves(rate * left)
+        update[...] = stacked(rate * left)
 
     pieces = []
     for y_ref, group in zip(ys, groups):
@@ -585,7 +592,7 @@
             rows = pl.ds(0, rank)
             pieces.append([(ups[i].at[rows, :], 0, 0), (dns[i].at[rows, :], 0, w), (y_ref.at[j], rank, 0)])
     y = fetcher(pieces, buf, sem)
-    w_out[...] = w_ref[...] - dot3((update[0], update[1]), halves(y))
+    w_out[...] = w_ref[...] - dot3(update[...], halves(y))
     right_out[...] = y[rank:].T / norm
 
 
@@ -613,7 +620,7 @@
             scratch_shapes=[
                 pltpu.VMEM((2, 2 * rank, w), F32),
                 pltpu.SemaphoreType.DMA((2, 3)),
-                pltpu.VMEM((2, rows, 2 * rank), BF16),
+                pltpu.VMEM((2 * rows, 2 * rank), BF16),
             ],
         ),
         cost_estimate=cost(12 * rows * cols * rank, 32 * rows * cols),

time: 166 us -> 166 us (level)
  no operation moved by 1% of the time
where the time goes in v6:
time: 166 us
  waiting for transfers between devices  59.9 us (36%)
  Pallas kernels  53.6 us (32%)
  starting transfers between devices  50.9 us (31%)
    ppermute x23, waiting for transfers between devices, flip(): return lax.ppermute(x, axis, [(i, i ^ bits) for i in range(size)])  44.2 us
    ppermute x23, starting transfers between devices, flip(): return lax.ppermute(x, axis, [(i, i ^ bits) for i in range(size)])  20.5 us
    ppermute x14, starting transfers between devices, step(): dn = lax.ppermute(dn, 'rep', back)  18.8 us
    ppermute x14, waiting for transfers between devices, step(): up = lax.ppermute(up, 'rep', ahead)  15.3 us
    pallas_call x3, Pallas kernels, advance(): pl.pallas_call(functools.partial(kernel, m), out_shape=outs, grid_spec=pl...  13.4 us
    pallas_call x2, Pallas kernels, orth_first(): pl.pallas_call(functools.partial(first_kernel, scaled), out_shape=shapes,...  12.5 us
    ppermute x14, starting transfers between devices, step(): up = lax.ppermute(up, 'rep', ahead)  11.6 us
    pallas_call x2, Pallas kernels, orth_second(): pl.pallas_call(second_kernel, out_shape=[jax.ShapeDtypeStruct((rows, rank...  11 us
  transfers between devices with their start and end apart: 51, of which 19 were waited for; matrix products, arithmetic and copies ran while one was open for 0% of the time, Pallas kernels for 26%

profile of v6, /device:TPU:0, one launch (start us, length us, event | category | flops | bytes accessed | tf_op | source)
XLA Modules:
  0.0 165.6 jit_solution(4399180937235069586)
XLA Ops:
  0.7 2.1 %lead.1 = (f32[576,128]{1,0:T(8,128)}, f32[576,128]{1,0:T(8,128)}) custom-call(s32[1]{0:T(128)} %bitcast.place_ref.at_ref.order_ref, f32[1,288,2048]{2,1,0:T(8,128)} %mom.1, bf16[2,1,288,2048]{3,2,1,0:T(8,128)(2,1)} %grads.1), custom_call_target="tpu_custom_call" | custom-call | flops 147456 | bytes 1179648 | tf_op jit(solution)/shard_map/lead/pallas_call | solution.py:233
  2.8 3.1 %collective-permute-start = (f32[576,128]{1,0:T(8,128)}, f32[576,128]{1,0:T(8,128)S(1)}, u32[]{:S(2)}, u32[]{:S(2)}) collective-permute-start(f32[576,128]{1,0:T(8,128)} %get-tuple-element.102), channel_id=1, source_target_pairs={{0,8},{8,16},{16,24},{24,28},{28,20},{20,12},{12,4},{4,0},{1,9},{9... | collective-permute-start | bytes 884744 | tf_op jit(solution)/shard_map/ppermute | solution.py:688
  5.9 6.2 %combine.1 = (f32[8,576,128]{2,1,0:T(8,128)S(1)}, f32[8,576,128]{2,1,0:T(8,128)S(1)}, f32[1,288,2048]{2,1,0:T(8,128)}, f32[72,256]{1,0:T(8,128)S(1)}, f32[72,256...) custom-call(s32[1]{0:T(128)} %bitcast.1.me_ref, f32[1,288,2048]{2,1,0:T(8,128)} %mom.1, ...), custom_call_target="tpu_custom_call" | custom-call | flops 1811939328 | bytes 16515072 | tf_op jit(solution)/shard_map/combine/pallas_call | solution.py:288
  15.3 6.0 %collective-permute-done.1.x_ref = f32[576,128]{1,0:T(8,128)S(1)} collective-permute-done((f32[576,128]{1,0:T(8,128)S(1)}, f32[576,128]{1,0:T(8,128)S(1)}, u32[]{:S(2)}, u32[]{:S(2)}) %collective-permute-start.1) | collective-permute-done | bytes 294944 | tf_op jit(solution)/shard_map/ppermute | solution.py:688
  25.4 3.1 %collective-permute-done.3.refs_2_ = f32[72,256]{1,0:T(8,128)S(1)} collective-permute-done((f32[72,256]{1,0:T(8,128)S(1)}, f32[72,256]{1,0:T(8,128)S(1)}, u32[]{:S(2)}, u32[]{:S(2)}) %collective-permute-start.3) | collective-permute-done | bytes 73760 | tf_op jit(solution)/shard_map/ppermute | solution.py:638
  31.8 2.5 %collective-permute-start.8 = (f32[72,256]{1,0:T(8,128)S(1)}, f32[72,256]{1,0:T(8,128)S(1)}, u32[]{:S(2)}, u32[]{:S(2)}) collective-permute-start(f32[72,256]{1,0:T(8,128)S(1)} %alike.8.refs_0_), channel_id=1, source_target_pairs={{0,12},{4,8},{8,4},{12,0},{16,28},{20,24},{24,20},{28,16},{1,13},{... | collective-permute-start | bytes 221192 | tf_op jit(solution)/shard_map/ppermute | solution.py:638
  35.3 6.8 %collective-permute-done.8.refs_3_ = f32[72,256]{1,0:T(8,128)S(1)} collective-permute-done((f32[72,256]{1,0:T(8,128)S(1)}, f32[72,256]{1,0:T(8,128)S(1)}, u32[]{:S(2)}, u32[]{:S(2)}) %collective-permute-start.8) | collective-permute-done | bytes 73760 | tf_op jit(solution)/shard_map/ppermute | solution.py:638
  45.7 2.6 %collective-permute-start.10 = (f32[72,256]{1,0:T(8,128)S(1)}, f32[72,256]{1,0:T(8,128)S(1)}, u32[]{:S(2)}, u32[]{:S(2)}) collective-permute-start(f32[72,256]{1,0:T(8,128)S(1)} %alike.9.refs_0_), channel_id=1, source_target_pairs={{0,16},{4,20},{8,24},{12,28},{16,0},{20,4},{24,8},{28,12},{1,17},{... | collective-permute-start | bytes 221192 | tf_op jit(solution)/shard_map/ppermute | solution.py:638
  48.3 8.6 %collective-permute-done.10.refs_1_ = f32[72,256]{1,0:T(8,128)S(1)} collective-permute-done((f32[72,256]{1,0:T(8,128)S(1)}, f32[72,256]{1,0:T(8,128)S(1)}, u32[]{:S(2)}, u32[]{:S(2)}) %collective-permute-start.10) | collective-permute-done | bytes 73760 | tf_op jit(solution)/shard_map/ppermute | solution.py:638
  57.0 2.1 %collective-permute-start.13 = (f32[72,256]{1,0:T(8,128)S(1)}, f32[72,256]{1,0:T(8,128)S(1)}, u32[]{:S(2)}, u32[]{:S(2)}) collective-permute-start(f32[72,256]{1,0:T(8,128)S(1)} %alike.10.refs_0_), channel_id=1, source_target_pairs={{0,2},{1,3},{2,0},{3,1},{4,6},{5,7},{6,4},{7,5},{8,10},{9,11},{10,... | collective-permute-start | bytes 221192 | tf_op jit(solution)/shard_map/ppermute | solution.py:638
  59.3 2.0 %collective-permute-start.22 = (f32[576,128]{1,0:T(8,128)S(1)}, f32[576,128]{1,0:T(8,128)S(1)}, u32[]{:S(2)}, u32[]{:S(2)}) collective-permute-start(f32[576,128]{1,0:T(8,128)S(1)} %ring_add.22), channel_id=1, source_target_pairs={{8,0},{16,8},{24,16},{28,24},{20,28},{12,20},{4,12},{0,4},{9,1},{1... | collective-permute-start | bytes 884744 | tf_op jit(solution)/shard_map/ppermute | solution.py:689
  63.0 6.2 %orth_first.2 = (f32[288,128]{1,0:T(8,128)S(1)}, f32[288,128]{1,0:T(8,128)S(1)}) custom-call(s32[1]{0:T(128)} %bitcast.1.me_ref, f32[72,256]{1,0:T(8,128)S(1)} %alike.10.refs_0_, f32[72,256]{1,0:T(8,128)S(1)} %collective-permute-done.12.refs_1_, f32[72,256]{1,0:T(8,128)S(1)} %collective-permute-done.13.refs_2_, f32[72,256]{1,0:T(8,128)S(1)} %collective-permute-done.14.refs_3_), custom_call_target="tpu_custom_call" | custom-call | flops 6000000000 | bytes 1000000 | tf_op jit(solution)/shard_map/orth_first/pallas_call | solution.py:176
  69.4 2.2 %collective-permute-start.23 = (f32[576,128]{1,0:T(8,128)S(1)}, f32[576,128]{1,0:T(8,128)S(1)}, u32[]{:S(2)}, u32[]{:S(2)}) collective-permute-start(f32[576,128]{1,0:T(8,128)S(1)} %ring_add.23), channel_id=1, source_target_pairs={{8,0},{16,8},{24,16},{28,24},{20,28},{12,20},{4,12},{0,4},{9,1},{1... | collective-permute-start | bytes 884744 | tf_op jit(solution)/shard_map/ppermute | solution.py:689
  71.6 5.5 %orth_second.2 = (f32[288,256]{1,0:T(8,128)S(1)}, f32[256,288]{1,0:T(8,128)S(1)}) custom-call(f32[288,128]{1,0:T(8,128)S(1)} %get-tuple-element.136.left_ref, f32[288,128]{1,0:T(8,128)S(1)} %get-tuple-element.137.rest_ref), custom_call_target="tpu_custom_call" | custom-call | flops 6000000000 | bytes 1000000 | tf_op jit(solution)/shard_map/orth_second/pallas_call | solution.py:190
  83.0 5.3 %collective-permute-done.24.refs_0_.refs_6_ = f32[544,128]{1,0:T(8,128)S(1)} collective-permute-done((f32[544,128]{1,0:T(8,128)S(1)}, f32[544,128]{1,0:T(8,128)S(1)}, u32[]{:S(2)}, u32[]{:S(2)}) %collective-permute-start.24) | collective-permute-done | bytes 278560 | tf_op jit(solution)/shard_map/ppermute | solution.py:688
  92.2 3.5 %collective-permute-done.26.refs_2_ = f32[80,256]{1,0:T(8,128)S(1)} collective-permute-done((f32[80,256]{1,0:T(8,128)S(1)}, f32[80,256]{1,0:T(8,128)S(1)}, u32[]{:S(2)}, u32[]{:S(2)}) %collective-permute-start.26) | collective-permute-done | bytes 81952 | tf_op jit(solution)/shard_map/ppermute | solution.py:638
  102.1 6.6 %collective-permute-done.31.refs_3_ = f32[80,256]{1,0:T(8,128)S(1)} collective-permute-done((f32[80,256]{1,0:T(8,128)S(1)}, f32[80,256]{1,0:T(8,128)S(1)}, u32[]{:S(2)}, u32[]{:S(2)}) %collective-permute-start.31) | collective-permute-done | bytes 81952 | tf_op jit(solution)/shard_map/ppermute | solution.py:638
  112.3 8.6 %collective-permute-done.33.refs_1_ = f32[80,256]{1,0:T(8,128)S(1)} collective-permute-done((f32[80,256]{1,0:T(8,128)S(1)}, f32[80,256]{1,0:T(8,128)S(1)}, u32[]{:S(2)}, u32[]{:S(2)}) %collective-permute-start.33) | collective-permute-done | bytes 81952 | tf_op jit(solution)/shard_map/ppermute | solution.py:638
  122.8 2.0 %collective-permute-start.44 = (f32[544,128]{1,0:T(8,128)S(1)}, f32[544,128]{1,0:T(8,128)S(1)}, u32[]{:S(2)}, u32[]{:S(2)}) collective-permute-start(f32[544,128]{1,0:T(8,128)S(1)} %collective-permute-done.43.refs_9_.refs_11_), channel_id=1, source_target_pairs={{8,0},{16,8},{24,16},{28,24},{20,28},{12,20},{4,12},{0,4},{9,1},{1... | collective-permute-start | bytes 835592 | tf_op jit(solution)/shard_map/ppermute | solution.py:689
  126.8 6.3 %orth_first.3 = (f32[288,128]{1,0:T(8,128)S(1)}, f32[288,128]{1,0:T(8,128)S(1)}, f32[1,256]{1,0:T(1,128)S(1)}) custom-call(s32[1]{0:T(128)} %bitcast.1.me_ref, f32[80,256]{1,0:T(8,128)S(1)} %alike.13.refs_0_, f32[80,256]{1,0:T(8,128)S(1)} %collective-permute-done.35.refs_1_, f32[80,256]{1,0:T(8,128)S(1)} %collective-permute-done.36.refs_2_, ...), custom_call_target="tpu_custom_call" | custom-call | flops 6000000000 | bytes 1000000 | tf_op jit(solution)/shard_map/orth_first/pallas_call | solution.py:176
  135.1 5.5 %orth_second.3 = (f32[288,256]{1,0:T(8,128)S(1)}, f32[256,288]{1,0:T(8,128)S(1)}) custom-call(f32[288,128]{1,0:T(8,128)S(1)} %get-tuple-element.166.left_ref, f32[288,128]{1,0:T(8,128)S(1)} %get-tuple-element.167.rest_ref), custom_call_target="tpu_custom_call" | custom-call | flops 6000000000 | bytes 1000000 | tf_op jit(solution)/shard_map/orth_second/pallas_call | solution.py:190
  144.2 9.0 %shard_map.67 = (f32[1,288,2048]{2,1,0:T(8,128)}, f32[6,256,256]{2,1,0:T(8,128)S(1)}, f32[8,256]{1,0:T(8,128)S(1)}) custom-call(s32[1]{0:T(128)} %bitcast.place_ref.at_ref.order_ref, f32[544,128]{1,0:T(8,128)S(1)} %get-tuple-element.147.up_ref.refs_0_, f32[544,128]{1,0:T(8,128)S(1)} %collective-permute-done.28.refs_1_, ...), custom_call_target="tpu_custom_call", output_to_operand_aliasing={{0}: (13, {})} | custom-call | flops 2264924160 | bytes 10616832 | tf_op jit(solution)/shard_map/pallas_call | solution.py:557
  156.6 2.9 %shard_map.69 = f32[1,288,2048]{2,1,0:T(8,128)} custom-call(s32[1]{0:T(128)} %bitcast.place_ref.at_ref.order_ref, f32[544,128]{1,0:T(8,128)S(1)} %collective-permute-done.24.refs_0_.refs_6_, f32[544,128]{1,0:T(8,128)S(1)} %collective-permute-done.46.refs_1_.refs_7_, ...), custom_call_target="tpu_custom_call", output_to_operand_aliasing={{}: (5, {})} | custom-call | flops 754974720 | bytes 3538944 | tf_op jit(solution)/shard_map/pallas_call | solution.py:557
  159.6 5.8 %finish.1 = (f32[288,2048]{1,0:T(8,128)}, f32[2048,256]{1,0:T(8,128)}) custom-call(s32[1]{0:T(128)} %bitcast.place_ref.at_ref.order_ref, f32[544,128]{1,0:T(8,128)S(1)} %get-tuple-element.147.up_ref.refs_0_, f32[544,128]{1,0:T(8,128)S(1)} %collective-permute-done.28.refs_1_, f32[544,128]{1,0:T(8,128)S(1)} %collective-permute-done.32.refs_2_, ...), custom_call_target="tpu_custom_call" | custom-call | flops 1811939328 | bytes 18874368 | tf_op jit(solution)/shard_map/finish/pallas_call | solution.py:607
  (114 shorter events, 49.6 us)
Async XLA Ops:
  2.8 10.3 %collective-permute-start = (f32[576,128]{1,0:T(8,128)}, f32[576,128]{1,0:T(8,128)S(1)}, u32[]{:S(2)}, u32[]{:S(2)}) collective-permute-start(f32[576,128]{1,0:T(8,128)} %get-tuple-element.102), channel_id=1, source_target_pairs={{0,8},{8,16},{16,24},{24,28},{28,20},{20,12},{12,4},{4,0},{1,9},{9... | collective-permute-start | bytes 884744 | tf_op jit(solution)/shard_map/ppermute | solution.py:688
  29.6 13.9 %collective-permute-start.9 = (f32[576,128]{1,0:T(8,128)S(1)}, f32[576,128]{1,0:T(8,128)S(1)}, u32[]{:S(2)}, u32[]{:S(2)}) collective-permute-start(f32[576,128]{1,0:T(8,128)S(1)} %ring_add.14), channel_id=1, source_target_pairs={{0,8},{8,16},{16,24},{24,28},{28,20},{20,12},{12,4},{4,0},{1,9},{9... | collective-permute-start | bytes 884744 | tf_op jit(solution)/shard_map/ppermute | solution.py:688
  31.3 12.7 %collective-permute-start.20 = (f32[576,128]{1,0:T(8,128)S(1)}, f32[576,128]{1,0:T(8,128)S(1)}, u32[]{:S(2)}, u32[]{:S(2)}) collective-permute-start(f32[576,128]{1,0:T(8,128)S(1)} %ring_add.20), channel_id=1, source_target_pairs={{8,0},{16,8},{24,16},{28,24},{20,28},{12,20},{4,12},{0,4},{9,1},{1... | collective-permute-start | bytes 884744 | tf_op jit(solution)/shard_map/ppermute | solution.py:689
  31.8 10.3 %collective-permute-start.8 = (f32[72,256]{1,0:T(8,128)S(1)}, f32[72,256]{1,0:T(8,128)S(1)}, u32[]{:S(2)}, u32[]{:S(2)}) collective-permute-start(f32[72,256]{1,0:T(8,128)S(1)} %alike.8.refs_0_), channel_id=1, source_target_pairs={{0,12},{4,8},{8,4},{12,0},{16,28},{20,24},{24,20},{28,16},{1,13},{... | collective-permute-start | bytes 221192 | tf_op jit(solution)/shard_map/ppermute | solution.py:638
  34.3 9.1 %collective-permute-start.7 = (f32[72,256]{1,0:T(8,128)S(1)}, f32[72,256]{1,0:T(8,128)S(1)}, u32[]{:S(2)}, u32[]{:S(2)}) collective-permute-start(f32[72,256]{1,0:T(8,128)S(1)} %alike.8.refs_0_), channel_id=1, source_target_pairs={{0,8},{4,12},{8,0},{12,4},{16,24},{20,28},{24,16},{28,20},{1,9},{5... | collective-permute-start | bytes 221192 | tf_op jit(solution)/shard_map/ppermute | solution.py:638
  43.5 15.6 %collective-permute-start.11 = (f32[576,128]{1,0:T(8,128)S(1)}, f32[576,128]{1,0:T(8,128)S(1)}, u32[]{:S(2)}, u32[]{:S(2)}) collective-permute-start(f32[576,128]{1,0:T(8,128)S(1)} %ring_add.15), channel_id=1, source_target_pairs={{0,8},{8,16},{16,24},{24,28},{28,20},{20,12},{12,4},{4,0},{1,9},{9... | collective-permute-start | bytes 884744 | tf_op jit(solution)/shard_map/ppermute | solution.py:688
  44.0 15.2 %collective-permute-start.21 = (f32[576,128]{1,0:T(8,128)S(1)}, f32[576,128]{1,0:T(8,128)S(1)}, u32[]{:S(2)}, u32[]{:S(2)}) collective-permute-start(f32[576,128]{1,0:T(8,128)S(1)} %ring_add.21), channel_id=1, source_target_pairs={{8,0},{16,8},{24,16},{28,24},{20,28},{12,20},{4,12},{0,4},{9,1},{1... | collective-permute-start | bytes 884744 | tf_op jit(solution)/shard_map/ppermute | solution.py:689
  45.7 11.2 %collective-permute-start.10 = (f32[72,256]{1,0:T(8,128)S(1)}, f32[72,256]{1,0:T(8,128)S(1)}, u32[]{:S(2)}, u32[]{:S(2)}) collective-permute-start(f32[72,256]{1,0:T(8,128)S(1)} %alike.9.refs_0_), channel_id=1, source_target_pairs={{0,16},{4,20},{8,24},{12,28},{16,0},{20,4},{24,8},{28,12},{1,17},{... | collective-permute-start | bytes 221192 | tf_op jit(solution)/shard_map/ppermute | solution.py:638
  59.2 10.0 %collective-permute-start.15 = (f32[576,128]{1,0:T(8,128)S(1)}, f32[576,128]{1,0:T(8,128)S(1)}, u32[]{:S(2)}, u32[]{:S(2)}) collective-permute-start(f32[576,128]{1,0:T(8,128)S(1)} %ring_add.16), channel_id=1, source_target_pairs={{0,8},{8,16},{16,24},{24,28},{28,20},{20,12},{12,4},{4,0},{1,9},{9... | collective-permute-start | bytes 884744 | tf_op jit(solution)/shard_map/ppermute | solution.py:688
  59.3 10.0 %collective-permute-start.22 = (f32[576,128]{1,0:T(8,128)S(1)}, f32[576,128]{1,0:T(8,128)S(1)}, u32[]{:S(2)}, u32[]{:S(2)}) collective-permute-start(f32[576,128]{1,0:T(8,128)S(1)} %ring_add.22), channel_id=1, source_target_pairs={{8,0},{16,8},{24,16},{28,24},{20,28},{12,20},{4,12},{0,4},{9,1},{1... | collective-permute-start | bytes 884744 | tf_op jit(solution)/shard_map/ppermute | solution.py:689
  69.3 9.3 %collective-permute-start.16 = (f32[576,128]{1,0:T(8,128)S(1)}, f32[576,128]{1,0:T(8,128)S(1)}, u32[]{:S(2)}, u32[]{:S(2)}) collective-permute-start(f32[576,128]{1,0:T(8,128)S(1)} %ring_add.17), channel_id=1, source_target_pairs={{0,8},{8,16},{16,24},{24,28},{28,20},{20,12},{12,4},{4,0},{1,9},{9... | collective-permute-start | bytes 884744 | tf_op jit(solution)/shard_map/ppermute | solution.py:688
  69.4 9.4 %collective-permute-start.23 = (f32[576,128]{1,0:T(8,128)S(1)}, f32[576,128]{1,0:T(8,128)S(1)}, u32[]{:S(2)}, u32[]{:S(2)}) collective-permute-start(f32[576,128]{1,0:T(8,128)S(1)} %ring_add.23), channel_id=1, source_target_pairs={{8,0},{16,8},{24,16},{28,24},{20,28},{12,20},{4,12},{0,4},{9,1},{1... | collective-permute-start | bytes 884744 | tf_op jit(solution)/shard_map/ppermute | solution.py:689
  96.5 12.5 %collective-permute-start.32 = (f32[544,128]{1,0:T(8,128)S(1)}, f32[544,128]{1,0:T(8,128)S(1)}, u32[]{:S(2)}, u32[]{:S(2)}) collective-permute-start(f32[544,128]{1,0:T(8,128)S(1)} %collective-permute-done.28.refs_1_), channel_id=1, source_target_pairs={{0,8},{8,16},{16,24},{24,28},{28,20},{20,12},{12,4},{4,0},{1,9},{9... | collective-permute-start | bytes 835592 | tf_op jit(solution)/shard_map/ppermute | solution.py:688
  96.9 13.9 %collective-permute-start.42 = (f32[544,128]{1,0:T(8,128)S(1)}, f32[544,128]{1,0:T(8,128)S(1)}, u32[]{:S(2)}, u32[]{:S(2)}) collective-permute-start(f32[544,128]{1,0:T(8,128)S(1)} %collective-permute-done.41.refs_11_.refs_13_), channel_id=1, source_target_pairs={{8,0},{16,8},{24,16},{28,24},{20,28},{12,20},{4,12},{0,4},{9,1},{1... | collective-permute-start | bytes 835592 | tf_op jit(solution)/shard_map/ppermute | solution.py:689
  98.6 10.1 %collective-permute-start.31 = (f32[80,256]{1,0:T(8,128)S(1)}, f32[80,256]{1,0:T(8,128)S(1)}, u32[]{:S(2)}, u32[]{:S(2)}) collective-permute-start(f32[80,256]{1,0:T(8,128)S(1)} %alike.11.refs_0_), channel_id=1, source_target_pairs={{0,12},{4,8},{8,4},{12,0},{16,28},{20,24},{24,20},{28,16},{1,13},{... | collective-permute-start | bytes 245768 | tf_op jit(solution)/shard_map/ppermute | solution.py:638
  109.1 13.8 %collective-permute-start.34 = (f32[544,128]{1,0:T(8,128)S(1)}, f32[544,128]{1,0:T(8,128)S(1)}, u32[]{:S(2)}, u32[]{:S(2)}) collective-permute-start(f32[544,128]{1,0:T(8,128)S(1)} %collective-permute-done.32.refs_2_), channel_id=1, source_target_pairs={{0,8},{8,16},{16,24},{24,28},{28,20},{20,12},{12,4},{4,0},{1,9},{9... | collective-permute-start | bytes 835592 | tf_op jit(solution)/shard_map/ppermute | solution.py:688
  110.8 12.1 %collective-permute-start.43 = (f32[544,128]{1,0:T(8,128)S(1)}, f32[544,128]{1,0:T(8,128)S(1)}, u32[]{:S(2)}, u32[]{:S(2)}) collective-permute-start(f32[544,128]{1,0:T(8,128)S(1)} %collective-permute-done.42.refs_10_.refs_12_), channel_id=1, source_target_pairs={{8,0},{16,8},{24,16},{28,24},{20,28},{12,20},{4,12},{0,4},{9,1},{1... | collective-permute-start | bytes 835592 | tf_op jit(solution)/shard_map/ppermute | solution.py:689
  111.1 9.7 %collective-permute-start.33 = (f32[80,256]{1,0:T(8,128)S(1)}, f32[80,256]{1,0:T(8,128)S(1)}, u32[]{:S(2)}, u32[]{:S(2)}) collective-permute-start(f32[80,256]{1,0:T(8,128)S(1)} %alike.12.refs_0_), channel_id=1, source_target_pairs={{0,16},{4,20},{8,24},{12,28},{16,0},{20,4},{24,8},{28,12},{1,17},{... | collective-permute-start | bytes 245768 | tf_op jit(solution)/shard_map/ppermute | solution.py:638
  122.8 10.2 %collective-permute-start.38 = (f32[544,128]{1,0:T(8,128)S(1)}, f32[544,128]{1,0:T(8,128)S(1)}, u32[]{:S(2)}, u32[]{:S(2)}) collective-permute-start(f32[544,128]{1,0:T(8,128)S(1)} %collective-permute-done.34.refs_3_), channel_id=1, source_target_pairs={{0,8},{8,16},{16,24},{24,28},{28,20},{20,12},{12,4},{4,0},{1,9},{9... | collective-permute-start | bytes 835592 | tf_op jit(solution)/shard_map/ppermute | solution.py:688
  122.8 10.3 %collective-permute-start.44 = (f32[544,128]{1,0:T(8,128)S(1)}, f32[544,128]{1,0:T(8,128)S(1)}, u32[]{:S(2)}, u32[]{:S(2)}) collective-permute-start(f32[544,128]{1,0:T(8,128)S(1)} %collective-permute-done.43.refs_9_.refs_11_), channel_id=1, source_target_pairs={{8,0},{16,8},{24,16},{28,24},{20,28},{12,20},{4,12},{0,4},{9,1},{1... | collective-permute-start | bytes 835592 | tf_op jit(solution)/shard_map/ppermute | solution.py:689
  133.1 9.1 %collective-permute-start.39 = (f32[544,128]{1,0:T(8,128)S(1)}, f32[544,128]{1,0:T(8,128)S(1)}, u32[]{:S(2)}, u32[]{:S(2)}) collective-permute-start(f32[544,128]{1,0:T(8,128)S(1)} %collective-permute-done.38.refs_4_), channel_id=1, source_target_pairs={{0,8},{8,16},{16,24},{24,28},{28,20},{20,12},{12,4},{4,0},{1,9},{9... | collective-permute-start | bytes 835592 | tf_op jit(solution)/shard_map/ppermute | solution.py:688
  133.1 9.3 %collective-permute-start.45 = (f32[544,128]{1,0:T(8,128)S(1)}, f32[544,128]{1,0:T(8,128)S(1)}, u32[]{:S(2)}, u32[]{:S(2)}) collective-permute-start(f32[544,128]{1,0:T(8,128)S(1)} %collective-permute-done.44.refs_8_.refs_10_), channel_id=1, source_target_pairs={{8,0},{16,8},{24,16},{28,24},{20,28},{12,20},{4,12},{0,4},{9,1},{1... | collective-permute-start | bytes 835592 | tf_op jit(solution)/shard_map/ppermute | solution.py:689
  142.1 11.1 %collective-permute-start.46 = (f32[544,128]{1,0:T(8,128)S(1)}, f32[544,128]{1,0:T(8,128)S(1)}, u32[]{:S(2)}, u32[]{:S(2)}) collective-permute-start(f32[544,128]{1,0:T(8,128)S(1)} %collective-permute-done.39.refs_5_), channel_id=1, source_target_pairs={{0,8},{8,16},{16,24},{24,28},{28,20},{20,12},{12,4},{4,0},{1,9},{9... | collective-permute-start | bytes 835592 | tf_op jit(solution)/shard_map/ppermute | solution.py:688
  142.4 10.8 %collective-permute-start.47 = (f32[544,128]{1,0:T(8,128)S(1)}, f32[544,128]{1,0:T(8,128)S(1)}, u32[]{:S(2)}, u32[]{:S(2)}) collective-permute-start(f32[544,128]{1,0:T(8,128)S(1)} %collective-permute-done.45.refs_7_.refs_9_), channel_id=1, source_target_pairs={{8,0},{16,8},{24,16},{28,24},{20,28},{12,20},{4,12},{0,4},{9,1},{1... | collective-permute-start | bytes 835592 | tf_op jit(solution)/shard_map/ppermute | solution.py:689
  (29 other events, 174.4 us)

commit v7 on v6

--- a/solution.py
+++ b/solution.py
@@ -359,7 +359,7 @@
     mean = jnp.concatenate([up, dn], axis=1) * inv
     averaged, later = mean[:rows], mean[rows:]
     right = dot(leftt_ref[...], averaged)
-    averaged = averaged - DAMPING * dot(left_ref[...], right) + later
+    averaged = averaged - DAMPING * dot3(stacked(left_ref[...]), halves(right)) + later
     up_out[:rank] = right[:, :w]
     dn_out[:rank] = right[:, w:]
     up_out[rank:] = averaged[:, :w]
@@ -445,7 +445,7 @@
 
 def advance_kernel(m, order_ref, *refs):
     ups, dns = refs[:m], refs[m : 2 * m]
-    both_ref, l1_ref, l2_ref, l2t_ref, mom_out, y_out, sq_out, buf, sem, project, update, acc = refs[2 * m :]
+    both_ref, l1_ref, l2_ref, l2t_ref, *_, mom_out, y_out, sq_out, buf, sem, project, update, acc = refs[2 * m :]
     k = pl.program_id(0)
     rank = l2t_ref.shape[0]
     w = buf.shape[2] // 2
@@ -501,7 +501,7 @@
 
 def moment_kernel(m, order_ref, *refs):
     ups, dns = refs[:m], refs[m : 2 * m]
-    both_ref, y_ref, l1_ref, l2_ref, mom_out, buf, sem, update = refs[2 * m :]
+    both_ref, y_ref, l1_ref, l2_ref, *_, mom_out, buf, sem, update = refs[2 * m :]
     rank = y_ref.shape[1]
     w = buf.shape[2] // 2
 
@@ -525,7 +525,7 @@
     return at
 
 
-def advance(mode, place, steps, n, ups, dns, both, y, l1, l2, l2t):
+def advance(mode, place, steps, n, ups, dns, both, done, y, l1, l2, l2t):
     m = len(ups)
     _, rows, _ = both.shape
     rank = l1.shape[1]
@@ -539,21 +539,25 @@
     project_scratch = pltpu.VMEM((2 * rank, rows), BF16)
     squares_scratch = pltpu.VMEM((rank, LANES), F32)
     moment_scratch = pltpu.VMEM((2 * rows, 2 * rank), BF16)
-    kernel, args, specs, outs, out_specs, scratch, fetched, aliases = {
+    kernel, args, specs, outs, out_specs, scratch, fetched = {
         "both": (
             advance_kernel, [both, l1, l2, l2t], [block] + factors + [whole((rank, rows))],
             moment + projected, [block, y_block, whole((8, rank))],
-            [project_scratch, moment_scratch, squares_scratch], rank + rows, {1 + 2 * m: 0},
+            [project_scratch, moment_scratch, squares_scratch], rank + rows,
         ),
         "project": (
             project_kernel, [l2t], [whole((rank, rows))],
-            projected, [y_block, whole((8, rank))], [project_scratch, squares_scratch], rows, {},
+            projected, [y_block, whole((8, rank))], [project_scratch, squares_scratch], rows,
         ),
         "moment": (
             moment_kernel, [both, y, l1, l2], [block, y_block] + factors,
-            moment, [block], [moment_scratch], rank, {1 + 2 * m: 0},
+            moment, [block], [moment_scratch], rank,
         ),
     }[mode]
+    aliases = {}
+    if done is not None:
+        aliases = {1 + 2 * m + len(args): 0}
+        args, specs = args + [done], specs + [pl.BlockSpec(memory_space=pl.ANY)]
     return pl.pallas_call(
         functools.partial(kernel, m),
         out_shape=outs,
@@ -740,15 +744,16 @@
         sides = ([ups[c] for c in new], [dns[(n - c) % n] for c in new])
         factors = (l1, box["left"], box["leftt"])
         if not last:
-            box["both"], y, squares = advance("both", place, new, n, *sides, box["both"], None, *factors)
+            done = box.get("done")
+            box["done"], y, squares = advance("both", place, new, n, *sides, both, done, None, *factors)
             ys.append(y)
             totals.append(squares)
             return None
-        y, squares = advance("project", place, new, n, *sides, box["both"], None, *factors)
+        y, squares = advance("project", place, new, n, *sides, both, None, None, *factors)
         ys.append(y)
         totals.append(squares)
         total = alike_total(totals, count)
-        (box["both"],) = advance("moment", place, new, n, *sides, box["both"], y, *factors)
+        (box["done"],) = advance("moment", place, new, n, *sides, both, box.get("done"), y, *factors)
         return total
 
     work = [[begin_again, stages[0]]] + [[stage] for stage in stages[1:]] + [[first(True)], [second]]
@@ -759,16 +764,14 @@
                 stage()
             (up,) = tie(box, up)
         else:
-            box.setdefault("both", both)
             advance_ready()
             (up,) = tie(box, up)
         ups.append(up)
         dns.append(dn)
-    box.setdefault("both", both)
     total = advance_ready(last=True)
     sides = ([ups[c] for c in ready], [dns[(n - c) % n] for c in ready])
     new_weights, new_right = finish(place, ready, *sides, ys, weights, l1, box["left"], box["norm"], [total], rate)
-    return new_weights, box["both"], new_right
+    return new_weights, box["done"], new_right
 
 
 def alike_total(totals, count):

time: 166 us -> 164 us (0.988)
  Pallas kernels: 53.6 us -> 51.4 us
    pallas_call x3, Pallas kernels: 13.4 us -> 11.5 us  [advance(): pl.pallas_call(functools.partial(kernel, m), out_shape=outs, grid_spec=pl...]
  transfers between devices with their start and end apart: 51 -> 51, of which waited for: 19 -> 19; matrix products, arithmetic and copies ran while one was open for 0% -> 0% of each run, Pallas kernels for 26% -> 25%
where the time goes in v7:
time: 164 us; the launch traced here: 163 us
  waiting for transfers between devices  59.9 us (37%)
  Pallas kernels  51.4 us (31%)
  starting transfers between devices  50.9 us (31%)
    ppermute x23, waiting for transfers between devices, flip(): return lax.ppermute(x, axis, [(i, i ^ bits) for i in range(size)])  44.3 us
    ppermute x23, starting transfers between devices, flip(): return lax.ppermute(x, axis, [(i, i ^ bits) for i in range(size)])  20.5 us
    ppermute x14, starting transfers between devices, step(): dn = lax.ppermute(dn, 'rep', back)  18.8 us
    ppermute x14, waiting for transfers between devices, step(): up = lax.ppermute(up, 'rep', ahead)  15.3 us
    pallas_call x2, Pallas kernels, orth_first(): pl.pallas_call(functools.partial(first_kernel, scaled), out_shape=shapes,...  12.5 us
    ppermute x14, starting transfers between devices, step(): up = lax.ppermute(up, 'rep', ahead)  11.6 us
    pallas_call x3, Pallas kernels, advance(): pl.pallas_call(functools.partial(kernel, m), out_shape=outs, grid_spec=pl...  11.5 us
    pallas_call x2, Pallas kernels, orth_second(): pl.pallas_call(second_kernel, out_shape=[jax.ShapeDtypeStruct((rows, rank...  11 us
  transfers between devices with their start and end apart: 51, of which 19 were waited for; matrix products, arithmetic and copies ran while one was open for 0% of the time, Pallas kernels for 25%

profile of v7, /device:TPU:0, one launch (start us, length us, event | category | flops | bytes accessed | tf_op | source)
XLA Modules:
  0.0 163.5 jit_solution(17979917716630892242)
XLA Ops:
  0.7 2.1 %lead.1 = (f32[576,128]{1,0:T(8,128)}, f32[576,128]{1,0:T(8,128)}) custom-call(s32[1]{0:T(128)} %bitcast.place_ref.at_ref.order_ref, f32[1,288,2048]{2,1,0:T(8,128)} %mom.1, bf16[2,1,288,2048]{3,2,1,0:T(8,128)(2,1)} %grads.1), custom_call_target="tpu_custom_call" | custom-call | flops 147456 | bytes 1179648 | tf_op jit(solution)/shard_map/lead/pallas_call | solution.py:233
  2.8 3.1 %collective-permute-start = (f32[576,128]{1,0:T(8,128)}, f32[576,128]{1,0:T(8,128)S(1)}, u32[]{:S(2)}, u32[]{:S(2)}) collective-permute-start(f32[576,128]{1,0:T(8,128)} %get-tuple-element.102), channel_id=1, source_target_pairs={{0,8},{8,16},{16,24},{24,28},{28,20},{20,12},{12,4},{4,0},{1,9},{9... | collective-permute-start | bytes 884744 | tf_op jit(solution)/shard_map/ppermute | solution.py:692
  5.9 6.2 %combine.1 = (f32[8,576,128]{2,1,0:T(8,128)S(1)}, f32[8,576,128]{2,1,0:T(8,128)S(1)}, f32[1,288,2048]{2,1,0:T(8,128)}, f32[72,256]{1,0:T(8,128)S(1)}, f32[72,256...) custom-call(s32[1]{0:T(128)} %bitcast.1.me_ref, f32[1,288,2048]{2,1,0:T(8,128)} %mom.1, ...), custom_call_target="tpu_custom_call" | custom-call | flops 1811939328 | bytes 16515072 | tf_op jit(solution)/shard_map/combine/pallas_call | solution.py:288
  15.3 6.0 %collective-permute-done.1.x_ref = f32[576,128]{1,0:T(8,128)S(1)} collective-permute-done((f32[576,128]{1,0:T(8,128)S(1)}, f32[576,128]{1,0:T(8,128)S(1)}, u32[]{:S(2)}, u32[]{:S(2)}) %collective-permute-start.1) | collective-permute-done | bytes 294944 | tf_op jit(solution)/shard_map/ppermute | solution.py:692
  25.4 3.1 %collective-permute-done.3.refs_2_ = f32[72,256]{1,0:T(8,128)S(1)} collective-permute-done((f32[72,256]{1,0:T(8,128)S(1)}, f32[72,256]{1,0:T(8,128)S(1)}, u32[]{:S(2)}, u32[]{:S(2)}) %collective-permute-start.3) | collective-permute-done | bytes 73760 | tf_op jit(solution)/shard_map/ppermute | solution.py:642
  31.8 2.5 %collective-permute-start.8 = (f32[72,256]{1,0:T(8,128)S(1)}, f32[72,256]{1,0:T(8,128)S(1)}, u32[]{:S(2)}, u32[]{:S(2)}) collective-permute-start(f32[72,256]{1,0:T(8,128)S(1)} %alike.8.refs_0_), channel_id=1, source_target_pairs={{0,12},{4,8},{8,4},{12,0},{16,28},{20,24},{24,20},{28,16},{1,13},{... | collective-permute-start | bytes 221192 | tf_op jit(solution)/shard_map/ppermute | solution.py:642
  35.3 6.8 %collective-permute-done.8.refs_3_ = f32[72,256]{1,0:T(8,128)S(1)} collective-permute-done((f32[72,256]{1,0:T(8,128)S(1)}, f32[72,256]{1,0:T(8,128)S(1)}, u32[]{:S(2)}, u32[]{:S(2)}) %collective-permute-start.8) | collective-permute-done | bytes 73760 | tf_op jit(solution)/shard_map/ppermute | solution.py:642
  45.7 2.6 %collective-permute-start.10 = (f32[72,256]{1,0:T(8,128)S(1)}, f32[72,256]{1,0:T(8,128)S(1)}, u32[]{:S(2)}, u32[]{:S(2)}) collective-permute-start(f32[72,256]{1,0:T(8,128)S(1)} %alike.9.refs_0_), channel_id=1, source_target_pairs={{0,16},{4,20},{8,24},{12,28},{16,0},{20,4},{24,8},{28,12},{1,17},{... | collective-permute-start | bytes 221192 | tf_op jit(solution)/shard_map/ppermute | solution.py:642
  48.3 8.6 %collective-permute-done.10.refs_1_ = f32[72,256]{1,0:T(8,128)S(1)} collective-permute-done((f32[72,256]{1,0:T(8,128)S(1)}, f32[72,256]{1,0:T(8,128)S(1)}, u32[]{:S(2)}, u32[]{:S(2)}) %collective-permute-start.10) | collective-permute-done | bytes 73760 | tf_op jit(solution)/shard_map/ppermute | solution.py:642
  57.0 2.1 %collective-permute-start.13 = (f32[72,256]{1,0:T(8,128)S(1)}, f32[72,256]{1,0:T(8,128)S(1)}, u32[]{:S(2)}, u32[]{:S(2)}) collective-permute-start(f32[72,256]{1,0:T(8,128)S(1)} %alike.10.refs_0_), channel_id=1, source_target_pairs={{0,2},{1,3},{2,0},{3,1},{4,6},{5,7},{6,4},{7,5},{8,10},{9,11},{10,... | collective-permute-start | bytes 221192 | tf_op jit(solution)/shard_map/ppermute | solution.py:642
  59.3 2.0 %collective-permute-start.22 = (f32[576,128]{1,0:T(8,128)S(1)}, f32[576,128]{1,0:T(8,128)S(1)}, u32[]{:S(2)}, u32[]{:S(2)}) collective-permute-start(f32[576,128]{1,0:T(8,128)S(1)} %ring_add.22), channel_id=1, source_target_pairs={{8,0},{16,8},{24,16},{28,24},{20,28},{12,20},{4,12},{0,4},{9,1},{1... | collective-permute-start | bytes 884744 | tf_op jit(solution)/shard_map/ppermute | solution.py:693
  63.0 6.2 %orth_first.2 = (f32[288,128]{1,0:T(8,128)S(1)}, f32[288,128]{1,0:T(8,128)S(1)}) custom-call(s32[1]{0:T(128)} %bitcast.1.me_ref, f32[72,256]{1,0:T(8,128)S(1)} %alike.10.refs_0_, f32[72,256]{1,0:T(8,128)S(1)} %collective-permute-done.12.refs_1_, f32[72,256]{1,0:T(8,128)S(1)} %collective-permute-done.13.refs_2_, f32[72,256]{1,0:T(8,128)S(1)} %collective-permute-done.14.refs_3_), custom_call_target="tpu_custom_call" | custom-call | flops 6000000000 | bytes 1000000 | tf_op jit(solution)/shard_map/orth_first/pallas_call | solution.py:176
  69.4 2.2 %collective-permute-start.23 = (f32[576,128]{1,0:T(8,128)S(1)}, f32[576,128]{1,0:T(8,128)S(1)}, u32[]{:S(2)}, u32[]{:S(2)}) collective-permute-start(f32[576,128]{1,0:T(8,128)S(1)} %ring_add.23), channel_id=1, source_target_pairs={{8,0},{16,8},{24,16},{28,24},{20,28},{12,20},{4,12},{0,4},{9,1},{1... | collective-permute-start | bytes 884744 | tf_op jit(solution)/shard_map/ppermute | solution.py:693
  71.6 5.5 %orth_second.2 = (f32[288,256]{1,0:T(8,128)S(1)}, f32[256,288]{1,0:T(8,128)S(1)}) custom-call(f32[288,128]{1,0:T(8,128)S(1)} %get-tuple-element.136.left_ref, f32[288,128]{1,0:T(8,128)S(1)} %get-tuple-element.137.rest_ref), custom_call_target="tpu_custom_call" | custom-call | flops 6000000000 | bytes 1000000 | tf_op jit(solution)/shard_map/orth_second/pallas_call | solution.py:190
  82.7 5.3 %collective-permute-done.24.refs_0_.refs_6_ = f32[544,128]{1,0:T(8,128)S(1)} collective-permute-done((f32[544,128]{1,0:T(8,128)S(1)}, f32[544,128]{1,0:T(8,128)S(1)}, u32[]{:S(2)}, u32[]{:S(2)}) %collective-permute-start.24) | collective-permute-done | bytes 278560 | tf_op jit(solution)/shard_map/ppermute | solution.py:692
  91.9 3.5 %collective-permute-done.26.refs_2_ = f32[80,256]{1,0:T(8,128)S(1)} collective-permute-done((f32[80,256]{1,0:T(8,128)S(1)}, f32[80,256]{1,0:T(8,128)S(1)}, u32[]{:S(2)}, u32[]{:S(2)}) %collective-permute-start.26) | collective-permute-done | bytes 81952 | tf_op jit(solution)/shard_map/ppermute | solution.py:642
  101.8 6.6 %collective-permute-done.31.refs_3_ = f32[80,256]{1,0:T(8,128)S(1)} collective-permute-done((f32[80,256]{1,0:T(8,128)S(1)}, f32[80,256]{1,0:T(8,128)S(1)}, u32[]{:S(2)}, u32[]{:S(2)}) %collective-permute-start.31) | collective-permute-done | bytes 81952 | tf_op jit(solution)/shard_map/ppermute | solution.py:642
  112.0 8.6 %collective-permute-done.33.refs_1_ = f32[80,256]{1,0:T(8,128)S(1)} collective-permute-done((f32[80,256]{1,0:T(8,128)S(1)}, f32[80,256]{1,0:T(8,128)S(1)}, u32[]{:S(2)}, u32[]{:S(2)}) %collective-permute-start.33) | collective-permute-done | bytes 81952 | tf_op jit(solution)/shard_map/ppermute | solution.py:642
  122.5 2.0 %collective-permute-start.44 = (f32[544,128]{1,0:T(8,128)S(1)}, f32[544,128]{1,0:T(8,128)S(1)}, u32[]{:S(2)}, u32[]{:S(2)}) collective-permute-start(f32[544,128]{1,0:T(8,128)S(1)} %collective-permute-done.43.refs_9_.refs_11_), channel_id=1, source_target_pairs={{8,0},{16,8},{24,16},{28,24},{20,28},{12,20},{4,12},{0,4},{9,1},{1... | collective-permute-start | bytes 835592 | tf_op jit(solution)/shard_map/ppermute | solution.py:693
  126.5 6.3 %orth_first.3 = (f32[288,128]{1,0:T(8,128)S(1)}, f32[288,128]{1,0:T(8,128)S(1)}, f32[1,256]{1,0:T(1,128)S(1)}) custom-call(s32[1]{0:T(128)} %bitcast.1.me_ref, f32[80,256]{1,0:T(8,128)S(1)} %alike.13.refs_0_, f32[80,256]{1,0:T(8,128)S(1)} %collective-permute-done.35.refs_1_, f32[80,256]{1,0:T(8,128)S(1)} %collective-permute-done.36.refs_2_, ...), custom_call_target="tpu_custom_call" | custom-call | flops 6000000000 | bytes 1000000 | tf_op jit(solution)/shard_map/orth_first/pallas_call | solution.py:176
  132.8 2.0 %collective-permute-start.45 = (f32[544,128]{1,0:T(8,128)S(1)}, f32[544,128]{1,0:T(8,128)S(1)}, u32[]{:S(2)}, u32[]{:S(2)}) collective-permute-start(f32[544,128]{1,0:T(8,128)S(1)} %collective-permute-done.44.refs_8_.refs_10_), channel_id=1, source_target_pairs={{8,0},{16,8},{24,16},{28,24},{20,28},{12,20},{4,12},{0,4},{9,1},{1... | collective-permute-start | bytes 835592 | tf_op jit(solution)/shard_map/ppermute | solution.py:693
  134.8 5.5 %orth_second.3 = (f32[288,256]{1,0:T(8,128)S(1)}, f32[256,288]{1,0:T(8,128)S(1)}) custom-call(f32[288,128]{1,0:T(8,128)S(1)} %get-tuple-element.166.left_ref, f32[288,128]{1,0:T(8,128)S(1)} %get-tuple-element.167.rest_ref), custom_call_target="tpu_custom_call" | custom-call | flops 6000000000 | bytes 1000000 | tf_op jit(solution)/shard_map/orth_second/pallas_call | solution.py:190
  143.8 8.2 %shard_map.67 = (f32[1,288,2048]{2,1,0:T(8,128)}, f32[6,256,256]{2,1,0:T(8,128)S(1)}, f32[8,256]{1,0:T(8,128)S(1)}) custom-call(s32[1]{0:T(128)} %bitcast.place_ref.at_ref.order_ref, f32[544,128]{1,0:T(8,128)S(1)} %get-tuple-element.147.up_ref.refs_0_, f32[544,128]{1,0:T(8,128)S(1)} %collective-permute-done.28.refs_1_, ...), custom_call_target="tpu_custom_call" | custom-call | flops 2264924160 | bytes 10616832 | tf_op jit(solution)/shard_map/pallas_call | solution.py:561
  157.5 5.8 %finish.1 = (f32[288,2048]{1,0:T(8,128)}, f32[2048,256]{1,0:T(8,128)}) custom-call(s32[1]{0:T(128)} %bitcast.place_ref.at_ref.order_ref, f32[544,128]{1,0:T(8,128)S(1)} %get-tuple-element.147.up_ref.refs_0_, f32[544,128]{1,0:T(8,128)S(1)} %collective-permute-done.28.refs_1_, f32[544,128]{1,0:T(8,128)S(1)} %collective-permute-done.32.refs_2_, ...), custom_call_target="tpu_custom_call" | custom-call | flops 1811939328 | bytes 18874368 | tf_op jit(solution)/shard_map/finish/pallas_call | solution.py:611
  (116 shorter events, 49.2 us)
Async XLA Ops:
  2.8 10.3 %collective-permute-start = (f32[576,128]{1,0:T(8,128)}, f32[576,128]{1,0:T(8,128)S(1)}, u32[]{:S(2)}, u32[]{:S(2)}) collective-permute-start(f32[576,128]{1,0:T(8,128)} %get-tuple-element.102), channel_id=1, source_target_pairs={{0,8},{8,16},{16,24},{24,28},{28,20},{20,12},{12,4},{4,0},{1,9},{9... | collective-permute-start | bytes 884744 | tf_op jit(solution)/shard_map/ppermute | solution.py:692
  29.6 13.9 %collective-permute-start.9 = (f32[576,128]{1,0:T(8,128)S(1)}, f32[576,128]{1,0:T(8,128)S(1)}, u32[]{:S(2)}, u32[]{:S(2)}) collective-permute-start(f32[576,128]{1,0:T(8,128)S(1)} %ring_add.14), channel_id=1, source_target_pairs={{0,8},{8,16},{16,24},{24,28},{28,20},{20,12},{12,4},{4,0},{1,9},{9... | collective-permute-start | bytes 884744 | tf_op jit(solution)/shard_map/ppermute | solution.py:692
  31.3 12.7 %collective-permute-start.20 = (f32[576,128]{1,0:T(8,128)S(1)}, f32[576,128]{1,0:T(8,128)S(1)}, u32[]{:S(2)}, u32[]{:S(2)}) collective-permute-start(f32[576,128]{1,0:T(8,128)S(1)} %ring_add.20), channel_id=1, source_target_pairs={{8,0},{16,8},{24,16},{28,24},{20,28},{12,20},{4,12},{0,4},{9,1},{1... | collective-permute-start | bytes 884744 | tf_op jit(solution)/shard_map/ppermute | solution.py:693
  31.8 10.3 %collective-permute-start.8 = (f32[72,256]{1,0:T(8,128)S(1)}, f32[72,256]{1,0:T(8,128)S(1)}, u32[]{:S(2)}, u32[]{:S(2)}) collective-permute-start(f32[72,256]{1,0:T(8,128)S(1)} %alike.8.refs_0_), channel_id=1, source_target_pairs={{0,12},{4,8},{8,4},{12,0},{16,28},{20,24},{24,20},{28,16},{1,13},{... | collective-permute-start | bytes 221192 | tf_op jit(solution)/shard_map/ppermute | solution.py:642
  34.3 9.1 %collective-permute-start.7 = (f32[72,256]{1,0:T(8,128)S(1)}, f32[72,256]{1,0:T(8,128)S(1)}, u32[]{:S(2)}, u32[]{:S(2)}) collective-permute-start(f32[72,256]{1,0:T(8,128)S(1)} %alike.8.refs_0_), channel_id=1, source_target_pairs={{0,8},{4,12},{8,0},{12,4},{16,24},{20,28},{24,16},{28,20},{1,9},{5... | collective-permute-start | bytes 221192 | tf_op jit(solution)/shard_map/ppermute | solution.py:642
  43.5 15.6 %collective-permute-start.11 = (f32[576,128]{1,0:T(8,128)S(1)}, f32[576,128]{1,0:T(8,128)S(1)}, u32[]{:S(2)}, u32[]{:S(2)}) collective-permute-start(f32[576,128]{1,0:T(8,128)S(1)} %ring_add.15), channel_id=1, source_target_pairs={{0,8},{8,16},{16,24},{24,28},{28,20},{20,12},{12,4},{4,0},{1,9},{9... | collective-permute-start | bytes 884744 | tf_op jit(solution)/shard_map/ppermute | solution.py:692
  44.0 15.2 %collective-permute-start.21 = (f32[576,128]{1,0:T(8,128)S(1)}, f32[576,128]{1,0:T(8,128)S(1)}, u32[]{:S(2)}, u32[]{:S(2)}) collective-permute-start(f32[576,128]{1,0:T(8,128)S(1)} %ring_add.21), channel_id=1, source_target_pairs={{8,0},{16,8},{24,16},{28,24},{20,28},{12,20},{4,12},{0,4},{9,1},{1... | collective-permute-start | bytes 884744 | tf_op jit(solution)/shard_map/ppermute | solution.py:693
  45.7 11.2 %collective-permute-start.10 = (f32[72,256]{1,0:T(8,128)S(1)}, f32[72,256]{1,0:T(8,128)S(1)}, u32[]{:S(2)}, u32[]{:S(2)}) collective-permute-start(f32[72,256]{1,0:T(8,128)S(1)} %alike.9.refs_0_), channel_id=1, source_target_pairs={{0,16},{4,20},{8,24},{12,28},{16,0},{20,4},{24,8},{28,12},{1,17},{... | collective-permute-start | bytes 221192 | tf_op jit(solution)/shard_map/ppermute | solution.py:642
  59.2 10.0 %collective-permute-start.15 = (f32[576,128]{1,0:T(8,128)S(1)}, f32[576,128]{1,0:T(8,128)S(1)}, u32[]{:S(2)}, u32[]{:S(2)}) collective-permute-start(f32[576,128]{1,0:T(8,128)S(1)} %ring_add.16), channel_id=1, source_target_pairs={{0,8},{8,16},{16,24},{24,28},{28,20},{20,12},{12,4},{4,0},{1,9},{9... | collective-permute-start | bytes 884744 | tf_op jit(solution)/shard_map/ppermute | solution.py:692
  59.3 10.0 %collective-permute-start.22 = (f32[576,128]{1,0:T(8,128)S(1)}, f32[576,128]{1,0:T(8,128)S(1)}, u32[]{:S(2)}, u32[]{:S(2)}) collective-permute-start(f32[576,128]{1,0:T(8,128)S(1)} %ring_add.22), channel_id=1, source_target_pairs={{8,0},{16,8},{24,16},{28,24},{20,28},{12,20},{4,12},{0,4},{9,1},{1... | collective-permute-start | bytes 884744 | tf_op jit(solution)/shard_map/ppermute | solution.py:693
  69.3 9.3 %collective-permute-start.16 = (f32[576,128]{1,0:T(8,128)S(1)}, f32[576,128]{1,0:T(8,128)S(1)}, u32[]{:S(2)}, u32[]{:S(2)}) collective-permute-start(f32[576,128]{1,0:T(8,128)S(1)} %ring_add.17), channel_id=1, source_target_pairs={{0,8},{8,16},{16,24},{24,28},{28,20},{20,12},{12,4},{4,0},{1,9},{9... | collective-permute-start | bytes 884744 | tf_op jit(solution)/shard_map/ppermute | solution.py:692
  69.4 9.4 %collective-permute-start.23 = (f32[576,128]{1,0:T(8,128)S(1)}, f32[576,128]{1,0:T(8,128)S(1)}, u32[]{:S(2)}, u32[]{:S(2)}) collective-permute-start(f32[576,128]{1,0:T(8,128)S(1)} %ring_add.23), channel_id=1, source_target_pairs={{8,0},{16,8},{24,16},{28,24},{20,28},{12,20},{4,12},{0,4},{9,1},{1... | collective-permute-start | bytes 884744 | tf_op jit(solution)/shard_map/ppermute | solution.py:693
  96.2 12.5 %collective-permute-start.32 = (f32[544,128]{1,0:T(8,128)S(1)}, f32[544,128]{1,0:T(8,128)S(1)}, u32[]{:S(2)}, u32[]{:S(2)}) collective-permute-start(f32[544,128]{1,0:T(8,128)S(1)} %collective-permute-done.28.refs_1_), channel_id=1, source_target_pairs={{0,8},{8,16},{16,24},{24,28},{28,20},{20,12},{12,4},{4,0},{1,9},{9... | collective-permute-start | bytes 835592 | tf_op jit(solution)/shard_map/ppermute | solution.py:692
  96.5 13.9 %collective-permute-start.42 = (f32[544,128]{1,0:T(8,128)S(1)}, f32[544,128]{1,0:T(8,128)S(1)}, u32[]{:S(2)}, u32[]{:S(2)}) collective-permute-start(f32[544,128]{1,0:T(8,128)S(1)} %collective-permute-done.41.refs_11_.refs_13_), channel_id=1, source_target_pairs={{8,0},{16,8},{24,16},{28,24},{20,28},{12,20},{4,12},{0,4},{9,1},{1... | collective-permute-start | bytes 835592 | tf_op jit(solution)/shard_map/ppermute | solution.py:693
  98.3 10.1 %collective-permute-start.31 = (f32[80,256]{1,0:T(8,128)S(1)}, f32[80,256]{1,0:T(8,128)S(1)}, u32[]{:S(2)}, u32[]{:S(2)}) collective-permute-start(f32[80,256]{1,0:T(8,128)S(1)} %alike.11.refs_0_), channel_id=1, source_target_pairs={{0,12},{4,8},{8,4},{12,0},{16,28},{20,24},{24,20},{28,16},{1,13},{... | collective-permute-start | bytes 245768 | tf_op jit(solution)/shard_map/ppermute | solution.py:642
  108.7 13.8 %collective-permute-start.34 = (f32[544,128]{1,0:T(8,128)S(1)}, f32[544,128]{1,0:T(8,128)S(1)}, u32[]{:S(2)}, u32[]{:S(2)}) collective-permute-start(f32[544,128]{1,0:T(8,128)S(1)} %collective-permute-done.32.refs_2_), channel_id=1, source_target_pairs={{0,8},{8,16},{16,24},{24,28},{28,20},{20,12},{12,4},{4,0},{1,9},{9... | collective-permute-start | bytes 835592 | tf_op jit(solution)/shard_map/ppermute | solution.py:692
  110.5 12.0 %collective-permute-start.43 = (f32[544,128]{1,0:T(8,128)S(1)}, f32[544,128]{1,0:T(8,128)S(1)}, u32[]{:S(2)}, u32[]{:S(2)}) collective-permute-start(f32[544,128]{1,0:T(8,128)S(1)} %collective-permute-done.42.refs_10_.refs_12_), channel_id=1, source_target_pairs={{8,0},{16,8},{24,16},{28,24},{20,28},{12,20},{4,12},{0,4},{9,1},{1... | collective-permute-start | bytes 835592 | tf_op jit(solution)/shard_map/ppermute | solution.py:693
  110.8 9.7 %collective-permute-start.33 = (f32[80,256]{1,0:T(8,128)S(1)}, f32[80,256]{1,0:T(8,128)S(1)}, u32[]{:S(2)}, u32[]{:S(2)}) collective-permute-start(f32[80,256]{1,0:T(8,128)S(1)} %alike.12.refs_0_), channel_id=1, source_target_pairs={{0,16},{4,20},{8,24},{12,28},{16,0},{20,4},{24,8},{28,12},{1,17},{... | collective-permute-start | bytes 245768 | tf_op jit(solution)/shard_map/ppermute | solution.py:642
  122.5 10.2 %collective-permute-start.38 = (f32[544,128]{1,0:T(8,128)S(1)}, f32[544,128]{1,0:T(8,128)S(1)}, u32[]{:S(2)}, u32[]{:S(2)}) collective-permute-start(f32[544,128]{1,0:T(8,128)S(1)} %collective-permute-done.34.refs_3_), channel_id=1, source_target_pairs={{0,8},{8,16},{16,24},{24,28},{28,20},{20,12},{12,4},{4,0},{1,9},{9... | collective-permute-start | bytes 835592 | tf_op jit(solution)/shard_map/ppermute | solution.py:692
  122.5 10.3 %collective-permute-start.44 = (f32[544,128]{1,0:T(8,128)S(1)}, f32[544,128]{1,0:T(8,128)S(1)}, u32[]{:S(2)}, u32[]{:S(2)}) collective-permute-start(f32[544,128]{1,0:T(8,128)S(1)} %collective-permute-done.43.refs_9_.refs_11_), channel_id=1, source_target_pairs={{8,0},{16,8},{24,16},{28,24},{20,28},{12,20},{4,12},{0,4},{9,1},{1... | collective-permute-start | bytes 835592 | tf_op jit(solution)/shard_map/ppermute | solution.py:693
  132.7 9.1 %collective-permute-start.39 = (f32[544,128]{1,0:T(8,128)S(1)}, f32[544,128]{1,0:T(8,128)S(1)}, u32[]{:S(2)}, u32[]{:S(2)}) collective-permute-start(f32[544,128]{1,0:T(8,128)S(1)} %collective-permute-done.38.refs_4_), channel_id=1, source_target_pairs={{0,8},{8,16},{16,24},{24,28},{28,20},{20,12},{12,4},{4,0},{1,9},{9... | collective-permute-start | bytes 835592 | tf_op jit(solution)/shard_map/ppermute | solution.py:692
  132.8 9.3 %collective-permute-start.45 = (f32[544,128]{1,0:T(8,128)S(1)}, f32[544,128]{1,0:T(8,128)S(1)}, u32[]{:S(2)}, u32[]{:S(2)}) collective-permute-start(f32[544,128]{1,0:T(8,128)S(1)} %collective-permute-done.44.refs_8_.refs_10_), channel_id=1, source_target_pairs={{8,0},{16,8},{24,16},{28,24},{20,28},{12,20},{4,12},{0,4},{9,1},{1... | collective-permute-start | bytes 835592 | tf_op jit(solution)/shard_map/ppermute | solution.py:693
  141.8 10.2 %collective-permute-start.46 = (f32[544,128]{1,0:T(8,128)S(1)}, f32[544,128]{1,0:T(8,128)S(1)}, u32[]{:S(2)}, u32[]{:S(2)}) collective-permute-start(f32[544,128]{1,0:T(8,128)S(1)} %collective-permute-done.39.refs_5_), channel_id=1, source_target_pairs={{0,8},{8,16},{16,24},{24,28},{28,20},{20,12},{12,4},{4,0},{1,9},{9... | collective-permute-start | bytes 835592 | tf_op jit(solution)/shard_map/ppermute | solution.py:692
  142.1 10.0 %collective-permute-start.47 = (f32[544,128]{1,0:T(8,128)S(1)}, f32[544,128]{1,0:T(8,128)S(1)}, u32[]{:S(2)}, u32[]{:S(2)}) collective-permute-start(f32[544,128]{1,0:T(8,128)S(1)} %collective-permute-done.45.refs_7_.refs_9_), channel_id=1, source_target_pairs={{8,0},{16,8},{24,16},{28,24},{20,28},{12,20},{4,12},{0,4},{9,1},{1... | collective-permute-start | bytes 835592 | tf_op jit(solution)/shard_map/ppermute | solution.py:693
  (30 other events, 181.5 us)

commit v8 on v7

--- a/solution.py
+++ b/solution.py
@@ -642,13 +642,14 @@
     return lax.ppermute(x, axis, [(i, i ^ bits) for i in range(size)])
 
 
-def rep_masks(reps):
-    return [[1, 2, 3]] + [[1 << b] for b in range(2, reps.bit_length() - 1)]
-
-
-def all_sum_stages(box):
+def rep_masks(reps, phase):
+    single = [[1 << b] for b in range(reps.bit_length() - 1)]
+    return single if phase == "reduce" else [[1, 2, 3]] + single[2:]
+
+
+def all_sum_stages(box, phase):
     cols = lax.axis_size("col")
-    masks = rep_masks(lax.axis_size("rep"))
+    masks = rep_masks(lax.axis_size("rep"), phase)
 
     def send(x, axis, partners):
         return [flip(part, axis, p) for part, p in zip(x, partners)]
@@ -703,7 +704,7 @@
         return stage
 
     box = {}
-    stages = all_sum_stages(box)
+    stages = all_sum_stages(box, "reduce")
 
     def begin():
         out = combine(me, momentum, grads, right_factor, n, count)
@@ -713,7 +714,7 @@
     def second():
         box["left"], box["leftt"] = orth_second(box.pop("left"), box.pop("rest"))
 
-    work = [[begin]] + [[stage] for stage in stages] + [[first(False)], [second]]
+    work = [[begin], stages[:2]] + [[stage] for stage in stages[2:]] + [[first(False)], [second]]
     up, dn = lead(place, momentum, grads, n)
     for k in range(1, n):
         up, dn = step(up, dn)
@@ -730,7 +731,7 @@
 
     box = {}
     mine = (up, dn)
-    stages = all_sum_stages(box)
+    stages = all_sum_stages(box, "gather")
 
     def begin_again():
         box["parts"] = list(partial_raw(me, *mine, rank, count))

time: 164 us -> 164 us (level)
    ppermute x14, waiting for transfers between devices: 15.3 us -> 9.38 us  [step(): up = lax.ppermute(up, 'rep', ahead)]
    ppermute x23 -> x22, waiting for transfers between devices: 44.3 us -> 49.6 us  [flip(): return lax.ppermute(x, axis, [(i, i ^ bits) for i in range(size)])]
    ppermute x23 -> x22, starting transfers between devices: 20.5 us -> 20.9 us  [flip(): return lax.ppermute(x, axis, [(i, i ^ bits) for i in range(size)])]
  transfers between devices with their start and end apart: 51 -> 50, of which waited for: 19 -> 19; matrix products, arithmetic and copies ran while one was open for 0% -> 0% of each run, Pallas kernels for 25% -> 25%
where the time goes in v8:
time: 164 us; the launch traced here: 163 us
  waiting for transfers between devices  59.3 us (36%)
  Pallas kernels  51.4 us (31%)
  starting transfers between devices  51.3 us (31%)
    ppermute x22, waiting for transfers between devices, flip(): return lax.ppermute(x, axis, [(i, i ^ bits) for i in range(size)])  49.6 us
    ppermute x22, starting transfers between devices, flip(): return lax.ppermute(x, axis, [(i, i ^ bits) for i in range(size)])  20.9 us
    ppermute x14, starting transfers between devices, step(): dn = lax.ppermute(dn, 'rep', back)  20.1 us
    pallas_call x2, Pallas kernels, orth_first(): pl.pallas_call(functools.partial(first_kernel, scaled), out_shape=shapes,...  12.5 us
    pallas_call x3, Pallas kernels, advance(): pl.pallas_call(functools.partial(kernel, m), out_shape=outs, grid_spec=pl...  11.5 us
    pallas_call x2, Pallas kernels, orth_second(): pl.pallas_call(second_kernel, out_shape=[jax.ShapeDtypeStruct((rows, rank...  11 us
    ppermute x14, starting transfers between devices, step(): up = lax.ppermute(up, 'rep', ahead)  10.3 us
    ppermute x14, waiting for transfers between devices, step(): up = lax.ppermute(up, 'rep', ahead)  9.38 us
  transfers between devices with their start and end apart: 50, of which 19 were waited for; matrix products, arithmetic and copies ran while one was open for 0% of the time, Pallas kernels for 25%

profile of v8, /device:TPU:0, one launch (start us, length us, event | category | flops | bytes accessed | tf_op | source)
XLA Modules:
  0.0 163.3 jit_solution(6596815367812405437)
XLA Ops:
  0.7 2.1 %lead.1 = (f32[576,128]{1,0:T(8,128)}, f32[576,128]{1,0:T(8,128)}) custom-call(s32[1]{0:T(128)} %bitcast.place_ref.at_ref.order_ref, f32[1,288,2048]{2,1,0:T(8,128)} %mom.1, bf16[2,1,288,2048]{3,2,1,0:T(8,128)(2,1)} %grads.1), custom_call_target="tpu_custom_call" | custom-call | flops 147456 | bytes 1179648 | tf_op jit(solution)/shard_map/lead/pallas_call | solution.py:233
  2.8 3.1 %collective-permute-start = (f32[576,128]{1,0:T(8,128)}, f32[576,128]{1,0:T(8,128)S(1)}, u32[]{:S(2)}, u32[]{:S(2)}) collective-permute-start(f32[576,128]{1,0:T(8,128)} %get-tuple-element.102), channel_id=1, source_target_pairs={{0,8},{8,16},{16,24},{24,28},{28,20},{20,12},{12,4},{4,0},{1,9},{9... | collective-permute-start | bytes 884744 | tf_op jit(solution)/shard_map/ppermute | solution.py:693
  5.9 6.2 %combine.1 = (f32[8,576,128]{2,1,0:T(8,128)S(1)}, f32[8,576,128]{2,1,0:T(8,128)S(1)}, f32[1,288,2048]{2,1,0:T(8,128)}, f32[72,256]{1,0:T(8,128)S(1)}, f32[72,256...) custom-call(s32[1]{0:T(128)} %bitcast.1.me_ref, f32[1,288,2048]{2,1,0:T(8,128)} %mom.1, ...), custom_call_target="tpu_custom_call" | custom-call | flops 1811939328 | bytes 16515072 | tf_op jit(solution)/shard_map/combine/pallas_call | solution.py:288
  17.1 2.8 %collective-permute-done.2.refs_2_ = f32[72,256]{1,0:T(8,128)S(1)} collective-permute-done((f32[72,256]{1,0:T(8,128)S(1)}, f32[72,256]{1,0:T(8,128)S(1)}, u32[]{:S(2)}, u32[]{:S(2)}) %collective-permute-start.2) | collective-permute-done | bytes 73760 | tf_op jit(solution)/shard_map/ppermute | solution.py:642
  25.3 7.0 %collective-permute-done.5.refs_1_ = f32[72,256]{1,0:T(8,128)S(1)} collective-permute-done((f32[72,256]{1,0:T(8,128)S(1)}, f32[72,256]{1,0:T(8,128)S(1)}, u32[]{:S(2)}, u32[]{:S(2)}) %collective-permute-start.5) | collective-permute-done | bytes 73760 | tf_op jit(solution)/shard_map/ppermute | solution.py:642
  32.6 1.9 %collective-permute-start.19 = (f32[576,128]{1,0:T(8,128)S(1)}, f32[576,128]{1,0:T(8,128)S(1)}, u32[]{:S(2)}, u32[]{:S(2)}) collective-permute-start(f32[576,128]{1,0:T(8,128)S(1)} %ring_add.20), channel_id=1, source_target_pairs={{8,0},{16,8},{24,16},{28,24},{20,28},{12,20},{4,12},{0,4},{9,1},{1... | collective-permute-start | bytes 884744 | tf_op jit(solution)/shard_map/ppermute | solution.py:694
  34.7 7.9 %collective-permute-done.7.refs_1_ = f32[72,256]{1,0:T(8,128)S(1)} collective-permute-done((f32[72,256]{1,0:T(8,128)S(1)}, f32[72,256]{1,0:T(8,128)S(1)}, u32[]{:S(2)}, u32[]{:S(2)}) %collective-permute-start.7) | collective-permute-done | bytes 73760 | tf_op jit(solution)/shard_map/ppermute | solution.py:642
  44.8 4.6 %collective-permute-start.9 = (f32[72,256]{1,0:T(8,128)S(1)}, f32[72,256]{1,0:T(8,128)S(1)}, u32[]{:S(2)}, u32[]{:S(2)}) collective-permute-start(f32[72,256]{1,0:T(8,128)S(1)} %alike.11.refs_0_), channel_id=1, source_target_pairs={{0,16},{4,20},{8,24},{12,28},{16,0},{20,4},{24,8},{28,12},{1,17},{... | collective-permute-start | bytes 221192 | tf_op jit(solution)/shard_map/ppermute | solution.py:642
  49.4 7.6 %collective-permute-done.9.refs_1_ = f32[72,256]{1,0:T(8,128)S(1)} collective-permute-done((f32[72,256]{1,0:T(8,128)S(1)}, f32[72,256]{1,0:T(8,128)S(1)}, u32[]{:S(2)}, u32[]{:S(2)}) %collective-permute-start.9) | collective-permute-done | bytes 73760 | tf_op jit(solution)/shard_map/ppermute | solution.py:642
  57.1 2.0 %collective-permute-start.12 = (f32[72,256]{1,0:T(8,128)S(1)}, f32[72,256]{1,0:T(8,128)S(1)}, u32[]{:S(2)}, u32[]{:S(2)}) collective-permute-start(f32[72,256]{1,0:T(8,128)S(1)} %alike.12.refs_0_), channel_id=1, source_target_pairs={{0,2},{1,3},{2,0},{3,1},{4,6},{5,7},{6,4},{7,5},{8,10},{9,11},{10,... | collective-permute-start | bytes 221192 | tf_op jit(solution)/shard_map/ppermute | solution.py:642
  59.4 2.0 %collective-permute-start.21 = (f32[576,128]{1,0:T(8,128)S(1)}, f32[576,128]{1,0:T(8,128)S(1)}, u32[]{:S(2)}, u32[]{:S(2)}) collective-permute-start(f32[576,128]{1,0:T(8,128)S(1)} %ring_add.22), channel_id=1, source_target_pairs={{8,0},{16,8},{24,16},{28,24},{20,28},{12,20},{4,12},{0,4},{9,1},{1... | collective-permute-start | bytes 884744 | tf_op jit(solution)/shard_map/ppermute | solution.py:694
  63.2 6.2 %orth_first.2 = (f32[288,128]{1,0:T(8,128)S(1)}, f32[288,128]{1,0:T(8,128)S(1)}) custom-call(s32[1]{0:T(128)} %bitcast.1.me_ref, f32[72,256]{1,0:T(8,128)S(1)} %alike.12.refs_0_, f32[72,256]{1,0:T(8,128)S(1)} %collective-permute-done.11.refs_1_, f32[72,256]{1,0:T(8,128)S(1)} %collective-permute-done.12.refs_2_, f32[72,256]{1,0:T(8,128)S(1)} %collective-permute-done.13.refs_3_), custom_call_target="tpu_custom_call" | custom-call | flops 6000000000 | bytes 1000000 | tf_op jit(solution)/shard_map/orth_first/pallas_call | solution.py:176
  69.6 2.2 %collective-permute-start.22 = (f32[576,128]{1,0:T(8,128)S(1)}, f32[576,128]{1,0:T(8,128)S(1)}, u32[]{:S(2)}, u32[]{:S(2)}) collective-permute-start(f32[576,128]{1,0:T(8,128)S(1)} %ring_add.23), channel_id=1, source_target_pairs={{8,0},{16,8},{24,16},{28,24},{20,28},{12,20},{4,12},{0,4},{9,1},{1... | collective-permute-start | bytes 884744 | tf_op jit(solution)/shard_map/ppermute | solution.py:694
  71.9 5.5 %orth_second.2 = (f32[288,256]{1,0:T(8,128)S(1)}, f32[256,288]{1,0:T(8,128)S(1)}) custom-call(f32[288,128]{1,0:T(8,128)S(1)} %get-tuple-element.136.left_ref, f32[288,128]{1,0:T(8,128)S(1)} %get-tuple-element.137.rest_ref), custom_call_target="tpu_custom_call" | custom-call | flops 6000000000 | bytes 1000000 | tf_op jit(solution)/shard_map/orth_second/pallas_call | solution.py:190
  82.8 5.2 %collective-permute-done.23.refs_0_.refs_6_ = f32[544,128]{1,0:T(8,128)S(1)} collective-permute-done((f32[544,128]{1,0:T(8,128)S(1)}, f32[544,128]{1,0:T(8,128)S(1)}, u32[]{:S(2)}, u32[]{:S(2)}) %collective-permute-start.23) | collective-permute-done | bytes 278560 | tf_op jit(solution)/shard_map/ppermute | solution.py:693
  91.9 3.5 %collective-permute-done.25.refs_2_ = f32[80,256]{1,0:T(8,128)S(1)} collective-permute-done((f32[80,256]{1,0:T(8,128)S(1)}, f32[80,256]{1,0:T(8,128)S(1)}, u32[]{:S(2)}, u32[]{:S(2)}) %collective-permute-start.25) | collective-permute-done | bytes 81952 | tf_op jit(solution)/shard_map/ppermute | solution.py:642
  101.8 6.6 %collective-permute-done.30.refs_3_ = f32[80,256]{1,0:T(8,128)S(1)} collective-permute-done((f32[80,256]{1,0:T(8,128)S(1)}, f32[80,256]{1,0:T(8,128)S(1)}, u32[]{:S(2)}, u32[]{:S(2)}) %collective-permute-start.30) | collective-permute-done | bytes 81952 | tf_op jit(solution)/shard_map/ppermute | solution.py:642
  112.0 8.5 %collective-permute-done.32.refs_1_ = f32[80,256]{1,0:T(8,128)S(1)} collective-permute-done((f32[80,256]{1,0:T(8,128)S(1)}, f32[80,256]{1,0:T(8,128)S(1)}, u32[]{:S(2)}, u32[]{:S(2)}) %collective-permute-start.32) | collective-permute-done | bytes 81952 | tf_op jit(solution)/shard_map/ppermute | solution.py:642
  122.5 2.0 %collective-permute-start.43 = (f32[544,128]{1,0:T(8,128)S(1)}, f32[544,128]{1,0:T(8,128)S(1)}, u32[]{:S(2)}, u32[]{:S(2)}) collective-permute-start(f32[544,128]{1,0:T(8,128)S(1)} %collective-permute-done.42.refs_9_.refs_11_), channel_id=1, source_target_pairs={{8,0},{16,8},{24,16},{28,24},{20,28},{12,20},{4,12},{0,4},{9,1},{1... | collective-permute-start | bytes 835592 | tf_op jit(solution)/shard_map/ppermute | solution.py:694
  126.1 6.3 %orth_first.3 = (f32[288,128]{1,0:T(8,128)S(1)}, f32[288,128]{1,0:T(8,128)S(1)}, f32[1,256]{1,0:T(1,128)S(1)}) custom-call(s32[1]{0:T(128)} %bitcast.1.me_ref, f32[80,256]{1,0:T(8,128)S(1)} %alike.15.refs_0_, f32[80,256]{1,0:T(8,128)S(1)} %collective-permute-done.34.refs_1_, f32[80,256]{1,0:T(8,128)S(1)} %collective-permute-done.35.refs_2_, ...), custom_call_target="tpu_custom_call" | custom-call | flops 6000000000 | bytes 1000000 | tf_op jit(solution)/shard_map/orth_first/pallas_call | solution.py:176
  132.5 2.0 %collective-permute-start.44 = (f32[544,128]{1,0:T(8,128)S(1)}, f32[544,128]{1,0:T(8,128)S(1)}, u32[]{:S(2)}, u32[]{:S(2)}) collective-permute-start(f32[544,128]{1,0:T(8,128)S(1)} %collective-permute-done.43.refs_8_.refs_10_), channel_id=1, source_target_pairs={{8,0},{16,8},{24,16},{28,24},{20,28},{12,20},{4,12},{0,4},{9,1},{1... | collective-permute-start | bytes 835592 | tf_op jit(solution)/shard_map/ppermute | solution.py:694
  134.5 5.5 %orth_second.3 = (f32[288,256]{1,0:T(8,128)S(1)}, f32[256,288]{1,0:T(8,128)S(1)}) custom-call(f32[288,128]{1,0:T(8,128)S(1)} %get-tuple-element.166.left_ref, f32[288,128]{1,0:T(8,128)S(1)} %get-tuple-element.167.rest_ref), custom_call_target="tpu_custom_call" | custom-call | flops 6000000000 | bytes 1000000 | tf_op jit(solution)/shard_map/orth_second/pallas_call | solution.py:190
  143.7 8.2 %shard_map.67 = (f32[1,288,2048]{2,1,0:T(8,128)}, f32[6,256,256]{2,1,0:T(8,128)S(1)}, f32[8,256]{1,0:T(8,128)S(1)}) custom-call(s32[1]{0:T(128)} %bitcast.place_ref.at_ref.order_ref, f32[544,128]{1,0:T(8,128)S(1)} %get-tuple-element.147.up_ref.refs_0_, f32[544,128]{1,0:T(8,128)S(1)} %collective-permute-done.27.refs_1_, ...), custom_call_target="tpu_custom_call" | custom-call | flops 2264924160 | bytes 10616832 | tf_op jit(solution)/shard_map/pallas_call | solution.py:561
  157.3 5.8 %finish.1 = (f32[288,2048]{1,0:T(8,128)}, f32[2048,256]{1,0:T(8,128)}) custom-call(s32[1]{0:T(128)} %bitcast.place_ref.at_ref.order_ref, f32[544,128]{1,0:T(8,128)S(1)} %get-tuple-element.147.up_ref.refs_0_, f32[544,128]{1,0:T(8,128)S(1)} %collective-permute-done.27.refs_1_, f32[544,128]{1,0:T(8,128)S(1)} %collective-permute-done.31.refs_2_, ...), custom_call_target="tpu_custom_call" | custom-call | flops 1811939328 | bytes 18874368 | tf_op jit(solution)/shard_map/finish/pallas_call | solution.py:611
  (115 shorter events, 47.1 us)
Async XLA Ops:
  2.8 10.3 %collective-permute-start = (f32[576,128]{1,0:T(8,128)}, f32[576,128]{1,0:T(8,128)S(1)}, u32[]{:S(2)}, u32[]{:S(2)}) collective-permute-start(f32[576,128]{1,0:T(8,128)} %get-tuple-element.102), channel_id=1, source_target_pairs={{0,8},{8,16},{16,24},{24,28},{28,20},{20,12},{12,4},{4,0},{1,9},{9... | collective-permute-start | bytes 884744 | tf_op jit(solution)/shard_map/ppermute | solution.py:693
  21.4 11.0 %collective-permute-start.6 = (f32[576,128]{1,0:T(8,128)S(1)}, f32[576,128]{1,0:T(8,128)S(1)}, u32[]{:S(2)}, u32[]{:S(2)}) collective-permute-start(f32[576,128]{1,0:T(8,128)S(1)} %ring_add.13), channel_id=1, source_target_pairs={{0,8},{8,16},{16,24},{24,28},{28,20},{20,12},{12,4},{4,0},{1,9},{9... | collective-permute-start | bytes 884744 | tf_op jit(solution)/shard_map/ppermute | solution.py:693
  23.3 9.3 %collective-permute-start.18 = (f32[576,128]{1,0:T(8,128)S(1)}, f32[576,128]{1,0:T(8,128)S(1)}, u32[]{:S(2)}, u32[]{:S(2)}) collective-permute-start(f32[576,128]{1,0:T(8,128)S(1)} %ring_add.19), channel_id=1, source_target_pairs={{8,0},{16,8},{24,16},{28,24},{20,28},{12,20},{4,12},{0,4},{9,1},{1... | collective-permute-start | bytes 884744 | tf_op jit(solution)/shard_map/ppermute | solution.py:694
  32.4 10.2 %collective-permute-start.8 = (f32[576,128]{1,0:T(8,128)S(1)}, f32[576,128]{1,0:T(8,128)S(1)}, u32[]{:S(2)}, u32[]{:S(2)}) collective-permute-start(f32[576,128]{1,0:T(8,128)S(1)} %ring_add.14), channel_id=1, source_target_pairs={{0,8},{8,16},{16,24},{24,28},{28,20},{20,12},{12,4},{4,0},{1,9},{9... | collective-permute-start | bytes 884744 | tf_op jit(solution)/shard_map/ppermute | solution.py:693
  32.6 10.2 %collective-permute-start.19 = (f32[576,128]{1,0:T(8,128)S(1)}, f32[576,128]{1,0:T(8,128)S(1)}, u32[]{:S(2)}, u32[]{:S(2)}) collective-permute-start(f32[576,128]{1,0:T(8,128)S(1)} %ring_add.20), channel_id=1, source_target_pairs={{8,0},{16,8},{24,16},{28,24},{20,28},{12,20},{4,12},{0,4},{9,1},{1... | collective-permute-start | bytes 884744 | tf_op jit(solution)/shard_map/ppermute | solution.py:694
  42.6 16.6 %collective-permute-start.10 = (f32[576,128]{1,0:T(8,128)S(1)}, f32[576,128]{1,0:T(8,128)S(1)}, u32[]{:S(2)}, u32[]{:S(2)}) collective-permute-start(f32[576,128]{1,0:T(8,128)S(1)} %ring_add.15), channel_id=1, source_target_pairs={{0,8},{8,16},{16,24},{24,28},{28,20},{20,12},{12,4},{4,0},{1,9},{9... | collective-permute-start | bytes 884744 | tf_op jit(solution)/shard_map/ppermute | solution.py:693
  42.9 16.4 %collective-permute-start.20 = (f32[576,128]{1,0:T(8,128)S(1)}, f32[576,128]{1,0:T(8,128)S(1)}, u32[]{:S(2)}, u32[]{:S(2)}) collective-permute-start(f32[576,128]{1,0:T(8,128)S(1)} %ring_add.21), channel_id=1, source_target_pairs={{8,0},{16,8},{24,16},{28,24},{20,28},{12,20},{4,12},{0,4},{9,1},{1... | collective-permute-start | bytes 884744 | tf_op jit(solution)/shard_map/ppermute | solution.py:694
  44.8 12.2 %collective-permute-start.9 = (f32[72,256]{1,0:T(8,128)S(1)}, f32[72,256]{1,0:T(8,128)S(1)}, u32[]{:S(2)}, u32[]{:S(2)}) collective-permute-start(f32[72,256]{1,0:T(8,128)S(1)} %alike.11.refs_0_), channel_id=1, source_target_pairs={{0,16},{4,20},{8,24},{12,28},{16,0},{20,4},{24,8},{28,12},{1,17},{... | collective-permute-start | bytes 221192 | tf_op jit(solution)/shard_map/ppermute | solution.py:642
  59.2 10.2 %collective-permute-start.14 = (f32[576,128]{1,0:T(8,128)S(1)}, f32[576,128]{1,0:T(8,128)S(1)}, u32[]{:S(2)}, u32[]{:S(2)}) collective-permute-start(f32[576,128]{1,0:T(8,128)S(1)} %ring_add.16), channel_id=1, source_target_pairs={{0,8},{8,16},{16,24},{24,28},{28,20},{20,12},{12,4},{4,0},{1,9},{9... | collective-permute-start | bytes 884744 | tf_op jit(solution)/shard_map/ppermute | solution.py:693
  59.4 10.2 %collective-permute-start.21 = (f32[576,128]{1,0:T(8,128)S(1)}, f32[576,128]{1,0:T(8,128)S(1)}, u32[]{:S(2)}, u32[]{:S(2)}) collective-permute-start(f32[576,128]{1,0:T(8,128)S(1)} %ring_add.22), channel_id=1, source_target_pairs={{8,0},{16,8},{24,16},{28,24},{20,28},{12,20},{4,12},{0,4},{9,1},{1... | collective-permute-start | bytes 884744 | tf_op jit(solution)/shard_map/ppermute | solution.py:694
  69.5 9.2 %collective-permute-start.15 = (f32[576,128]{1,0:T(8,128)S(1)}, f32[576,128]{1,0:T(8,128)S(1)}, u32[]{:S(2)}, u32[]{:S(2)}) collective-permute-start(f32[576,128]{1,0:T(8,128)S(1)} %ring_add.17), channel_id=1, source_target_pairs={{0,8},{8,16},{16,24},{24,28},{28,20},{20,12},{12,4},{4,0},{1,9},{9... | collective-permute-start | bytes 884744 | tf_op jit(solution)/shard_map/ppermute | solution.py:693
  69.6 9.4 %collective-permute-start.22 = (f32[576,128]{1,0:T(8,128)S(1)}, f32[576,128]{1,0:T(8,128)S(1)}, u32[]{:S(2)}, u32[]{:S(2)}) collective-permute-start(f32[576,128]{1,0:T(8,128)S(1)} %ring_add.23), channel_id=1, source_target_pairs={{8,0},{16,8},{24,16},{28,24},{20,28},{12,20},{4,12},{0,4},{9,1},{1... | collective-permute-start | bytes 884744 | tf_op jit(solution)/shard_map/ppermute | solution.py:694
  96.2 12.5 %collective-permute-start.31 = (f32[544,128]{1,0:T(8,128)S(1)}, f32[544,128]{1,0:T(8,128)S(1)}, u32[]{:S(2)}, u32[]{:S(2)}) collective-permute-start(f32[544,128]{1,0:T(8,128)S(1)} %collective-permute-done.27.refs_1_), channel_id=1, source_target_pairs={{0,8},{8,16},{16,24},{24,28},{28,20},{20,12},{12,4},{4,0},{1,9},{9... | collective-permute-start | bytes 835592 | tf_op jit(solution)/shard_map/ppermute | solution.py:693
  96.6 13.9 %collective-permute-start.41 = (f32[544,128]{1,0:T(8,128)S(1)}, f32[544,128]{1,0:T(8,128)S(1)}, u32[]{:S(2)}, u32[]{:S(2)}) collective-permute-start(f32[544,128]{1,0:T(8,128)S(1)} %collective-permute-done.40.refs_11_.refs_13_), channel_id=1, source_target_pairs={{8,0},{16,8},{24,16},{28,24},{20,28},{12,20},{4,12},{0,4},{9,1},{1... | collective-permute-start | bytes 835592 | tf_op jit(solution)/shard_map/ppermute | solution.py:694
  98.3 10.1 %collective-permute-start.30 = (f32[80,256]{1,0:T(8,128)S(1)}, f32[80,256]{1,0:T(8,128)S(1)}, u32[]{:S(2)}, u32[]{:S(2)}) collective-permute-start(f32[80,256]{1,0:T(8,128)S(1)} %alike.13.refs_0_), channel_id=1, source_target_pairs={{0,12},{4,8},{8,4},{12,0},{16,28},{20,24},{24,20},{28,16},{1,13},{... | collective-permute-start | bytes 245768 | tf_op jit(solution)/shard_map/ppermute | solution.py:642
  108.8 13.7 %collective-permute-start.33 = (f32[544,128]{1,0:T(8,128)S(1)}, f32[544,128]{1,0:T(8,128)S(1)}, u32[]{:S(2)}, u32[]{:S(2)}) collective-permute-start(f32[544,128]{1,0:T(8,128)S(1)} %collective-permute-done.31.refs_2_), channel_id=1, source_target_pairs={{0,8},{8,16},{16,24},{24,28},{28,20},{20,12},{12,4},{4,0},{1,9},{9... | collective-permute-start | bytes 835592 | tf_op jit(solution)/shard_map/ppermute | solution.py:693
  110.5 12.0 %collective-permute-start.42 = (f32[544,128]{1,0:T(8,128)S(1)}, f32[544,128]{1,0:T(8,128)S(1)}, u32[]{:S(2)}, u32[]{:S(2)}) collective-permute-start(f32[544,128]{1,0:T(8,128)S(1)} %collective-permute-done.41.refs_10_.refs_12_), channel_id=1, source_target_pairs={{8,0},{16,8},{24,16},{28,24},{20,28},{12,20},{4,12},{0,4},{9,1},{1... | collective-permute-start | bytes 835592 | tf_op jit(solution)/shard_map/ppermute | solution.py:694
  110.8 9.7 %collective-permute-start.32 = (f32[80,256]{1,0:T(8,128)S(1)}, f32[80,256]{1,0:T(8,128)S(1)}, u32[]{:S(2)}, u32[]{:S(2)}) collective-permute-start(f32[80,256]{1,0:T(8,128)S(1)} %alike.14.refs_0_), channel_id=1, source_target_pairs={{0,16},{4,20},{8,24},{12,28},{16,0},{20,4},{24,8},{28,12},{1,17},{... | collective-permute-start | bytes 245768 | tf_op jit(solution)/shard_map/ppermute | solution.py:642
  122.5 9.9 %collective-permute-start.37 = (f32[544,128]{1,0:T(8,128)S(1)}, f32[544,128]{1,0:T(8,128)S(1)}, u32[]{:S(2)}, u32[]{:S(2)}) collective-permute-start(f32[544,128]{1,0:T(8,128)S(1)} %collective-permute-done.33.refs_3_), channel_id=1, source_target_pairs={{0,8},{8,16},{16,24},{24,28},{28,20},{20,12},{12,4},{4,0},{1,9},{9... | collective-permute-start | bytes 835592 | tf_op jit(solution)/shard_map/ppermute | solution.py:693
  122.5 9.9 %collective-permute-start.43 = (f32[544,128]{1,0:T(8,128)S(1)}, f32[544,128]{1,0:T(8,128)S(1)}, u32[]{:S(2)}, u32[]{:S(2)}) collective-permute-start(f32[544,128]{1,0:T(8,128)S(1)} %collective-permute-done.42.refs_9_.refs_11_), channel_id=1, source_target_pairs={{8,0},{16,8},{24,16},{28,24},{20,28},{12,20},{4,12},{0,4},{9,1},{1... | collective-permute-start | bytes 835592 | tf_op jit(solution)/shard_map/ppermute | solution.py:694
  132.4 9.3 %collective-permute-start.38 = (f32[544,128]{1,0:T(8,128)S(1)}, f32[544,128]{1,0:T(8,128)S(1)}, u32[]{:S(2)}, u32[]{:S(2)}) collective-permute-start(f32[544,128]{1,0:T(8,128)S(1)} %collective-permute-done.37.refs_4_), channel_id=1, source_target_pairs={{0,8},{8,16},{16,24},{24,28},{28,20},{20,12},{12,4},{4,0},{1,9},{9... | collective-permute-start | bytes 835592 | tf_op jit(solution)/shard_map/ppermute | solution.py:693
  132.5 9.5 %collective-permute-start.44 = (f32[544,128]{1,0:T(8,128)S(1)}, f32[544,128]{1,0:T(8,128)S(1)}, u32[]{:S(2)}, u32[]{:S(2)}) collective-permute-start(f32[544,128]{1,0:T(8,128)S(1)} %collective-permute-done.43.refs_8_.refs_10_), channel_id=1, source_target_pairs={{8,0},{16,8},{24,16},{28,24},{20,28},{12,20},{4,12},{0,4},{9,1},{1... | collective-permute-start | bytes 835592 | tf_op jit(solution)/shard_map/ppermute | solution.py:694
  141.6 10.2 %collective-permute-start.45 = (f32[544,128]{1,0:T(8,128)S(1)}, f32[544,128]{1,0:T(8,128)S(1)}, u32[]{:S(2)}, u32[]{:S(2)}) collective-permute-start(f32[544,128]{1,0:T(8,128)S(1)} %collective-permute-done.38.refs_5_), channel_id=1, source_target_pairs={{0,8},{8,16},{16,24},{24,28},{28,20},{20,12},{12,4},{4,0},{1,9},{9... | collective-permute-start | bytes 835592 | tf_op jit(solution)/shard_map/ppermute | solution.py:693
  141.9 10.0 %collective-permute-start.46 = (f32[544,128]{1,0:T(8,128)S(1)}, f32[544,128]{1,0:T(8,128)S(1)}, u32[]{:S(2)}, u32[]{:S(2)}) collective-permute-start(f32[544,128]{1,0:T(8,128)S(1)} %collective-permute-done.44.refs_7_.refs_9_), channel_id=1, source_target_pairs={{8,0},{16,8},{24,16},{28,24},{20,28},{12,20},{4,12},{0,4},{9,1},{1... | collective-permute-start | bytes 835592 | tf_op jit(solution)/shard_map/ppermute | solution.py:694
  (29 other events, 172.2 us)
